TPU v7x, 512 devices: a whole 4x8x8 slice. The times are simulated.
512 devices in a mesh: dp: 32 (over y, z_lo), tensor: 16 (over z_hi, x, core).
Axes of the slice: x: 4, y: 8, z: 8 (z_hi: 2, z_lo: 4; z = z_hi * 4 + z_lo), core: 2. Of those that a mesh axis runs over, the one named last changes fastest.
Arguments:
- hidden: bfloat16 [24576, 14336], P('dp', 'tensor'), may hold values from -0.0390625 to 0.0390625
- out_grad: bfloat16 [24576, 8192], P(('dp', 'tensor')), may hold values from -6 to 6
- weights: bfloat16 [16, 32, 128, 128], P('tensor'), may hold values from -0.125 to 0.125
- block_rows: int32 [16, 32], P('tensor'), may hold values from 0 to 6, as said below
- block_cols: int32 [16, 32], P('tensor'), may hold values from 0 to 63, as said below
- counts: int32 [16], P('tensor'), may hold values from 16 to 32, as said below
Outputs:
- weight_grad: float32 [16, 32, 128, 128], P('tensor', 'dp')
- input_grad: bfloat16 [24576, 14336], P('dp', 'tensor')
Inputs may be any that keep to these rules, and one draw needn't show every extreme that they name: `block_rows`: within one member, no two slots name the same pair of block row and block column. `block_cols`: pairs with block_rows as stated there. `counts`: some member has all 32 slots live.
All inputs are finite; a program needn't handle non-finite values.
Results may differ from a plain program's by a relative error of at most 0.001.
Values may be sent and summed in bfloat16 or wider, within the bound.
No kernel may reach another device: no remote copies, remote signals or barrier semaphores. Data moves between devices by JAX's collectives and lax.ppermute only.
A program may use at most 128 MiB of HBM per device.

v0:
```python
import math

import jax
import jax.numpy as jnp
from jax import lax
from jax.sharding import PartitionSpec as P

BLK = 128


def shards(hidden, out_grad, weights, block_rows, block_cols, counts):
    slot_weights = weights[0]
    position_rows = block_rows[0]
    slot_cols = block_cols[0]
    panel_blocks = hidden.shape[1] // BLK
    col_blocks = out_grad.shape[1] // BLK
    active_flags = (jnp.arange(position_rows.shape[0], dtype=jnp.int32) < counts[0]).astype(
        jnp.float32
    )
    assignment = (
        position_rows[:, None] == jnp.arange(panel_blocks, dtype=jnp.int32)[None, :]
    ).astype(jnp.float32)
    assignment = assignment * active_flags[:, None]
    initial = (jnp.zeros(slot_weights.shape, jnp.float32), jnp.zeros(hidden.shape, jnp.float32))
    rows_piece = lax.all_gather(out_grad, "tensor", axis=0, tiled=True)
    height = rows_piece.shape[0]
    stride = math.gcd(height, 256)

    def row_step(position, sums):
        gradient_accumulator, input_acc = sums
        first_row = position * stride
        grad_rows = lax.dynamic_slice_in_dim(rows_piece, first_row, stride, 0)
        act_rows = lax.dynamic_slice_in_dim(hidden, first_row, stride, 0)
        grad_sel = jnp.take(grad_rows.reshape(stride, col_blocks, BLK), slot_cols, axis=1)
        act_sel = jnp.take(act_rows.reshape(stride, panel_blocks, BLK), position_rows, axis=1)
        gradient_accumulator = gradient_accumulator + jnp.einsum(
            "nsa,nsb->sab", act_sel, grad_sel, preferred_element_type=jnp.float32
        )
        contribution = jnp.einsum(
            "nsb,sab->nsa", grad_sel, slot_weights, preferred_element_type=jnp.float32
        )
        placed = jnp.einsum(
            "nsa,sp->npa", contribution, assignment, precision=lax.Precision.HIGHEST
        )
        input_acc = lax.dynamic_update_slice_in_dim(
            input_acc, placed.reshape(stride, -1), first_row, 0
        )
        return (gradient_accumulator, input_acc)

    gradient_accumulator, input_acc = lax.fori_loop(0, height // stride, row_step, initial)
    gradient_accumulator = gradient_accumulator * active_flags[:, None, None]
    summed = lax.psum(gradient_accumulator, "dp")
    share = summed.shape[0] // lax.axis_size("dp")
    mine = lax.dynamic_slice_in_dim(summed, lax.axis_index("dp") * share, share, 0)
    return (mine[None], input_acc.astype(jnp.bfloat16))


def solution(mesh):
    in_specs = (
        P("dp", "tensor"),
        P(("dp", "tensor"), None),
        P("tensor", None, None, None),
        P("tensor", None),
        P("tensor", None),
        P("tensor"),
    )
    out_specs = (P("tensor", "dp", None, None), P("dp", "tensor"))
    return jax.shard_map(shards, mesh=mesh, in_specs=in_specs, out_specs=out_specs, check_vma=False)
```

profile of v0, /device:TPU:6, one launch (start us, length us, event | category | flops | bytes accessed | tf_op | source)
XLA Modules:
  0.0 594.6 jit_solution(14581286451371529007)
XLA Ops:
  7.2 0.7 all-gather.2.cloned.1.call-update
  8.6 152.3 %all-gather.2.cloned.1.call-done = bf16[768,8192]{1,0:T(8,128)(2,1)} async-done(((bf16[48,8192]{1,0:T(8,128)(2,1)}), bf16[768,8192]{1,0:T(8,128)(2,1)}) %all-gather.2.cloned.1.call-update) | async-done | bytes 12582928 | tf_op jit(solution)/shard_map/all_gather | solution.py:25
  160.9 1.2 broadcast_in_dim.47.clone
  162.1 106.1 %while.18 = (s32[]{:T(128)}, f32[32,128,128]{2,1,0:T(8,128)}, bf16[768,896]{1,0:T(8,128)(2,1)}, s32[32]{0:T(128)S(1)}, bf16[768,896]{1,0:T(8,128)(2,1)}, /*index...) while((s32[]{:T(128)}, f32[32,128,128]{2,1,0:T(8,128)}, ...), condition=%wide.region_1.0_spmd.clone.clone.clone, body=%wide.region_0.1_spmd.clone.clone.clone.sunk | while | flops 629148672 | bytes 63645564 | solution.py:50
  162.1 4.6 constant_dynamic-slice_fusion.5
  166.7 6.4 %copy.49 = bf16[256,8192]{0,1:T(8,128)(2,1)} copy(bf16[256,8192]{1,0:T(8,128)(2,1)} %constant_dynamic-slice_fusion.5) | data formatting | bytes 8388608 | tf_op jit(solution)/shard_map/while/body/eval_jaxpr/dynamic_slice | solution.py:32
  173.1 6.4 %copy.50 = bf16[256,64,128]{2,0,1:T(8,128)(2,1)} copy(bf16[256,64,128]{0,2,1:T(8,128)(2,1)} %bitcast.62) | data formatting | bytes 8388608 | tf_op jit(solution)/shard_map/while/body/eval_jaxpr/reshape | solution.py:34
  179.4 3.1 gather_fusion.1
  182.6 1.1 constant_dynamic-slice_fusion.4
  183.7 0.2 copy.47
  183.9 0.3 copy.48
  184.1 2.1 gather_fusion
  186.3 4.0 select_add_fusion.2
  190.3 0.8 convolution_bitcast_fusion.2
  191.1 4.6 fusion.44
  195.7 0.3 copy.51
  196.0 0.2 copy.52
  196.3 0.8 constant_dynamic-update-slice_fusion.2
  197.1 4.6 constant_dynamic-slice_fusion.5
  201.6 6.4 %copy.49 = bf16[256,8192]{0,1:T(8,128)(2,1)} copy(bf16[256,8192]{1,0:T(8,128)(2,1)} %constant_dynamic-slice_fusion.5) | data formatting | bytes 8388608 | tf_op jit(solution)/shard_map/while/body/eval_jaxpr/dynamic_slice | solution.py:32
  208.0 6.4 %copy.50 = bf16[256,64,128]{2,0,1:T(8,128)(2,1)} copy(bf16[256,64,128]{0,2,1:T(8,128)(2,1)} %bitcast.62) | data formatting | bytes 8388608 | tf_op jit(solution)/shard_map/while/body/eval_jaxpr/reshape | solution.py:34
  214.4 3.1 gather_fusion.1
  217.5 1.1 constant_dynamic-slice_fusion.4
  218.6 0.2 copy.47
  218.8 0.3 copy.48
  219.1 2.1 gather_fusion
  221.3 4.6 select_add_fusion.2
  225.9 0.8 convolution_bitcast_fusion.2
  226.6 4.6 fusion.44
  231.3 0.3 copy.51
  231.6 0.2 copy.52
  231.8 0.8 constant_dynamic-update-slice_fusion.2
  232.6 4.6 constant_dynamic-slice_fusion.5
  237.2 6.4 %copy.49 = bf16[256,8192]{0,1:T(8,128)(2,1)} copy(bf16[256,8192]{1,0:T(8,128)(2,1)} %constant_dynamic-slice_fusion.5) | data formatting | bytes 8388608 | tf_op jit(solution)/shard_map/while/body/eval_jaxpr/dynamic_slice | solution.py:32
  243.6 6.4 %copy.50 = bf16[256,64,128]{2,0,1:T(8,128)(2,1)} copy(bf16[256,64,128]{0,2,1:T(8,128)(2,1)} %bitcast.62) | data formatting | bytes 8388608 | tf_op jit(solution)/shard_map/while/body/eval_jaxpr/reshape | solution.py:34
  249.9 3.1 gather_fusion.1
  253.1 1.1 constant_dynamic-slice_fusion.4
  254.4 0.3 copy.48
  254.6 2.1 gather_fusion
  256.8 4.6 select_add_fusion.2
  261.4 0.8 convolution_bitcast_fusion.2
  262.2 4.6 fusion.44
  266.8 0.3 copy.51
  267.1 0.2 copy.52
  267.4 0.8 constant_dynamic-update-slice_fusion.2
  268.2 3.1 broadcast_multiply_fusion
  271.4 314.9 %all-reduce.2.cloned.1.call-done = f32[32,128,128]{2,1,0:T(8,128)} async-done(((f32[32,128,128]{2,1,0:T(8,128)}), f32[32,128,128]{2,1,0:T(8,128)}) %all-reduce.2.cloned.1.call-update) | async-done | bytes 2097168 | tf_op jit(solution)/shard_map/psum | solution.py:52
  586.3 1.5 dynamic-slice_bitcast_fusion
  (28 shorter events, 0.4 us)
Async XLA Ops:
  7.2 155.0 %copy-start.1 = (s32[1,32]{1,0:T(1,128)S(1)}, s32[1,32]{1,0:T(1,128)}, u32[]{:S(2)}) copy-start(s32[1,32]{1,0:T(1,128)} %param.11) | copy-start | bytes 388
  7.2 155.0 %copy-start.2 = (s32[1,32]{1,0:T(1,128)S(1)}, s32[1,32]{1,0:T(1,128)}, u32[]{:S(2)}) copy-start(s32[1,32]{1,0:T(1,128)} %param.12) | copy-start | bytes 388
  7.2 153.8 %all-gather.2.cloned.1.call-start = ((), (), s32[]{:S(2)}) async-start(), calls=%async_computation | async-start | bytes 13369344 | tf_op jit(solution)/shard_map/all_gather | solution.py:25
  7.9 578.4 %all-reduce.2.cloned.1.call-start = ((), (), s32[]{:S(2)}) async-start(), calls=%async_computation.1 | async-start | bytes 4194304 | tf_op jit(solution)/shard_map/psum | solution.py:52
  186.3 4.0 copy-start
  221.2 4.6 copy-start
  256.8 4.6 copy-start
Sparse Core Ops, SparseCore 0:
  11.3 149.5 all-gather.1
  271.5 314.7 all-reduce.1
where the time goes:
time: 596 us; the launch traced here: 595 us
  waiting for transfers between devices  468 us (79%)
  local copies, waits for them, and re-layouts  79.1 us (13%)
  matrix products  29.3 us (5%)
  between operations  14.7 us (2%)
    psum x1, waiting for transfers between devices, shards(): summed = lax.psum(gradient_accumulator, 'dp')  315 us
    all_gather x1, waiting for transfers between devices, shards(): rows_piece = lax.all_gather(out_grad, 'tensor', axis=0, tiled=True)  152 us
    dynamic_slice x6, local copies, waits for them, and re-layouts, row_step(): grad_rows = lax.dynamic_slice_in_dim(rows_piece, first_row, stride, 0)  32.8 us
    reshape x3, local copies, waits for them, and re-layouts, row_step(): grad_rows.reshape(stride, col_blocks, BLK)  19.1 us
    dot_general x3, matrix products, row_step(): jnp.einsum('nsa,sp->npa', contribution, assignment, precision=lax.Precisi...  13.8 us
    dot_general x3, matrix products, row_step(): jnp.einsum('nsa,nsb->sab', act_sel, grad_sel, preferred_element_type=jnp....  13.2 us
  transfers between devices with their start and end apart: 2, of which 2 were waited for; matrix products, arithmetic and copies ran while one was open for 0% of the time, Pallas kernels for 0%

commit v1 on v0

v1 whole, which is shorter than its diff:
```python
import functools

import jax
import jax.numpy as jnp
from jax import lax
from jax.experimental import pallas as pl
from jax.experimental.pallas import tpu as pltpu
from jax.sharding import PartitionSpec as P


BLK = 128
EXTRA = 8
SHIFT = 14.0
TINY = 1e-30
X = 4
MEMBERS = 4 * X
HALF = 2 * X


def swap_half(i):
    return i ^ HALF


def swap_core(i):
    return i ^ 1


def along_x(step):
    def move(i):
        return (i // HALF) * HALF + ((i // 2 + step) % X) * 2 + i % 2

    return move


def send(value, target):
    return lax.ppermute(value, "tensor", [(i, target(i)) for i in range(MEMBERS)])


def gather_rows(pieces, cols):
    return jnp.concatenate(
        [jnp.concatenate([piece[:, c] for piece in pieces], 0) for c in cols], 1
    )


def blocks_of(table_ref, slots):
    return [pl.ds(pl.multiple_of(table_ref[s] * BLK, BLK), BLK) for s in slots]


def weight_kernel(count, first, coded, rows_ref, cols_ref, offs_ref, *refs):
    pieces, hidden_ref, out_ref = refs[:count], refs[count], refs[-1]
    height = pieces[0].shape[0]
    offs = [pl.multiple_of(offs_ref[first + i], 16) for i in range(count)]

    def pair_step(pair, carry):
        slots = (2 * pair, 2 * pair + 1)
        grad = gather_rows(pieces, blocks_of(cols_ref, slots))
        act = jnp.concatenate(
            [
                jnp.concatenate([hidden_ref[pl.ds(o, height), r] for o in offs], 0)
                for r in blocks_of(rows_ref, slots)
            ],
            1,
        )
        blocks = lax.dot_general(
            act, grad, (((0,), (0,)), ((), ())), preferred_element_type=jnp.float32
        )
        for k, s in enumerate(slots):
            block = blocks[k * BLK : (k + 1) * BLK, k * BLK : (k + 1) * BLK]
            if coded:
                block = block + refs[count + 1][s]
                top = jnp.max(jnp.abs(block), axis=0, keepdims=True)
                power = jnp.ceil(jnp.log2(jnp.maximum(top, TINY)))
                out_ref[s, :BLK, :] = block * jnp.exp2(SHIFT - power)
                out_ref[s, BLK:, :] = jnp.broadcast_to(power, (EXTRA, BLK))
            else:
                out_ref[s] = block
        return carry

    lax.fori_loop(0, rows_ref.shape[0] // 2, pair_step, 0)


def input_kernel(count, rows_ref, cols_ref, offs_ref, counts_ref, *refs):
    pieces, (weights_ref, out_ref, total) = refs[:count], refs[count:]
    height = pieces[0].shape[0]
    total[...] = jnp.zeros_like(total)
    nothing = jnp.zeros((BLK, BLK), weights_ref.dtype)

    def pair_step(pair, carry):
        slots = (2 * pair, 2 * pair + 1)
        grad = gather_rows(pieces, blocks_of(cols_ref, slots))
        w = []
        for s in slots:
            live = (s < counts_ref[0]).astype(jnp.float32)
            w.append((weights_ref[s].astype(jnp.float32) * live).astype(weights_ref.dtype))
        both = jnp.concatenate(
            [jnp.concatenate([w[0], nothing], 1), jnp.concatenate([nothing, w[1]], 1)], 0
        )
        moved = lax.dot_general(
            grad, both, (((1,), (1,)), ((), ())), preferred_element_type=jnp.float32
        )
        for k, r in enumerate(blocks_of(rows_ref, slots)):
            total[:, r] += moved[:, k * BLK : (k + 1) * BLK]
        return carry

    lax.fori_loop(0, rows_ref.shape[0] // 2, pair_step, 0)
    for i in range(count):
        o = pl.multiple_of(offs_ref[i], 16)
        out_ref[pl.ds(o, height), :] = total[i * height : (i + 1) * height, :].astype(out_ref.dtype)


def staged(kernel, n_tables, n_in, out_staged, *refs):
    tables, sources, out_ref = refs[:n_tables], refs[n_tables : n_tables + n_in], refs[n_tables + n_in]
    sems, *held = refs[n_tables + n_in + 1 :]
    held, extra = held[:n_in], held[n_in:]
    copies = [pltpu.make_async_copy(sources[i], held[i], sems.at[i]) for i in range(n_in)]
    for copy in copies:
        copy.start()
    for copy in copies:
        copy.wait()
    if not out_staged:
        kernel(*tables, *held, out_ref, *extra)
        return
    kernel(*tables, *held, extra[0], *extra[1:])
    copy = pltpu.make_async_copy(extra[0], out_ref, sems.at[n_in])
    copy.start()
    copy.wait()


def call(kernel, tables, operands, out, scratch, flops, out_staged=False):
    far = pl.BlockSpec(memory_space=pltpu.HBM)
    zeros = (0,) * len(out.shape)
    near = pl.BlockSpec(out.shape, lambda i, *_: zeros, pipeline_mode=pl.Buffered(1))
    size = sum(v.size * v.dtype.itemsize for v in (*operands, out))
    held = [pltpu.VMEM(v.shape, v.dtype) for v in operands + ((out,) if out_staged else ())]
    return pl.pallas_call(
        functools.partial(staged, kernel, len(tables), len(operands), out_staged),
        grid_spec=pltpu.PrefetchScalarGridSpec(
            num_scalar_prefetch=len(tables),
            grid=(1,),
            in_specs=[far for _ in operands],
            out_specs=far if out_staged else near,
            scratch_shapes=[pltpu.SemaphoreType.DMA((len(operands) + 1,)), *held, *scratch],
        ),
        out_shape=out,
        compiler_params=pltpu.CompilerParams(vmem_limit_bytes=GRANT),
        cost_estimate=pl.CostEstimate(flops=flops, bytes_accessed=size, transcendentals=0),
    )(*tables, *operands)


def weight_grads(pieces, first, tables, hidden, slots, prior=None):
    coded = prior is not None
    kernel = functools.partial(weight_kernel, len(pieces), first, coded)
    out = jax.ShapeDtypeStruct((slots, BLK + EXTRA * coded, BLK), jnp.float32)
    operands = (*pieces, hidden) + ((prior,) if coded else ())
    flops = 4 * slots * len(pieces) * pieces[0].shape[0] * BLK * BLK
    return call(kernel, tables, operands, out, [], flops, out_staged=not coded)


def input_grads(pieces, tables, weights, like):
    kernel = functools.partial(input_kernel, len(pieces))
    out = jax.ShapeDtypeStruct(like.shape, like.dtype)
    flops = 4 * weights.shape[0] * like.shape[0] * BLK * BLK
    scratch = [pltpu.VMEM(like.shape, jnp.float32)]
    return call(kernel, tables, (*pieces, weights), out, scratch, flops)


def shards(hidden, out_grad, weights, block_rows, block_cols, counts):
    return body(hidden, out_grad, weights[0], block_rows[0], block_cols[0], counts)


def body(hidden, out_grad, weights, rows, cols, counts):
    height = out_grad.shape[0]
    slots = weights.shape[0]
    me = lax.axis_index("tensor")
    half, x, core = me // HALF, (me // 2) % X, me % 2

    other = send(out_grad, swap_half)
    near = [out_grad] + [send(out_grad, along_x(k)) for k in STEPS[1:]]
    far = [other] + [send(other, along_x(k)) for k in STEPS[1:]]
    pieces, places = [], []
    for shards_, h in ((near, half), (far, 1 - half)):
        for k, shard in zip(STEPS, shards_):
            chip = h * HALF + (x - k) % X * 2
            pieces += [shard, send(shard, swap_core)]
            places += [(chip + core) * height, (chip + 1 - core) * height]
    tables = (rows, cols, jnp.stack(places))

    prior = weight_grads(pieces[:EARLY], 0, tables, hidden, slots)
    coded = weight_grads(pieces[EARLY:], EARLY, tables, hidden, slots, prior)
    parts = lax.all_to_all(coded.astype(jnp.float16), "dp", split_axis=0, concat_axis=0, tiled=True)
    input_grad = input_grads(pieces, (*tables, counts), weights, hidden)

    share = slots // lax.axis_size("dp")
    parts = parts.astype(jnp.float32).reshape(-1, share, BLK + EXTRA, BLK)
    summed = (parts[:, :, :BLK] * jnp.exp2(parts[:, :, BLK : BLK + 1] - SHIFT)).sum(0)
    mine = lax.axis_index("dp") * share + jnp.arange(share, dtype=jnp.int32)
    summed = jnp.where((mine < counts[0])[:, None, None], summed, 0.0)
    return summed[None], input_grad


STEPS = (0, 1, X - 1, 2)
EARLY = 2 * X + 2
GRANT = 60 * 2**20


def solution(mesh):
    in_specs = (
        P("dp", "tensor"),
        P(("dp", "tensor"), None),
        P("tensor", None, None, None),
        P("tensor", None),
        P("tensor", None),
        P("tensor"),
    )
    out_specs = (P("tensor", "dp", None, None), P("dp", "tensor"))
    return jax.shard_map(
        shards, mesh=mesh, in_specs=in_specs, out_specs=out_specs, check_vma=False
    )
```

time: 596 us -> 163 us (0.27)
  waiting for transfers between devices: 468 us -> 54.4 us
  local copies, waits for them, and re-layouts: 79.1 us -> 0.71 us
  starting transfers between devices: 0.08 us -> 65.6 us
  Pallas kernels: 0 us -> 33.5 us
  matrix products: 29.3 us -> 0 us
  between operations: 14.7 us -> 1.74 us
    psum x1 -> x0, waiting for transfers between devices: 315 us -> none  [shards(): summed = lax.psum(gradient_accumulator, 'dp')]
    all_gather x1 -> x0, waiting for transfers between devices: 152 us -> none  [shards(): rows_piece = lax.all_gather(out_grad, 'tensor', axis=0, tiled=True)]
    ppermute x0 -> x15, starting transfers between devices: none -> 48 us  [send(): lax.ppermute(value, 'tensor', [(i, target(i)) for i in range(MEMBERS)])]
    ppermute x0 -> x15, waiting for transfers between devices: none -> 38.2 us  [send(): lax.ppermute(value, 'tensor', [(i, target(i)) for i in range(MEMBERS)])]
    dynamic_slice x12 -> x0, local copies, waits for them, and re-layouts: 36.6 us -> none  [the longest x6 32.8 us: row_step(): grad_rows = lax.dynamic_slice_in_dim(rows_piece, first_row, stride, 0)]
    pallas_call x0 -> x3, Pallas kernels: none -> 33.5 us  [call(): pl.pallas_call(functools.partial(staged, kernel, len(tables), len(operand...]
    dot_general x9 -> x0, matrix products: 29.3 us -> none  [the longest x3 13.8 us: row_step(): jnp.einsum('nsa,sp->npa', contribution, assignment, precision=lax.Precisi...]
    reshape x6 -> x0, local copies, waits for them, and re-layouts: 19.8 us -> none  [the longest x3 19.1 us: row_step(): grad_rows.reshape(stride, col_blocks, BLK)]
  transfers between devices with their start and end apart: 2 -> 16, of which waited for: 2 -> 5; matrix products, arithmetic and copies ran while one was open for 0% -> 0% of each run, Pallas kernels for 0% -> 15%
where the time goes in v1:
time: 163 us; the launch traced here: 160 us
  starting transfers between devices  65.6 us (40%)
  waiting for transfers between devices  54.4 us (33%)
  Pallas kernels  33.5 us (21%)
  other arithmetic  3.8 us (2%)
  between operations  1.74 us (1%)
    ppermute x15, starting transfers between devices, send(): lax.ppermute(value, 'tensor', [(i, target(i)) for i in range(MEMBERS)])  48 us
    ppermute x15, waiting for transfers between devices, send(): lax.ppermute(value, 'tensor', [(i, target(i)) for i in range(MEMBERS)])  38.2 us
    pallas_call x3, Pallas kernels, call(): pl.pallas_call(functools.partial(staged, kernel, len(tables), len(operand...  33.5 us
    all_to_all x1, starting transfers between devices, body(): lax.all_to_all(coded.astype(jnp.float16), 'dp', split_axis=0, concat_axis...  17.6 us
    all_to_all x1, waiting for transfers between devices, body(): lax.all_to_all(coded.astype(jnp.float16), 'dp', split_axis=0, concat_axis...  16.3 us
  transfers between devices with their start and end apart: 16, of which 5 were waited for; matrix products, arithmetic and copies ran while one was open for 0% of the time, Pallas kernels for 15%

profile of v1, /device:TPU:6, one launch (start us, length us, event | category | flops | bytes accessed | tf_op | source)
XLA Modules:
  0.0 159.8 jit_solution(17007596222030013987)
XLA Ops:
  0.6 3.3 %collective-permute-start.12 = (bf16[48,8192]{1,0:T(8,128)(2,1)}, bf16[48,8192]{1,0:T(8,128)(2,1)S(1)}, u32[]{:S(2)}, u32[]{:S(2)}) collective-permute-start(bf16[48,8192]{1,0:T(8,128)(2,1)} %refs_4_.1), channel_id=1, source_target_pairs={{0,4},{1,5},{2,6},{3,7},{4,0},{5,1},{6,2},{7,3},{8,12},{9,13},{10,... | collective-permute-start | bytes 2359304 | tf_op jit(solution)/shard_map/ppermute | solution.py:36
  4.0 7.2 %collective-permute-start.10 = (bf16[48,8192]{1,0:T(8,128)(2,1)}, bf16[48,8192]{1,0:T(8,128)(2,1)S(1)}, u32[]{:S(2)}, u32[]{:S(2)}) collective-permute-start(bf16[48,8192]{1,0:T(8,128)(2,1)} %refs_4_.1), channel_id=1, source_target_pairs={{0,6},{1,7},{2,0},{3,1},{4,2},{5,3},{6,4},{7,5},{8,14},{9,15},{10,... | collective-permute-start | bytes 2359304 | tf_op jit(solution)/shard_map/ppermute | solution.py:36
  11.1 5.7 %collective-permute-start = (bf16[48,8192]{1,0:T(8,128)(2,1)}, bf16[48,8192]{1,0:T(8,128)(2,1)S(1)}, u32[]{:S(2)}, u32[]{:S(2)}) collective-permute-start(bf16[48,8192]{1,0:T(8,128)(2,1)} %refs_4_.1), channel_id=1, source_target_pairs={{0,8},{1,9},{2,10},{3,11},{4,12},{5,13},{6,14},{7,15},{8,0},{9,1},... | collective-permute-start | bytes 2359304 | tf_op jit(solution)/shard_map/ppermute | solution.py:36
  16.8 5.1 %collective-permute-start.8 = (bf16[48,8192]{1,0:T(8,128)(2,1)}, bf16[48,8192]{1,0:T(8,128)(2,1)S(1)}, u32[]{:S(2)}, u32[]{:S(2)}) collective-permute-start(bf16[48,8192]{1,0:T(8,128)(2,1)} %refs_4_.1), channel_id=1, source_target_pairs={{0,2},{1,3},{2,4},{3,5},{4,6},{5,7},{6,0},{7,1},{8,10},{9,11},{10,... | collective-permute-start | bytes 2359304 | tf_op jit(solution)/shard_map/ppermute | solution.py:36
  22.0 1.9 %collective-permute-start.7 = (bf16[48,8192]{1,0:T(8,128)(2,1)}, bf16[48,8192]{1,0:T(8,128)(2,1)S(1)}, u32[]{:S(2)}, u32[]{:S(2)}) collective-permute-start(bf16[48,8192]{1,0:T(8,128)(2,1)} %refs_4_.1), channel_id=1, source_target_pairs={{0,1},{1,0},{2,3},{3,2},{4,5},{5,4},{6,7},{7,6},{8,9},{9,8},{10,11... | collective-permute-start | bytes 2359304 | tf_op jit(solution)/shard_map/ppermute | solution.py:36
  23.9 0.8 collective-permute-done.12.refs_9_.refs_10_
  24.7 1.9 %collective-permute-start.13 = (bf16[48,8192]{1,0:T(8,128)(2,1)S(1)}, bf16[48,8192]{1,0:T(8,128)(2,1)S(1)}, u32[]{:S(2)}, u32[]{:S(2)}) collective-permute-start(bf16[48,8192]{1,0:T(8,128)(2,1)S(1)} %collective-permute-done.12.refs_9_.refs_10_), channel_id=1, source_target_pairs={{0,1},{1,0},{2,3},{3,2},{4,5},{5,4},{6,7},{7,6},{8,9},{9,8},{10,11... | collective-permute-start | bytes 2359304 | tf_op jit(solution)/shard_map/ppermute | solution.py:36
  26.6 13.8 %collective-permute-done.10.refs_7_.refs_8_ = bf16[48,8192]{1,0:T(8,128)(2,1)S(1)} collective-permute-done((bf16[48,8192]{1,0:T(8,128)(2,1)}, bf16[48,8192]{1,0:T(8,128)(2,1)S(1)}, u32[]{:S(2)}, u32[]{:S(2)}) %collective-permute-start.10) | collective-permute-done | bytes 786464 | tf_op jit(solution)/shard_map/ppermute | solution.py:36
  40.4 1.9 %collective-permute-start.11 = (bf16[48,8192]{1,0:T(8,128)(2,1)S(1)}, bf16[48,8192]{1,0:T(8,128)(2,1)S(1)}, u32[]{:S(2)}, u32[]{:S(2)}) collective-permute-start(bf16[48,8192]{1,0:T(8,128)(2,1)S(1)} %collective-permute-done.10.refs_7_.refs_8_), channel_id=1, source_target_pairs={{0,1},{1,0},{2,3},{3,2},{4,5},{5,4},{6,7},{7,6},{8,9},{9,8},{10,11... | collective-permute-start | bytes 2359304 | tf_op jit(solution)/shard_map/ppermute | solution.py:36
  42.3 0.0 collective-permute-done.refs_11_.refs_12_
  42.3 0.0 copy-start.2
  42.3 3.3 %collective-permute-start.5 = (bf16[48,8192]{1,0:T(8,128)(2,1)S(1)}, bf16[48,8192]{1,0:T(8,128)(2,1)}, u32[]{:S(2)}, u32[]{:S(2)}) collective-permute-start(bf16[48,8192]{1,0:T(8,128)(2,1)S(1)} %collective-permute-done.refs_11_.refs_12_), channel_id=1, source_target_pairs={{0,4},{1,5},{2,6},{3,7},{4,0},{5,1},{6,2},{7,3},{8,12},{9,13},{10,... | collective-permute-start | bytes 2359304 | tf_op jit(solution)/shard_map/ppermute | solution.py:36
  45.6 0.0 collective-permute-done.8.refs_5_.refs_6_
  45.7 0.0 copy-start.3
  45.7 2.0 %collective-permute-start.3 = (bf16[48,8192]{1,0:T(8,128)(2,1)S(1)}, bf16[48,8192]{1,0:T(8,128)(2,1)}, u32[]{:S(2)}, u32[]{:S(2)}) collective-permute-start(bf16[48,8192]{1,0:T(8,128)(2,1)S(1)} %collective-permute-done.refs_11_.refs_12_), channel_id=1, source_target_pairs={{0,6},{1,7},{2,0},{3,1},{4,2},{5,3},{6,4},{7,5},{8,14},{9,15},{10,... | collective-permute-start | bytes 2359304 | tf_op jit(solution)/shard_map/ppermute | solution.py:36
  47.6 0.0 collective-permute-done.7.refs_4_.refs_5_
  47.6 0.0 copy-start.4
  47.7 5.1 %collective-permute-start.1 = (bf16[48,8192]{1,0:T(8,128)(2,1)S(1)}, bf16[48,8192]{1,0:T(8,128)(2,1)}, u32[]{:S(2)}, u32[]{:S(2)}) collective-permute-start(bf16[48,8192]{1,0:T(8,128)(2,1)S(1)} %collective-permute-done.refs_11_.refs_12_), channel_id=1, source_target_pairs={{0,2},{1,3},{2,4},{3,5},{4,6},{5,7},{6,0},{7,1},{8,10},{9,11},{10,... | collective-permute-start | bytes 2359304 | tf_op jit(solution)/shard_map/ppermute | solution.py:36
  52.8 0.0 collective-permute-done.13.refs_10_.refs_11_
  52.8 0.0 copy-start.5
  52.8 1.9 %collective-permute-start.9 = (bf16[48,8192]{1,0:T(8,128)(2,1)S(1)}, bf16[48,8192]{1,0:T(8,128)(2,1)}, u32[]{:S(2)}, u32[]{:S(2)}) collective-permute-start(bf16[48,8192]{1,0:T(8,128)(2,1)S(1)} %collective-permute-done.8.refs_5_.refs_6_), channel_id=1, source_target_pairs={{0,1},{1,0},{2,3},{3,2},{4,5},{5,4},{6,7},{7,6},{8,9},{9,8},{10,11... | collective-permute-start | bytes 2359304 | tf_op jit(solution)/shard_map/ppermute | solution.py:36
  54.7 0.0 collective-permute-done.11.refs_8_.refs_9_
  54.7 0.0 copy-start.6
  54.7 2.4 %collective-permute-start.14 = (bf16[48,8192]{1,0:T(8,128)(2,1)S(1)}, bf16[48,8192]{1,0:T(8,128)(2,1)}, u32[]{:S(2)}, u32[]{:S(2)}) collective-permute-start(bf16[48,8192]{1,0:T(8,128)(2,1)S(1)} %collective-permute-done.refs_11_.refs_12_), channel_id=1, source_target_pairs={{0,1},{1,0},{2,3},{3,2},{4,5},{5,4},{6,7},{7,6},{8,9},{9,8},{10,11... | collective-permute-start | bytes 2359304 | tf_op jit(solution)/shard_map/ppermute | solution.py:36
  57.1 9.1 %collective-permute-done.5.refs_7_.refs_18_ = bf16[48,8192]{1,0:T(8,128)(2,1)} collective-permute-done((bf16[48,8192]{1,0:T(8,128)(2,1)S(1)}, bf16[48,8192]{1,0:T(8,128)(2,1)}, u32[]{:S(2)}, u32[]{:S(2)}) %collective-permute-start.5) | collective-permute-done | bytes 786464 | tf_op jit(solution)/shard_map/ppermute | solution.py:36
  66.3 1.9 %collective-permute-start.6 = (bf16[48,8192]{1,0:T(8,128)(2,1)}, bf16[48,8192]{1,0:T(8,128)(2,1)}, u32[]{:S(2)}, u32[]{:S(2)}) collective-permute-start(bf16[48,8192]{1,0:T(8,128)(2,1)} %collective-permute-done.5.refs_7_.refs_18_), channel_id=1, source_target_pairs={{0,1},{1,0},{2,3},{3,2},{4,5},{5,4},{6,7},{7,6},{8,9},{9,8},{10,11... | collective-permute-start | bytes 2359304 | tf_op jit(solution)/shard_map/ppermute | solution.py:36
  68.2 14.4 %collective-permute-done.3.refs_5_.refs_16_ = bf16[48,8192]{1,0:T(8,128)(2,1)} collective-permute-done((bf16[48,8192]{1,0:T(8,128)(2,1)S(1)}, bf16[48,8192]{1,0:T(8,128)(2,1)}, u32[]{:S(2)}, u32[]{:S(2)}) %collective-permute-start.3) | collective-permute-done | bytes 786464 | tf_op jit(solution)/shard_map/ppermute | solution.py:36
  82.6 1.9 %collective-permute-start.4 = (bf16[48,8192]{1,0:T(8,128)(2,1)}, bf16[48,8192]{1,0:T(8,128)(2,1)}, u32[]{:S(2)}, u32[]{:S(2)}) collective-permute-start(bf16[48,8192]{1,0:T(8,128)(2,1)} %collective-permute-done.3.refs_5_.refs_16_), channel_id=1, source_target_pairs={{0,1},{1,0},{2,3},{3,2},{4,5},{5,4},{6,7},{7,6},{8,9},{9,8},{10,11... | collective-permute-start | bytes 2359304 | tf_op jit(solution)/shard_map/ppermute | solution.py:36
  84.6 0.0 collective-permute-done.1.refs_3_.refs_14_
  84.6 0.0 copy-done.4
  84.6 2.4 %collective-permute-start.2 = (bf16[48,8192]{1,0:T(8,128)(2,1)}, bf16[48,8192]{1,0:T(8,128)(2,1)}, u32[]{:S(2)}, u32[]{:S(2)}) collective-permute-start(bf16[48,8192]{1,0:T(8,128)(2,1)} %collective-permute-done.1.refs_3_.refs_14_), channel_id=1, source_target_pairs={{0,1},{1,0},{2,3},{3,2},{4,5},{5,4},{6,7},{7,6},{8,9},{9,8},{10,11... | collective-permute-start | bytes 2359304 | tf_op jit(solution)/shard_map/ppermute | solution.py:36
  87.0 0.0 copy-done.5
  87.0 0.0 copy-done.6
  87.1 0.7 stack.67.refs_2_
  87.8 0.0 collective-permute-done.9.refs_6_.refs_7_
  87.8 0.0 collective-permute-done.14.refs_12_.refs_13_
  87.8 10.5 %shard_map.77.refs_10_ = f32[32,128,128]{2,1,0:T(8,128)} custom-call(s32[32]{0:T(128)} %bitcast.29, s32[32]{0:T(128)} %bitcast.32, s32[16]{0:T(128)} %stack.67.refs_2_, bf16[48,8192]{1,0:T(8,128)(2,1)} %refs_4_.1, bf16[48,8192]{1,0:T(8,128)(2,1)} %copy-done.4, bf16[48,8192]{1,0:T(8,128)(2,1)} %copy-done.3, ...), custom_call_target="tpu_custom_call" | custom-call | flops 1006632960 | bytes 11337728 | tf_op jit(solution)/shard_map/pallas_call | solution.py:135
  98.3 0.0 collective-permute-done.6.refs_8_.refs_19_
  98.3 0.0 collective-permute-done.4.refs_6_.refs_17_
  98.3 0.0 collective-permute-done.2.refs_4_.refs_15_
  98.4 10.3 %shard_map.78 = f32[32,136,128]{2,1,0:T(8,128)} custom-call(s32[32]{0:T(128)} %bitcast.30, s32[32]{0:T(128)} %bitcast.33, s32[16]{0:T(128)} %stack.67.refs_2_, bf16[48,8192]{1,0:T(8,128)(2,1)} %collective-permute-done.1.refs_3_.refs_14_, bf16[48,8192]{1,0:T(8,128)(2,1)} %collective-permute-done.2.refs_4_.refs_15_, ...), custom_call_target="tpu_custom_call" | custom-call | flops 603979776 | bytes 10420224 | tf_op jit(solution)/shard_map/pallas_call | solution.py:135
  108.7 2.8 %convert_element_type.4 = f16[32,136,128]{2,1,0:T(8,128)(2,1)} convert(f32[32,136,128]{2,1,0:T(8,128)} %shard_map.78) | non-fusion elementwise | flops 557056 | bytes 3342336 | tf_op jit(solution)/shard_map/convert_element_type | solution.py:190
  111.5 17.6 %all-to-all-start = ((f16[32,136,128]{2,1,0:T(8,128)(2,1)}), f16[32,136,128]{2,1,0:T(8,128)(2,1)S(1)}, u32[]{:S(2)}, u32[]{:S(2)}) async-start(f16[32,136,128]{2,1,0:T(8,128)(2,1)} %convert_element_type.4), calls=%async_computation | async-start | bytes 2228224 | tf_op jit(solution)/shard_map/all_to_all | solution.py:190
  129.7 12.7 %shard_map.79 = bf16[768,896]{1,0:T(8,128)(2,1)} custom-call(s32[32]{0:T(128)} %bitcast.31, s32[32]{0:T(128)} %bitcast.34, s32[16]{0:T(128)} %stack.67.refs_2_, s32[1]{0:T(128)S(6)} %copy.8.refs_3_, bf16[48,8192]{1,0:T(8,128)(2,1)} %refs_4_.1, bf16[48,8192]{1,0:T(8,128)(2,1)} %copy-done.4, bf16[48,8192]{1,0:T(8,128)(2,1)} %copy-done.3, ...), custom_call_target="tpu_custom_call" | custom-call | flops 1610612736 | bytes 15007744 | tf_op jit(solution)/shard_map/pallas_call | solution.py:135
  142.5 16.3 %all-to-all-done = f16[32,136,128]{2,1,0:T(8,128)(2,1)S(1)} async-done(((f16[32,136,128]{2,1,0:T(8,128)(2,1)}), f16[32,136,128]{2,1,0:T(8,128)(2,1)S(1)}, u32[]{:S(2)}, u32[]{:S(2)}) %all-to-all-start) | async-done | bytes 1114144 | tf_op jit(solution)/shard_map/all_to_all | solution.py:190
  158.7 0.1 bitcast_convert_fusion
  158.9 0.2 fusion
  159.1 0.6 select_bitcast_fusion
  (7 shorter events, 0.0 us)
Async XLA Ops:
  0.6 24.1 %collective-permute-start.12 = (bf16[48,8192]{1,0:T(8,128)(2,1)}, bf16[48,8192]{1,0:T(8,128)(2,1)S(1)}, u32[]{:S(2)}, u32[]{:S(2)}) collective-permute-start(bf16[48,8192]{1,0:T(8,128)(2,1)} %refs_4_.1), channel_id=1, source_target_pairs={{0,4},{1,5},{2,6},{3,7},{4,0},{5,1},{6,2},{7,3},{8,12},{9,13},{10,... | collective-permute-start | bytes 2359304 | tf_op jit(solution)/shard_map/ppermute | solution.py:36
  4.0 36.4 %collective-permute-start.10 = (bf16[48,8192]{1,0:T(8,128)(2,1)}, bf16[48,8192]{1,0:T(8,128)(2,1)S(1)}, u32[]{:S(2)}, u32[]{:S(2)}) collective-permute-start(bf16[48,8192]{1,0:T(8,128)(2,1)} %refs_4_.1), channel_id=1, source_target_pairs={{0,6},{1,7},{2,0},{3,1},{4,2},{5,3},{6,4},{7,5},{8,14},{9,15},{10,... | collective-permute-start | bytes 2359304 | tf_op jit(solution)/shard_map/ppermute | solution.py:36
  11.1 31.2 %collective-permute-start = (bf16[48,8192]{1,0:T(8,128)(2,1)}, bf16[48,8192]{1,0:T(8,128)(2,1)S(1)}, u32[]{:S(2)}, u32[]{:S(2)}) collective-permute-start(bf16[48,8192]{1,0:T(8,128)(2,1)} %refs_4_.1), channel_id=1, source_target_pairs={{0,8},{1,9},{2,10},{3,11},{4,12},{5,13},{6,14},{7,15},{8,0},{9,1},... | collective-permute-start | bytes 2359304 | tf_op jit(solution)/shard_map/ppermute | solution.py:36
  16.8 28.8 %collective-permute-start.8 = (bf16[48,8192]{1,0:T(8,128)(2,1)}, bf16[48,8192]{1,0:T(8,128)(2,1)S(1)}, u32[]{:S(2)}, u32[]{:S(2)}) collective-permute-start(bf16[48,8192]{1,0:T(8,128)(2,1)} %refs_4_.1), channel_id=1, source_target_pairs={{0,2},{1,3},{2,4},{3,5},{4,6},{5,7},{6,0},{7,1},{8,10},{9,11},{10,... | collective-permute-start | bytes 2359304 | tf_op jit(solution)/shard_map/ppermute | solution.py:36
  22.0 25.7 %collective-permute-start.7 = (bf16[48,8192]{1,0:T(8,128)(2,1)}, bf16[48,8192]{1,0:T(8,128)(2,1)S(1)}, u32[]{:S(2)}, u32[]{:S(2)}) collective-permute-start(bf16[48,8192]{1,0:T(8,128)(2,1)} %refs_4_.1), channel_id=1, source_target_pairs={{0,1},{1,0},{2,3},{3,2},{4,5},{5,4},{6,7},{7,6},{8,9},{9,8},{10,11... | collective-permute-start | bytes 2359304 | tf_op jit(solution)/shard_map/ppermute | solution.py:36
  24.7 63.1 %copy-start = (bf16[48,8192]{1,0:T(8,128)(2,1)}, bf16[48,8192]{1,0:T(8,128)(2,1)S(1)}, u32[]{:S(2)}) copy-start(bf16[48,8192]{1,0:T(8,128)(2,1)S(1)} %collective-permute-done.12.refs_9_.refs_10_) | copy-start | bytes 2359300
  24.7 28.1 %collective-permute-start.13 = (bf16[48,8192]{1,0:T(8,128)(2,1)S(1)}, bf16[48,8192]{1,0:T(8,128)(2,1)S(1)}, u32[]{:S(2)}, u32[]{:S(2)}) collective-permute-start(bf16[48,8192]{1,0:T(8,128)(2,1)S(1)} %collective-permute-done.12.refs_9_.refs_10_), channel_id=1, source_target_pairs={{0,1},{1,0},{2,3},{3,2},{4,5},{5,4},{6,7},{7,6},{8,9},{9,8},{10,11... | collective-permute-start | bytes 2359304 | tf_op jit(solution)/shard_map/ppermute | solution.py:36
  40.4 47.4 %copy-start.1 = (bf16[48,8192]{1,0:T(8,128)(2,1)}, bf16[48,8192]{1,0:T(8,128)(2,1)S(1)}, u32[]{:S(2)}) copy-start(bf16[48,8192]{1,0:T(8,128)(2,1)S(1)} %collective-permute-done.10.refs_7_.refs_8_) | copy-start | bytes 2359300
  40.4 14.3 %collective-permute-start.11 = (bf16[48,8192]{1,0:T(8,128)(2,1)S(1)}, bf16[48,8192]{1,0:T(8,128)(2,1)S(1)}, u32[]{:S(2)}, u32[]{:S(2)}) collective-permute-start(bf16[48,8192]{1,0:T(8,128)(2,1)S(1)} %collective-permute-done.10.refs_7_.refs_8_), channel_id=1, source_target_pairs={{0,1},{1,0},{2,3},{3,2},{4,5},{5,4},{6,7},{7,6},{8,9},{9,8},{10,11... | collective-permute-start | bytes 2359304 | tf_op jit(solution)/shard_map/ppermute | solution.py:36
  42.3 45.5 %copy-start.2 = (bf16[48,8192]{1,0:T(8,128)(2,1)}, bf16[48,8192]{1,0:T(8,128)(2,1)S(1)}, u32[]{:S(2)}) copy-start(bf16[48,8192]{1,0:T(8,128)(2,1)S(1)} %collective-permute-done.refs_11_.refs_12_) | copy-start | bytes 2359300
  42.3 24.0 %collective-permute-start.5 = (bf16[48,8192]{1,0:T(8,128)(2,1)S(1)}, bf16[48,8192]{1,0:T(8,128)(2,1)}, u32[]{:S(2)}, u32[]{:S(2)}) collective-permute-start(bf16[48,8192]{1,0:T(8,128)(2,1)S(1)} %collective-permute-done.refs_11_.refs_12_), channel_id=1, source_target_pairs={{0,4},{1,5},{2,6},{3,7},{4,0},{5,1},{6,2},{7,3},{8,12},{9,13},{10,... | collective-permute-start | bytes 2359304 | tf_op jit(solution)/shard_map/ppermute | solution.py:36
  45.7 42.2 %copy-start.3 = (bf16[48,8192]{1,0:T(8,128)(2,1)}, bf16[48,8192]{1,0:T(8,128)(2,1)S(1)}, u32[]{:S(2)}) copy-start(bf16[48,8192]{1,0:T(8,128)(2,1)S(1)} %collective-permute-done.8.refs_5_.refs_6_) | copy-start | bytes 2359300
  45.7 37.0 %collective-permute-start.3 = (bf16[48,8192]{1,0:T(8,128)(2,1)S(1)}, bf16[48,8192]{1,0:T(8,128)(2,1)}, u32[]{:S(2)}, u32[]{:S(2)}) collective-permute-start(bf16[48,8192]{1,0:T(8,128)(2,1)S(1)} %collective-permute-done.refs_11_.refs_12_), channel_id=1, source_target_pairs={{0,6},{1,7},{2,0},{3,1},{4,2},{5,3},{6,4},{7,5},{8,14},{9,15},{10,... | collective-permute-start | bytes 2359304 | tf_op jit(solution)/shard_map/ppermute | solution.py:36
  47.6 36.9 %copy-start.4 = (bf16[48,8192]{1,0:T(8,128)(2,1)}, bf16[48,8192]{1,0:T(8,128)(2,1)S(1)}, u32[]{:S(2)}) copy-start(bf16[48,8192]{1,0:T(8,128)(2,1)S(1)} %collective-permute-done.7.refs_4_.refs_5_) | copy-start | bytes 2359300
  47.7 36.9 %collective-permute-start.1 = (bf16[48,8192]{1,0:T(8,128)(2,1)S(1)}, bf16[48,8192]{1,0:T(8,128)(2,1)}, u32[]{:S(2)}, u32[]{:S(2)}) collective-permute-start(bf16[48,8192]{1,0:T(8,128)(2,1)S(1)} %collective-permute-done.refs_11_.refs_12_), channel_id=1, source_target_pairs={{0,2},{1,3},{2,4},{3,5},{4,6},{5,7},{6,0},{7,1},{8,10},{9,11},{10,... | collective-permute-start | bytes 2359304 | tf_op jit(solution)/shard_map/ppermute | solution.py:36
  52.8 34.2 %copy-start.5 = (bf16[48,8192]{1,0:T(8,128)(2,1)}, bf16[48,8192]{1,0:T(8,128)(2,1)S(1)}, u32[]{:S(2)}) copy-start(bf16[48,8192]{1,0:T(8,128)(2,1)S(1)} %collective-permute-done.13.refs_10_.refs_11_) | copy-start | bytes 2359300
  52.8 35.0 %collective-permute-start.9 = (bf16[48,8192]{1,0:T(8,128)(2,1)S(1)}, bf16[48,8192]{1,0:T(8,128)(2,1)}, u32[]{:S(2)}, u32[]{:S(2)}) collective-permute-start(bf16[48,8192]{1,0:T(8,128)(2,1)S(1)} %collective-permute-done.8.refs_5_.refs_6_), channel_id=1, source_target_pairs={{0,1},{1,0},{2,3},{3,2},{4,5},{5,4},{6,7},{7,6},{8,9},{9,8},{10,11... | collective-permute-start | bytes 2359304 | tf_op jit(solution)/shard_map/ppermute | solution.py:36
  54.7 32.3 %copy-start.6 = (bf16[48,8192]{1,0:T(8,128)(2,1)}, bf16[48,8192]{1,0:T(8,128)(2,1)S(1)}, u32[]{:S(2)}) copy-start(bf16[48,8192]{1,0:T(8,128)(2,1)S(1)} %collective-permute-done.11.refs_8_.refs_9_) | copy-start | bytes 2359300
  54.7 33.1 %collective-permute-start.14 = (bf16[48,8192]{1,0:T(8,128)(2,1)S(1)}, bf16[48,8192]{1,0:T(8,128)(2,1)}, u32[]{:S(2)}, u32[]{:S(2)}) collective-permute-start(bf16[48,8192]{1,0:T(8,128)(2,1)S(1)} %collective-permute-done.refs_11_.refs_12_), channel_id=1, source_target_pairs={{0,1},{1,0},{2,3},{3,2},{4,5},{5,4},{6,7},{7,6},{8,9},{9,8},{10,11... | collective-permute-start | bytes 2359304 | tf_op jit(solution)/shard_map/ppermute | solution.py:36
  66.3 32.0 %collective-permute-start.6 = (bf16[48,8192]{1,0:T(8,128)(2,1)}, bf16[48,8192]{1,0:T(8,128)(2,1)}, u32[]{:S(2)}, u32[]{:S(2)}) collective-permute-start(bf16[48,8192]{1,0:T(8,128)(2,1)} %collective-permute-done.5.refs_7_.refs_18_), channel_id=1, source_target_pairs={{0,1},{1,0},{2,3},{3,2},{4,5},{5,4},{6,7},{7,6},{8,9},{9,8},{10,11... | collective-permute-start | bytes 2359304 | tf_op jit(solution)/shard_map/ppermute | solution.py:36
  82.6 15.7 %collective-permute-start.4 = (bf16[48,8192]{1,0:T(8,128)(2,1)}, bf16[48,8192]{1,0:T(8,128)(2,1)}, u32[]{:S(2)}, u32[]{:S(2)}) collective-permute-start(bf16[48,8192]{1,0:T(8,128)(2,1)} %collective-permute-done.3.refs_5_.refs_16_), channel_id=1, source_target_pairs={{0,1},{1,0},{2,3},{3,2},{4,5},{5,4},{6,7},{7,6},{8,9},{9,8},{10,11... | collective-permute-start | bytes 2359304 | tf_op jit(solution)/shard_map/ppermute | solution.py:36
  84.6 13.8 %collective-permute-start.2 = (bf16[48,8192]{1,0:T(8,128)(2,1)}, bf16[48,8192]{1,0:T(8,128)(2,1)}, u32[]{:S(2)}, u32[]{:S(2)}) collective-permute-start(bf16[48,8192]{1,0:T(8,128)(2,1)} %collective-permute-done.1.refs_3_.refs_14_), channel_id=1, source_target_pairs={{0,1},{1,0},{2,3},{3,2},{4,5},{5,4},{6,7},{7,6},{8,9},{9,8},{10,11... | collective-permute-start | bytes 2359304 | tf_op jit(solution)/shard_map/ppermute | solution.py:36
  111.5 47.3 %all-to-all-start = ((f16[32,136,128]{2,1,0:T(8,128)(2,1)}), f16[32,136,128]{2,1,0:T(8,128)(2,1)S(1)}, u32[]{:S(2)}, u32[]{:S(2)}) async-start(f16[32,136,128]{2,1,0:T(8,128)(2,1)} %convert_element_type.4), calls=%async_computation | async-start | bytes 2228224 | tf_op jit(solution)/shard_map/all_to_all | solution.py:190

commit v2 on v1

--- a/solution.py
+++ b/solution.py
@@ -48,15 +48,17 @@
 
 def weight_kernel(count, first, coded, rows_ref, cols_ref, offs_ref, *refs):
     pieces, hidden_ref, out_ref = refs[:count], refs[count], refs[-1]
-    height = pieces[0].shape[0]
-    offs = [pl.multiple_of(offs_ref[first + i], 16) for i in range(count)]
+    spans = [
+        pl.ds(pl.multiple_of(offs_ref[first + i], 16), piece.shape[0])
+        for i, piece in enumerate(pieces)
+    ]
 
     def pair_step(pair, carry):
         slots = (2 * pair, 2 * pair + 1)
         grad = gather_rows(pieces, blocks_of(cols_ref, slots))
         act = jnp.concatenate(
             [
-                jnp.concatenate([hidden_ref[pl.ds(o, height), r] for o in offs], 0)
+                jnp.concatenate([hidden_ref[span, r] for span in spans], 0)
                 for r in blocks_of(rows_ref, slots)
             ],
             1,
@@ -81,7 +83,6 @@
 
 def input_kernel(count, rows_ref, cols_ref, offs_ref, counts_ref, *refs):
     pieces, (weights_ref, out_ref, total) = refs[:count], refs[count:]
-    height = pieces[0].shape[0]
     total[...] = jnp.zeros_like(total)
     nothing = jnp.zeros((BLK, BLK), weights_ref.dtype)
 
@@ -103,46 +104,25 @@
         return carry
 
     lax.fori_loop(0, rows_ref.shape[0] // 2, pair_step, 0)
-    for i in range(count):
-        o = pl.multiple_of(offs_ref[i], 16)
-        out_ref[pl.ds(o, height), :] = total[i * height : (i + 1) * height, :].astype(out_ref.dtype)
-
-
-def staged(kernel, n_tables, n_in, out_staged, *refs):
-    tables, sources, out_ref = refs[:n_tables], refs[n_tables : n_tables + n_in], refs[n_tables + n_in]
-    sems, *held = refs[n_tables + n_in + 1 :]
-    held, extra = held[:n_in], held[n_in:]
-    copies = [pltpu.make_async_copy(sources[i], held[i], sems.at[i]) for i in range(n_in)]
-    for copy in copies:
-        copy.start()
-    for copy in copies:
-        copy.wait()
-    if not out_staged:
-        kernel(*tables, *held, out_ref, *extra)
-        return
-    kernel(*tables, *held, extra[0], *extra[1:])
-    copy = pltpu.make_async_copy(extra[0], out_ref, sems.at[n_in])
-    copy.start()
-    copy.wait()
-
-
-def call(kernel, tables, operands, out, scratch, flops, out_staged=False):
-    far = pl.BlockSpec(memory_space=pltpu.HBM)
-    zeros = (0,) * len(out.shape)
-    near = pl.BlockSpec(out.shape, lambda i, *_: zeros, pipeline_mode=pl.Buffered(1))
+    done = 0
+    for i, piece in enumerate(pieces):
+        height = piece.shape[0]
+        span = pl.ds(pl.multiple_of(offs_ref[i], 16), height)
+        out_ref[span, :] = total[done : done + height, :].astype(out_ref.dtype)
+        done += height
+
+
+def call(kernel, tables, operands, out, scratch, flops, grant):
     size = sum(v.size * v.dtype.itemsize for v in (*operands, out))
-    held = [pltpu.VMEM(v.shape, v.dtype) for v in operands + ((out,) if out_staged else ())]
+    held = pl.BlockSpec(memory_space=pltpu.VMEM)
+    table = pl.BlockSpec(memory_space=pltpu.SMEM)
     return pl.pallas_call(
-        functools.partial(staged, kernel, len(tables), len(operands), out_staged),
-        grid_spec=pltpu.PrefetchScalarGridSpec(
-            num_scalar_prefetch=len(tables),
-            grid=(1,),
-            in_specs=[far for _ in operands],
-            out_specs=far if out_staged else near,
-            scratch_shapes=[pltpu.SemaphoreType.DMA((len(operands) + 1,)), *held, *scratch],
-        ),
+        kernel,
+        in_specs=[table for _ in tables] + [held for _ in operands],
+        out_specs=held,
+        scratch_shapes=scratch,
         out_shape=out,
-        compiler_params=pltpu.CompilerParams(vmem_limit_bytes=GRANT),
+        compiler_params=pltpu.CompilerParams(vmem_limit_bytes=grant),
         cost_estimate=pl.CostEstimate(flops=flops, bytes_accessed=size, transcendentals=0),
     )(*tables, *operands)
 
@@ -152,16 +132,16 @@
     kernel = functools.partial(weight_kernel, len(pieces), first, coded)
     out = jax.ShapeDtypeStruct((slots, BLK + EXTRA * coded, BLK), jnp.float32)
     operands = (*pieces, hidden) + ((prior,) if coded else ())
-    flops = 4 * slots * len(pieces) * pieces[0].shape[0] * BLK * BLK
-    return call(kernel, tables, operands, out, [], flops, out_staged=not coded)
+    flops = 2 * slots * sum(p.shape[0] for p in pieces) * BLK * BLK
+    return call(kernel, tables, operands, out, [], flops, GRANT)
 
 
 def input_grads(pieces, tables, weights, like):
     kernel = functools.partial(input_kernel, len(pieces))
     out = jax.ShapeDtypeStruct(like.shape, like.dtype)
-    flops = 4 * weights.shape[0] * like.shape[0] * BLK * BLK
+    flops = 2 * weights.shape[0] * like.shape[0] * BLK * BLK
     scratch = [pltpu.VMEM(like.shape, jnp.float32)]
-    return call(kernel, tables, (*pieces, weights), out, scratch, flops)
+    return call(kernel, tables, (*pieces, weights), out, scratch, flops, 3 * GRANT)
 
 
 def shards(hidden, out_grad, weights, block_rows, block_cols, counts):
@@ -175,19 +155,32 @@
     half, x, core = me // HALF, (me // 2) % X, me % 2
 
     other = send(out_grad, swap_half)
-    near = [out_grad] + [send(out_grad, along_x(k)) for k in STEPS[1:]]
-    far = [other] + [send(other, along_x(k)) for k in STEPS[1:]]
-    pieces, places = [], []
-    for shards_, h in ((near, half), (far, 1 - half)):
-        for k, shard in zip(STEPS, shards_):
-            chip = h * HALF + (x - k) % X * 2
-            pieces += [shard, send(shard, swap_core)]
-            places += [(chip + core) * height, (chip + 1 - core) * height]
-    tables = (rows, cols, jnp.stack(places))
+    parts = {}
+    for side, own in (("near", out_grad), ("far", other)):
+        parts[side, 0] = own
+        parts[side, 1] = send(own, along_x(1))
+        parts[side, X - 1] = send(own, along_x(X - 1))
+    parts["near", 2] = send(parts["near", 1], along_x(1))
+    parts["far", 2] = send(parts["far", 1][:CUT], along_x(1))
+    parts["far", -2] = send(parts["far", X - 1][CUT:], along_x(X - 1))
+    pieces, table = [], []
+    for side, k in ORDER:
+        shard = parts[side, k]
+        pieces += [shard, send(shard, swap_core)]
+        start = CUT if k == -2 else 0
+        table += [(int(side == "far"), k % X, swapped, start) for swapped in (0, 1)]
+    flip, step, swapped, start = (jnp.array(v, jnp.int32) for v in zip(*table))
+    chip = (half ^ flip) * HALF + (x - step + X) % X * 2
+    tables = (rows, cols, (chip + (core ^ swapped)) * height + start)
 
     prior = weight_grads(pieces[:EARLY], 0, tables, hidden, slots)
     coded = weight_grads(pieces[EARLY:], EARLY, tables, hidden, slots, prior)
-    parts = lax.all_to_all(coded.astype(jnp.float16), "dp", split_axis=0, concat_axis=0, tiled=True)
+    parts = lax.all_to_all(
+        coded.astype(jnp.float16), "dp", split_axis=0, concat_axis=0, tiled=True
+    )
+    for i in range(EARLY, len(pieces), 2):
+        shard, _ = lax.optimization_barrier((pieces[i], coded))
+        pieces[i + 1] = send(shard, swap_core)
     input_grad = input_grads(pieces, (*tables, counts), weights, hidden)
 
     share = slots // lax.axis_size("dp")
@@ -198,9 +191,13 @@
     return summed[None], input_grad
 
 
-STEPS = (0, 1, X - 1, 2)
-EARLY = 2 * X + 2
-GRANT = 60 * 2**20
+ORDER = (
+    ("near", 0), ("near", 1), ("near", X - 1), ("far", 0),
+    ("near", 2), ("far", 1), ("far", X - 1), ("far", 2), ("far", -2),
+)
+EARLY = 8
+CUT = 16
+GRANT = 8 * 2**20
 
 
 def solution(mesh):

time: 163 us -> 182 us (1.12)
  the two profiles are of different devices: /device:TPU:6 before, /device:TPU:1 now
where the time goes in v2:
time: 182 us; the launch traced here: 180 us
  starting transfers between devices  95.6 us (53%)
  waiting for transfers between devices  32.3 us (18%)
  local copies, waits for them, and re-layouts  25.6 us (14%)
  Pallas kernels  20.8 us (11%)
  other arithmetic  4.1 us (2%)
    ppermute x22, starting transfers between devices, send(): lax.ppermute(value, 'tensor', [(i, target(i)) for i in range(MEMBERS)])  69.7 us
    ppermute x22, waiting for transfers between devices, send(): lax.ppermute(value, 'tensor', [(i, target(i)) for i in range(MEMBERS)])  32.3 us
    all_to_all x1, starting transfers between devices, body(): lax.all_to_all(coded.astype(jnp.float16), 'dp', split_axis=0, concat_axis...  25.9 us
    unnamed x58, local copies, waits for them, and re-layouts  24.9 us
    pallas_call x3, Pallas kernels, call(): pl.pallas_call(kernel, in_specs=[table for _ in tables] + [held for _ in...  20.8 us
  transfers between devices with their start and end apart: 23, of which 5 were waited for; matrix products, arithmetic and copies ran while one was open for 1% of the time, Pallas kernels for 8%

profile of v2, /device:TPU:1, one launch (start us, length us, event | category | flops | bytes accessed | tf_op | source)
XLA Modules:
  0.0 180.3 jit_solution(7075086571393353519)
XLA Ops:
  0.6 11.6 %collective-permute-start.3 = (bf16[48,8192]{1,0:T(8,128)(2,1)}, bf16[48,8192]{1,0:T(8,128)(2,1)S(1)}, u32[]{:S(2)}, u32[]{:S(2)}) collective-permute-start(bf16[48,8192]{1,0:T(8,128)(2,1)} %refs_0_.3), channel_id=1, source_target_pairs={{0,8},{1,9},{2,10},{3,11},{4,12},{5,13},{6,14},{7,15},{8,0},{9,1},... | collective-permute-start | bytes 2359304 | tf_op jit(solution)/shard_map/ppermute | solution.py:36
  12.2 3.1 %collective-permute-start = (bf16[48,8192]{1,0:T(8,128)(2,1)}, bf16[48,8192]{1,0:T(8,128)(2,1)S(1)}, u32[]{:S(2)}, u32[]{:S(2)}) collective-permute-start(bf16[48,8192]{1,0:T(8,128)(2,1)} %refs_0_.3), channel_id=1, source_target_pairs={{0,2},{1,3},{2,4},{3,5},{4,6},{5,7},{6,0},{7,1},{8,10},{9,11},{10,... | collective-permute-start | bytes 2359304 | tf_op jit(solution)/shard_map/ppermute | solution.py:36
  15.4 3.4 %collective-permute-start.14 = (bf16[48,8192]{1,0:T(8,128)(2,1)}, bf16[48,8192]{1,0:T(8,128)(2,1)S(1)}, u32[]{:S(2)}, u32[]{:S(2)}) collective-permute-start(bf16[48,8192]{1,0:T(8,128)(2,1)} %refs_0_.3), channel_id=1, source_target_pairs={{0,6},{1,7},{2,0},{3,1},{4,2},{5,3},{6,4},{7,5},{8,14},{9,15},{10,... | collective-permute-start | bytes 2359304 | tf_op jit(solution)/shard_map/ppermute | solution.py:36
  18.7 3.4 %collective-permute-start.12 = (bf16[48,8192]{1,0:T(8,128)(2,1)}, bf16[48,8192]{1,0:T(8,128)(2,1)S(1)}, u32[]{:S(2)}, u32[]{:S(2)}) collective-permute-start(bf16[48,8192]{1,0:T(8,128)(2,1)} %refs_0_.3), channel_id=1, source_target_pairs={{0,1},{1,0},{2,3},{3,2},{4,5},{5,4},{6,7},{7,6},{8,9},{9,8},{10,11... | collective-permute-start | bytes 2359304 | tf_op jit(solution)/shard_map/ppermute | solution.py:36
  22.2 6.8 %collective-permute-done.3.refs_6_ = bf16[48,8192]{1,0:T(8,128)(2,1)S(1)} collective-permute-done((bf16[48,8192]{1,0:T(8,128)(2,1)}, bf16[48,8192]{1,0:T(8,128)(2,1)S(1)}, u32[]{:S(2)}, u32[]{:S(2)}) %collective-permute-start.3) | collective-permute-done | bytes 786464 | tf_op jit(solution)/shard_map/ppermute | solution.py:36
  29.0 5.2 %collective-permute-start.6 = (bf16[48,8192]{1,0:T(8,128)(2,1)S(1)}, bf16[48,8192]{1,0:T(8,128)(2,1)S(1)}, u32[]{:S(2)}, u32[]{:S(2)}) collective-permute-start(bf16[48,8192]{1,0:T(8,128)(2,1)S(1)} %collective-permute-done.3.refs_6_), channel_id=1, source_target_pairs={{0,6},{1,7},{2,0},{3,1},{4,2},{5,3},{6,4},{7,5},{8,14},{9,15},{10,... | collective-permute-start | bytes 2359304 | tf_op jit(solution)/shard_map/ppermute | solution.py:36
  34.2 3.5 %collective-permute-start.16 = (bf16[48,8192]{1,0:T(8,128)(2,1)S(1)}, bf16[48,8192]{1,0:T(8,128)(2,1)S(1)}, u32[]{:S(2)}, u32[]{:S(2)}) collective-permute-start(bf16[48,8192]{1,0:T(8,128)(2,1)S(1)} %collective-permute-done.3.refs_6_), channel_id=1, source_target_pairs={{0,1},{1,0},{2,3},{3,2},{4,5},{5,4},{6,7},{7,6},{8,9},{9,8},{10,11... | collective-permute-start | bytes 2359304 | tf_op jit(solution)/shard_map/ppermute | solution.py:36
  37.7 1.9 %collective-permute-start.13 = (bf16[48,8192]{1,0:T(8,128)(2,1)S(1)}, bf16[48,8192]{1,0:T(8,128)(2,1)S(1)}, u32[]{:S(2)}, u32[]{:S(2)}) collective-permute-start(bf16[48,8192]{1,0:T(8,128)(2,1)S(1)} %collective-permute-done.refs_2_), channel_id=1, source_target_pairs={{0,1},{1,0},{2,3},{3,2},{4,5},{5,4},{6,7},{7,6},{8,9},{9,8},{10,11... | collective-permute-start | bytes 2359304 | tf_op jit(solution)/shard_map/ppermute | solution.py:36
  39.6 1.9 %collective-permute-start.4 = (bf16[48,8192]{1,0:T(8,128)(2,1)S(1)}, bf16[48,8192]{1,0:T(8,128)(2,1)S(1)}, u32[]{:S(2)}, u32[]{:S(2)}) collective-permute-start(bf16[48,8192]{1,0:T(8,128)(2,1)S(1)} %collective-permute-done.3.refs_6_), channel_id=1, source_target_pairs={{0,2},{1,3},{2,4},{3,5},{4,6},{5,7},{6,0},{7,1},{8,10},{9,11},{10,... | collective-permute-start | bytes 2359304 | tf_op jit(solution)/shard_map/ppermute | solution.py:36
  42.5 2.1 %collective-permute-start.1 = (bf16[48,8192]{1,0:T(8,128)(2,1)S(1)}, bf16[48,8192]{1,0:T(8,128)(2,1)}, u32[]{:S(2)}, u32[]{:S(2)}) collective-permute-start(bf16[48,8192]{1,0:T(8,128)(2,1)S(1)} %collective-permute-done.refs_2_), channel_id=1, source_target_pairs={{0,2},{1,3},{2,4},{3,5},{4,6},{5,7},{6,0},{7,1},{8,10},{9,11},{10,... | collective-permute-start | bytes 2359304 | tf_op jit(solution)/shard_map/ppermute | solution.py:36
  45.4 6.7 %collective-permute-done.6.refs_4_.refs_12_ = bf16[48,8192]{1,0:T(8,128)(2,1)S(1)} collective-permute-done((bf16[48,8192]{1,0:T(8,128)(2,1)S(1)}, bf16[48,8192]{1,0:T(8,128)(2,1)S(1)}, u32[]{:S(2)}, u32[]{:S(2)}) %collective-permute-start.6) | collective-permute-done | bytes 786464 | tf_op jit(solution)/shard_map/ppermute | solution.py:36
  52.2 4.0 %collective-permute-start.15 = (bf16[48,8192]{1,0:T(8,128)(2,1)S(1)}, bf16[48,8192]{1,0:T(8,128)(2,1)S(1)}, u32[]{:S(2)}, u32[]{:S(2)}) collective-permute-start(bf16[48,8192]{1,0:T(8,128)(2,1)S(1)} %collective-permute-done.14.refs_4_), channel_id=1, source_target_pairs={{0,1},{1,0},{2,3},{3,2},{4,5},{5,4},{6,7},{7,6},{8,9},{9,8},{10,11... | collective-permute-start | bytes 2359304 | tf_op jit(solution)/shard_map/ppermute | solution.py:36
  58.0 4.6 %collective-permute-start.10 = (bf16[32,8192]{1,0:T(8,128)(2,1)S(1)}, bf16[32,8192]{1,0:T(8,128)(2,1)S(1)}, u32[]{:S(2)}, u32[]{:S(2)}) collective-permute-start(bf16[32,8192]{1,0:T(8,128)(2,1)S(1)} %slice.17), channel_id=1, source_target_pairs={{0,6},{1,7},{2,0},{3,1},{4,2},{5,3},{6,4},{7,5},{8,14},{9,15},{10,... | collective-permute-start | bytes 1572872 | tf_op jit(solution)/shard_map/ppermute | solution.py:36
  63.5 2.2 %collective-permute-start.7 = (bf16[48,8192]{1,0:T(8,128)(2,1)S(1)}, bf16[48,8192]{1,0:T(8,128)(2,1)}, u32[]{:S(2)}, u32[]{:S(2)}) collective-permute-start(bf16[48,8192]{1,0:T(8,128)(2,1)S(1)} %collective-permute-done.6.refs_4_.refs_12_), channel_id=1, source_target_pairs={{0,1},{1,0},{2,3},{3,2},{4,5},{5,4},{6,7},{7,6},{8,9},{9,8},{10,11... | collective-permute-start | bytes 2359304 | tf_op jit(solution)/shard_map/ppermute | solution.py:36
  65.7 2.1 %collective-permute-start.5 = (bf16[48,8192]{1,0:T(8,128)(2,1)S(1)}, bf16[48,8192]{1,0:T(8,128)(2,1)}, u32[]{:S(2)}, u32[]{:S(2)}) collective-permute-start(bf16[48,8192]{1,0:T(8,128)(2,1)S(1)} %collective-permute-done.4.refs_2_.refs_10_), channel_id=1, source_target_pairs={{0,1},{1,0},{2,3},{3,2},{4,5},{5,4},{6,7},{7,6},{8,9},{9,8},{10,11... | collective-permute-start | bytes 2359304 | tf_op jit(solution)/shard_map/ppermute | solution.py:36
  67.9 10.5 %collective-permute-done.1.refs_0_.refs_8_ = bf16[48,8192]{1,0:T(8,128)(2,1)} collective-permute-done((bf16[48,8192]{1,0:T(8,128)(2,1)S(1)}, bf16[48,8192]{1,0:T(8,128)(2,1)}, u32[]{:S(2)}, u32[]{:S(2)}) %collective-permute-start.1) | collective-permute-done | bytes 786464 | tf_op jit(solution)/shard_map/ppermute | solution.py:36
  78.3 3.3 %collective-permute-start.2 = (bf16[48,8192]{1,0:T(8,128)(2,1)}, bf16[48,8192]{1,0:T(8,128)(2,1)}, u32[]{:S(2)}, u32[]{:S(2)}) collective-permute-start(bf16[48,8192]{1,0:T(8,128)(2,1)} %collective-permute-done.1.refs_0_.refs_8_), channel_id=1, source_target_pairs={{0,1},{1,0},{2,3},{3,2},{4,5},{5,4},{6,7},{7,6},{8,9},{9,8},{10,11... | collective-permute-start | bytes 2359304 | tf_op jit(solution)/shard_map/ppermute | solution.py:36
  83.2 1.9 %collective-permute-start.8 = (bf16[16,8192]{1,0:T(8,128)(2,1)}, bf16[16,8192]{1,0:T(8,128)(2,1)}, u32[]{:S(2)}, u32[]{:S(2)}) collective-permute-start(bf16[16,8192]{1,0:T(8,128)(2,1)} %slice.16), channel_id=1, source_target_pairs={{0,2},{1,3},{2,4},{3,5},{4,6},{5,7},{6,0},{7,1},{8,10},{9,11},{10,... | collective-permute-start | bytes 786440 | tf_op jit(solution)/shard_map/ppermute | solution.py:36
  85.2 1.9 %collective-permute-start.11 = (bf16[32,8192]{1,0:T(8,128)(2,1)S(1)}, bf16[32,8192]{1,0:T(8,128)(2,1)}, u32[]{:S(2)}, u32[]{:S(2)}) collective-permute-start(bf16[32,8192]{1,0:T(8,128)(2,1)S(1)} %collective-permute-done.10.refs_8_.refs_16_), channel_id=1, source_target_pairs={{0,1},{1,0},{2,3},{3,2},{4,5},{5,4},{6,7},{7,6},{8,9},{9,8},{10,11... | collective-permute-start | bytes 1572872 | tf_op jit(solution)/shard_map/ppermute | solution.py:36
  87.1 7.4 %collective-permute-done.8.refs_6_.refs_14_ = bf16[16,8192]{1,0:T(8,128)(2,1)} collective-permute-done((bf16[16,8192]{1,0:T(8,128)(2,1)}, bf16[16,8192]{1,0:T(8,128)(2,1)}, u32[]{:S(2)}, u32[]{:S(2)}) %collective-permute-start.8) | collective-permute-done | bytes 262176 | tf_op jit(solution)/shard_map/ppermute | solution.py:36
  94.5 2.8 %collective-permute-start.9 = (bf16[16,8192]{1,0:T(8,128)(2,1)}, bf16[16,8192]{1,0:T(8,128)(2,1)S(1)}, u32[]{:S(2)}, u32[]{:S(2)}) collective-permute-start(bf16[16,8192]{1,0:T(8,128)(2,1)} %collective-permute-done.8.refs_6_.refs_14_), channel_id=1, source_target_pairs={{0,1},{1,0},{2,3},{3,2},{4,5},{5,4},{6,7},{7,6},{8,9},{9,8},{10,11... | collective-permute-start | bytes 786440 | tf_op jit(solution)/shard_map/ppermute | solution.py:36
  98.0 1.1 copy-done.1
  99.2 1.1 copy-done.4
  100.3 1.1 copy-done.7
  101.4 1.1 copy-done.10
  102.6 1.1 copy-done.13
  103.7 1.1 copy-done.16
  104.8 1.1 copy-done.19
  106.0 1.1 copy-done.22
  108.4 4.9 %shard_map.113.refs_11_ = f32[32,128,128]{2,1,0:T(8,128)S(1)} custom-call(s32[32]{0:T(128)S(1)} %bitcast.12, s32[32]{0:T(128)S(1)} %bitcast.15, s32[18]{0:T(128)S(1)} %multiply_add_fusion.offs_ref, bf16[48,8192]{1,0:T(8,128)(2,1)S(1)} %copy-done.1, bf16[48,8192]{1,0:T(8,128)(2,1)S(1)} %copy-done.13, bf16[48,8192]{1,0:T(8,128)(2,1)S(1)} %copy-done.7, ...), custom_call_target="tpu_custom_call" | custom-call | flops 402653184 | bytes 9764864 | tf_op jit(solution)/shard_map/pallas_call | solution.py:119
  113.4 6.8 %shard_map.114 = f32[32,136,128]{2,1,0:T(8,128)S(1)} custom-call(s32[32]{0:T(128)S(1)} %bitcast.13, s32[32]{0:T(128)S(1)} %bitcast.16, s32[18]{0:T(128)S(1)} %multiply_add_fusion.offs_ref, bf16[48,8192]{1,0:T(8,128)(2,1)} %collective-permute-done.1.refs_0_.refs_8_, bf16[48,8192]{1,0:T(8,128)(2,1)} %collective-permute-done.2.refs_1_, ...), custom_call_target="tpu_custom_call" | custom-call | flops 402653184 | bytes 11993088 | tf_op jit(solution)/shard_map/pallas_call | solution.py:119
  120.2 1.1 convert_element_type.4
  121.4 25.9 %all-to-all-start = ((f16[32,136,128]{2,1,0:T(8,128)(2,1)}), f16[32,136,128]{2,1,0:T(8,128)(2,1)}, u32[]{:S(2)}, u32[]{:S(2)}) async-start(f16[32,136,128]{2,1,0:T(8,128)(2,1)} %convert_element_type.4), calls=%async_computation | async-start | bytes 2228224 | tf_op jit(solution)/shard_map/all_to_all | solution.py:178
  147.3 2.2 %collective-permute-start.17 = (bf16[48,8192]{1,0:T(8,128)(2,1)}, bf16[48,8192]{1,0:T(8,128)(2,1)}, u32[]{:S(2)}, u32[]{:S(2)}) collective-permute-start(bf16[48,8192]{1,0:T(8,128)(2,1)} %collective-permute-done.1.refs_0_.refs_8_), channel_id=1, source_target_pairs={{0,1},{1,0},{2,3},{3,2},{4,5},{5,4},{6,7},{7,6},{8,9},{9,8},{10,11... | collective-permute-start | bytes 2359304 | tf_op jit(solution)/shard_map/ppermute | solution.py:36
  149.5 2.1 %collective-permute-start.18 = (bf16[48,8192]{1,0:T(8,128)(2,1)S(1)}, bf16[48,8192]{1,0:T(8,128)(2,1)}, u32[]{:S(2)}, u32[]{:S(2)}) collective-permute-start(bf16[48,8192]{1,0:T(8,128)(2,1)S(1)} %collective-permute-done.4.refs_2_.refs_10_), channel_id=1, source_target_pairs={{0,1},{1,0},{2,3},{3,2},{4,5},{5,4},{6,7},{7,6},{8,9},{9,8},{10,11... | collective-permute-start | bytes 2359304 | tf_op jit(solution)/shard_map/ppermute | solution.py:36
  151.6 2.2 %collective-permute-start.19 = (bf16[48,8192]{1,0:T(8,128)(2,1)S(1)}, bf16[48,8192]{1,0:T(8,128)(2,1)}, u32[]{:S(2)}, u32[]{:S(2)}) collective-permute-start(bf16[48,8192]{1,0:T(8,128)(2,1)S(1)} %collective-permute-done.6.refs_4_.refs_12_), channel_id=1, source_target_pairs={{0,1},{1,0},{2,3},{3,2},{4,5},{5,4},{6,7},{7,6},{8,9},{9,8},{10,11... | collective-permute-start | bytes 2359304 | tf_op jit(solution)/shard_map/ppermute | solution.py:36
  153.8 2.1 %collective-permute-start.21 = (bf16[32,8192]{1,0:T(8,128)(2,1)S(1)}, bf16[32,8192]{1,0:T(8,128)(2,1)S(1)}, u32[]{:S(2)}, u32[]{:S(2)}) collective-permute-start(bf16[32,8192]{1,0:T(8,128)(2,1)S(1)} %collective-permute-done.10.refs_8_.refs_16_), channel_id=1, source_target_pairs={{0,1},{1,0},{2,3},{3,2},{4,5},{5,4},{6,7},{7,6},{8,9},{9,8},{10,11... | collective-permute-start | bytes 1572872 | tf_op jit(solution)/shard_map/ppermute | solution.py:36
  156.0 2.2 %collective-permute-start.20 = (bf16[16,8192]{1,0:T(8,128)(2,1)}, bf16[16,8192]{1,0:T(8,128)(2,1)}, u32[]{:S(2)}, u32[]{:S(2)}) collective-permute-start(bf16[16,8192]{1,0:T(8,128)(2,1)} %collective-permute-done.8.refs_6_.refs_14_), channel_id=1, source_target_pairs={{0,1},{1,0},{2,3},{3,2},{4,5},{5,4},{6,7},{7,6},{8,9},{9,8},{10,11... | collective-permute-start | bytes 786440 | tf_op jit(solution)/shard_map/ppermute | solution.py:36
  159.8 1.1 copy-done.5
  160.9 1.1 copy-done.8
  162.1 1.1 copy-done.11
  163.2 1.1 copy-done.14
  164.3 1.1 copy-done.17
  165.5 1.1 copy-done.20
  166.6 1.1 copy-done.23
  167.7 1.2 copy-done.24
  168.9 9.1 %shard_map.115 = bf16[768,896]{1,0:T(8,128)(2,1)} custom-call(s32[32]{0:T(128)S(1)} %bitcast.14, s32[32]{0:T(128)S(1)} %bitcast.17, s32[18]{0:T(128)S(1)} %multiply_add_fusion.offs_ref, s32[1]{0:T(128)S(6)} %copy.12.counts_ref, bf16[48,8192]{1,0:T(8,128)(2,1)S(1)} %copy-done.2, bf16[48,8192]{1,0:T(8,128)(2,1)S(1)} %copy-done.14, ...), custom_call_target="tpu_custom_call" | custom-call | flops 805306368 | bytes 15007744 | tf_op jit(solution)/shard_map/pallas_call | solution.py:119
  178.0 1.4 bitcast_convert_fusion
  (67 shorter events, 10.0 us)
Async XLA Ops:
  0.6 97.4 %copy-start = (bf16[768,896]{1,0:T(8,128)(2,1)S(1)}, bf16[768,896]{1,0:T(8,128)(2,1)}, u32[]{:S(2)}) copy-start(bf16[768,896]{1,0:T(8,128)(2,1)} %refs_10_.1) | copy-start | bytes 4128772
  0.6 28.4 %collective-permute-start.3 = (bf16[48,8192]{1,0:T(8,128)(2,1)}, bf16[48,8192]{1,0:T(8,128)(2,1)S(1)}, u32[]{:S(2)}, u32[]{:S(2)}) collective-permute-start(bf16[48,8192]{1,0:T(8,128)(2,1)} %refs_0_.3), channel_id=1, source_target_pairs={{0,8},{1,9},{2,10},{3,11},{4,12},{5,13},{6,14},{7,15},{8,0},{9,1},... | collective-permute-start | bytes 2359304 | tf_op jit(solution)/shard_map/ppermute | solution.py:36
  12.2 25.5 %collective-permute-start = (bf16[48,8192]{1,0:T(8,128)(2,1)}, bf16[48,8192]{1,0:T(8,128)(2,1)S(1)}, u32[]{:S(2)}, u32[]{:S(2)}) collective-permute-start(bf16[48,8192]{1,0:T(8,128)(2,1)} %refs_0_.3), channel_id=1, source_target_pairs={{0,2},{1,3},{2,4},{3,5},{4,6},{5,7},{6,0},{7,1},{8,10},{9,11},{10,... | collective-permute-start | bytes 2359304 | tf_op jit(solution)/shard_map/ppermute | solution.py:36
  15.4 24.3 %collective-permute-start.14 = (bf16[48,8192]{1,0:T(8,128)(2,1)}, bf16[48,8192]{1,0:T(8,128)(2,1)S(1)}, u32[]{:S(2)}, u32[]{:S(2)}) collective-permute-start(bf16[48,8192]{1,0:T(8,128)(2,1)} %refs_0_.3), channel_id=1, source_target_pairs={{0,6},{1,7},{2,0},{3,1},{4,2},{5,3},{6,4},{7,5},{8,14},{9,15},{10,... | collective-permute-start | bytes 2359304 | tf_op jit(solution)/shard_map/ppermute | solution.py:36
  18.7 22.8 %collective-permute-start.12 = (bf16[48,8192]{1,0:T(8,128)(2,1)}, bf16[48,8192]{1,0:T(8,128)(2,1)S(1)}, u32[]{:S(2)}, u32[]{:S(2)}) collective-permute-start(bf16[48,8192]{1,0:T(8,128)(2,1)} %refs_0_.3), channel_id=1, source_target_pairs={{0,1},{1,0},{2,3},{3,2},{4,5},{5,4},{6,7},{7,6},{8,9},{9,8},{10,11... | collective-permute-start | bytes 2359304 | tf_op jit(solution)/shard_map/ppermute | solution.py:36
  29.0 36.7 %copy-start.3 = (bf16[48,8192]{1,0:T(8,128)(2,1)}, bf16[48,8192]{1,0:T(8,128)(2,1)S(1)}, u32[]{:S(2)}) copy-start(bf16[48,8192]{1,0:T(8,128)(2,1)S(1)} %collective-permute-done.3.refs_6_) | copy-start | bytes 2359300
  29.0 23.2 %collective-permute-start.6 = (bf16[48,8192]{1,0:T(8,128)(2,1)S(1)}, bf16[48,8192]{1,0:T(8,128)(2,1)S(1)}, u32[]{:S(2)}, u32[]{:S(2)}) collective-permute-start(bf16[48,8192]{1,0:T(8,128)(2,1)S(1)} %collective-permute-done.3.refs_6_), channel_id=1, source_target_pairs={{0,6},{1,7},{2,0},{3,1},{4,2},{5,3},{6,4},{7,5},{8,14},{9,15},{10,... | collective-permute-start | bytes 2359304 | tf_op jit(solution)/shard_map/ppermute | solution.py:36
  34.2 22.9 %collective-permute-start.16 = (bf16[48,8192]{1,0:T(8,128)(2,1)S(1)}, bf16[48,8192]{1,0:T(8,128)(2,1)S(1)}, u32[]{:S(2)}, u32[]{:S(2)}) collective-permute-start(bf16[48,8192]{1,0:T(8,128)(2,1)S(1)} %collective-permute-done.3.refs_6_), channel_id=1, source_target_pairs={{0,1},{1,0},{2,3},{3,2},{4,5},{5,4},{6,7},{7,6},{8,9},{9,8},{10,11... | collective-permute-start | bytes 2359304 | tf_op jit(solution)/shard_map/ppermute | solution.py:36
  37.7 24.9 %collective-permute-start.13 = (bf16[48,8192]{1,0:T(8,128)(2,1)S(1)}, bf16[48,8192]{1,0:T(8,128)(2,1)S(1)}, u32[]{:S(2)}, u32[]{:S(2)}) collective-permute-start(bf16[48,8192]{1,0:T(8,128)(2,1)S(1)} %collective-permute-done.refs_2_), channel_id=1, source_target_pairs={{0,1},{1,0},{2,3},{3,2},{4,5},{5,4},{6,7},{7,6},{8,9},{9,8},{10,11... | collective-permute-start | bytes 2359304 | tf_op jit(solution)/shard_map/ppermute | solution.py:36
  39.6 26.1 %collective-permute-start.4 = (bf16[48,8192]{1,0:T(8,128)(2,1)S(1)}, bf16[48,8192]{1,0:T(8,128)(2,1)S(1)}, u32[]{:S(2)}, u32[]{:S(2)}) collective-permute-start(bf16[48,8192]{1,0:T(8,128)(2,1)S(1)} %collective-permute-done.3.refs_6_), channel_id=1, source_target_pairs={{0,2},{1,3},{2,4},{3,5},{4,6},{5,7},{6,0},{7,1},{8,10},{9,11},{10,... | collective-permute-start | bytes 2359304 | tf_op jit(solution)/shard_map/ppermute | solution.py:36
  41.6 0.9 copy-start.12
  42.5 35.8 %collective-permute-start.1 = (bf16[48,8192]{1,0:T(8,128)(2,1)S(1)}, bf16[48,8192]{1,0:T(8,128)(2,1)}, u32[]{:S(2)}, u32[]{:S(2)}) collective-permute-start(bf16[48,8192]{1,0:T(8,128)(2,1)S(1)} %collective-permute-done.refs_2_), channel_id=1, source_target_pairs={{0,2},{1,3},{2,4},{3,5},{4,6},{5,7},{6,0},{7,1},{8,10},{9,11},{10,... | collective-permute-start | bytes 2359304 | tf_op jit(solution)/shard_map/ppermute | solution.py:36
  52.2 30.1 %collective-permute-start.15 = (bf16[48,8192]{1,0:T(8,128)(2,1)S(1)}, bf16[48,8192]{1,0:T(8,128)(2,1)S(1)}, u32[]{:S(2)}, u32[]{:S(2)}) collective-permute-start(bf16[48,8192]{1,0:T(8,128)(2,1)S(1)} %collective-permute-done.14.refs_4_), channel_id=1, source_target_pairs={{0,1},{1,0},{2,3},{3,2},{4,5},{5,4},{6,7},{7,6},{8,9},{9,8},{10,11... | collective-permute-start | bytes 2359304 | tf_op jit(solution)/shard_map/ppermute | solution.py:36
  56.2 0.9 copy-start.9
  58.0 27.2 %collective-permute-start.10 = (bf16[32,8192]{1,0:T(8,128)(2,1)S(1)}, bf16[32,8192]{1,0:T(8,128)(2,1)S(1)}, u32[]{:S(2)}, u32[]{:S(2)}) collective-permute-start(bf16[32,8192]{1,0:T(8,128)(2,1)S(1)} %slice.17), channel_id=1, source_target_pairs={{0,6},{1,7},{2,0},{3,1},{4,2},{5,3},{6,4},{7,5},{8,14},{9,15},{10,... | collective-permute-start | bytes 1572872 | tf_op jit(solution)/shard_map/ppermute | solution.py:36
  62.6 0.9 copy-start.18
  63.5 49.8 %collective-permute-start.7 = (bf16[48,8192]{1,0:T(8,128)(2,1)S(1)}, bf16[48,8192]{1,0:T(8,128)(2,1)}, u32[]{:S(2)}, u32[]{:S(2)}) collective-permute-start(bf16[48,8192]{1,0:T(8,128)(2,1)S(1)} %collective-permute-done.6.refs_4_.refs_12_), channel_id=1, source_target_pairs={{0,1},{1,0},{2,3},{3,2},{4,5},{5,4},{6,7},{7,6},{8,9},{9,8},{10,11... | collective-permute-start | bytes 2359304 | tf_op jit(solution)/shard_map/ppermute | solution.py:36
  65.7 47.6 %collective-permute-start.5 = (bf16[48,8192]{1,0:T(8,128)(2,1)S(1)}, bf16[48,8192]{1,0:T(8,128)(2,1)}, u32[]{:S(2)}, u32[]{:S(2)}) collective-permute-start(bf16[48,8192]{1,0:T(8,128)(2,1)S(1)} %collective-permute-done.4.refs_2_.refs_10_), channel_id=1, source_target_pairs={{0,1},{1,0},{2,3},{3,2},{4,5},{5,4},{6,7},{7,6},{8,9},{9,8},{10,11... | collective-permute-start | bytes 2359304 | tf_op jit(solution)/shard_map/ppermute | solution.py:36
  78.3 35.0 %collective-permute-start.2 = (bf16[48,8192]{1,0:T(8,128)(2,1)}, bf16[48,8192]{1,0:T(8,128)(2,1)}, u32[]{:S(2)}, u32[]{:S(2)}) collective-permute-start(bf16[48,8192]{1,0:T(8,128)(2,1)} %collective-permute-done.1.refs_0_.refs_8_), channel_id=1, source_target_pairs={{0,1},{1,0},{2,3},{3,2},{4,5},{5,4},{6,7},{7,6},{8,9},{9,8},{10,11... | collective-permute-start | bytes 2359304 | tf_op jit(solution)/shard_map/ppermute | solution.py:36
  82.3 0.9 copy-start.21
  83.2 11.3 %collective-permute-start.8 = (bf16[16,8192]{1,0:T(8,128)(2,1)}, bf16[16,8192]{1,0:T(8,128)(2,1)}, u32[]{:S(2)}, u32[]{:S(2)}) collective-permute-start(bf16[16,8192]{1,0:T(8,128)(2,1)} %slice.16), channel_id=1, source_target_pairs={{0,2},{1,3},{2,4},{3,5},{4,6},{5,7},{6,0},{7,1},{8,10},{9,11},{10,... | collective-permute-start | bytes 786440 | tf_op jit(solution)/shard_map/ppermute | solution.py:36
  85.2 28.2 %collective-permute-start.11 = (bf16[32,8192]{1,0:T(8,128)(2,1)S(1)}, bf16[32,8192]{1,0:T(8,128)(2,1)}, u32[]{:S(2)}, u32[]{:S(2)}) collective-permute-start(bf16[32,8192]{1,0:T(8,128)(2,1)S(1)} %collective-permute-done.10.refs_8_.refs_16_), channel_id=1, source_target_pairs={{0,1},{1,0},{2,3},{3,2},{4,5},{5,4},{6,7},{7,6},{8,9},{9,8},{10,11... | collective-permute-start | bytes 1572872 | tf_op jit(solution)/shard_map/ppermute | solution.py:36
  94.5 18.8 %collective-permute-start.9 = (bf16[16,8192]{1,0:T(8,128)(2,1)}, bf16[16,8192]{1,0:T(8,128)(2,1)S(1)}, u32[]{:S(2)}, u32[]{:S(2)}) collective-permute-start(bf16[16,8192]{1,0:T(8,128)(2,1)} %collective-permute-done.8.refs_6_.refs_14_), channel_id=1, source_target_pairs={{0,1},{1,0},{2,3},{3,2},{4,5},{5,4},{6,7},{7,6},{8,9},{9,8},{10,11... | collective-permute-start | bytes 786440 | tf_op jit(solution)/shard_map/ppermute | solution.py:36
  98.0 1.1 copy-start.1
  99.2 1.1 copy-start.4
  100.3 1.1 copy-start.7
  101.4 1.1 copy-start.10
  102.6 1.1 copy-start.13
  103.7 1.1 copy-start.16
  104.8 1.1 copy-start.19
  106.0 1.1 copy-start.22
  120.2 39.6 %copy-start.2 = (bf16[48,8192]{1,0:T(8,128)(2,1)S(1)}, bf16[48,8192]{1,0:T(8,128)(2,1)}, u32[]{:S(2)}) copy-start(bf16[48,8192]{1,0:T(8,128)(2,1)} %refs_0_.3) | copy-start | bytes 2359300
  120.2 39.6 %copy-start.26 = (s32[1,32]{1,0:T(1,128)S(1)}, s32[1,32]{1,0:T(1,128)}, u32[]{:S(2)}) copy-start(s32[1,32]{1,0:T(1,128)} %param.13) | copy-start | bytes 388
  120.2 39.6 %copy-start.28 = (s32[1,32]{1,0:T(1,128)S(1)}, s32[1,32]{1,0:T(1,128)}, u32[]{:S(2)}) copy-start(s32[1,32]{1,0:T(1,128)} %param.14) | copy-start | bytes 388
  121.4 56.6 %all-to-all-start = ((f16[32,136,128]{2,1,0:T(8,128)(2,1)}), f16[32,136,128]{2,1,0:T(8,128)(2,1)}, u32[]{:S(2)}, u32[]{:S(2)}) async-start(f16[32,136,128]{2,1,0:T(8,128)(2,1)} %convert_element_type.4), calls=%async_computation | async-start | bytes 2228224 | tf_op jit(solution)/shard_map/all_to_all | solution.py:178
  147.3 12.5 %collective-permute-start.17 = (bf16[48,8192]{1,0:T(8,128)(2,1)}, bf16[48,8192]{1,0:T(8,128)(2,1)}, u32[]{:S(2)}, u32[]{:S(2)}) collective-permute-start(bf16[48,8192]{1,0:T(8,128)(2,1)} %collective-permute-done.1.refs_0_.refs_8_), channel_id=1, source_target_pairs={{0,1},{1,0},{2,3},{3,2},{4,5},{5,4},{6,7},{7,6},{8,9},{9,8},{10,11... | collective-permute-start | bytes 2359304 | tf_op jit(solution)/shard_map/ppermute | solution.py:36
  149.5 10.3 %collective-permute-start.18 = (bf16[48,8192]{1,0:T(8,128)(2,1)S(1)}, bf16[48,8192]{1,0:T(8,128)(2,1)}, u32[]{:S(2)}, u32[]{:S(2)}) collective-permute-start(bf16[48,8192]{1,0:T(8,128)(2,1)S(1)} %collective-permute-done.4.refs_2_.refs_10_), channel_id=1, source_target_pairs={{0,1},{1,0},{2,3},{3,2},{4,5},{5,4},{6,7},{7,6},{8,9},{9,8},{10,11... | collective-permute-start | bytes 2359304 | tf_op jit(solution)/shard_map/ppermute | solution.py:36
  151.6 8.1 %collective-permute-start.19 = (bf16[48,8192]{1,0:T(8,128)(2,1)S(1)}, bf16[48,8192]{1,0:T(8,128)(2,1)}, u32[]{:S(2)}, u32[]{:S(2)}) collective-permute-start(bf16[48,8192]{1,0:T(8,128)(2,1)S(1)} %collective-permute-done.6.refs_4_.refs_12_), channel_id=1, source_target_pairs={{0,1},{1,0},{2,3},{3,2},{4,5},{5,4},{6,7},{7,6},{8,9},{9,8},{10,11... | collective-permute-start | bytes 2359304 | tf_op jit(solution)/shard_map/ppermute | solution.py:36
  153.8 5.9 %collective-permute-start.21 = (bf16[32,8192]{1,0:T(8,128)(2,1)S(1)}, bf16[32,8192]{1,0:T(8,128)(2,1)S(1)}, u32[]{:S(2)}, u32[]{:S(2)}) collective-permute-start(bf16[32,8192]{1,0:T(8,128)(2,1)S(1)} %collective-permute-done.10.refs_8_.refs_16_), channel_id=1, source_target_pairs={{0,1},{1,0},{2,3},{3,2},{4,5},{5,4},{6,7},{7,6},{8,9},{9,8},{10,11... | collective-permute-start | bytes 1572872 | tf_op jit(solution)/shard_map/ppermute | solution.py:36
  156.0 3.8 %collective-permute-start.20 = (bf16[16,8192]{1,0:T(8,128)(2,1)}, bf16[16,8192]{1,0:T(8,128)(2,1)}, u32[]{:S(2)}, u32[]{:S(2)}) collective-permute-start(bf16[16,8192]{1,0:T(8,128)(2,1)} %collective-permute-done.8.refs_6_.refs_14_), channel_id=1, source_target_pairs={{0,1},{1,0},{2,3},{3,2},{4,5},{5,4},{6,7},{7,6},{8,9},{9,8},{10,11... | collective-permute-start | bytes 786440 | tf_op jit(solution)/shard_map/ppermute | solution.py:36
  159.8 1.1 copy-start.5
  160.9 1.1 copy-start.8
  162.1 1.1 copy-start.11
  163.2 1.1 copy-start.14
  164.3 1.1 copy-start.17
  165.5 1.1 copy-start.20
  166.6 1.1 copy-start.23
  167.7 1.2 copy-start.24
  (4 other events, 3.1 us)

commit v3 on v2

--- a/solution.py
+++ b/solution.py
@@ -42,11 +42,14 @@
     )
 
 
-def blocks_of(table_ref, slots):
-    return [pl.ds(pl.multiple_of(table_ref[s] * BLK, BLK), BLK) for s in slots]
-
-
-def weight_kernel(count, first, coded, rows_ref, cols_ref, offs_ref, *refs):
+def blocks_of(cells_ref, wide, slots):
+    cells = [cells_ref[s] for s in slots]
+    rows = [pl.ds(pl.multiple_of(lax.div(c, wide) * BLK, BLK), BLK) for c in cells]
+    cols = [pl.ds(pl.multiple_of(lax.rem(c, wide) * BLK, BLK), BLK) for c in cells]
+    return rows, cols
+
+
+def weight_kernel(count, first, coded, cells_ref, offs_ref, *refs):
     pieces, hidden_ref, out_ref = refs[:count], refs[count], refs[-1]
     spans = [
         pl.ds(pl.multiple_of(offs_ref[first + i], 16), piece.shape[0])
@@ -55,11 +58,12 @@
 
     def pair_step(pair, carry):
         slots = (2 * pair, 2 * pair + 1)
-        grad = gather_rows(pieces, blocks_of(cols_ref, slots))
+        rows, cols = blocks_of(cells_ref, pieces[0].shape[1] // BLK, slots)
+        grad = gather_rows(pieces, cols)
         act = jnp.concatenate(
             [
                 jnp.concatenate([hidden_ref[span, r] for span in spans], 0)
-                for r in blocks_of(rows_ref, slots)
+                for r in rows
             ],
             1,
         )
@@ -78,17 +82,18 @@
                 out_ref[s] = block
         return carry
 
-    lax.fori_loop(0, rows_ref.shape[0] // 2, pair_step, 0)
-
-
-def input_kernel(count, rows_ref, cols_ref, offs_ref, counts_ref, *refs):
+    lax.fori_loop(0, cells_ref.shape[0] // 2, pair_step, 0)
+
+
+def input_kernel(count, cells_ref, offs_ref, counts_ref, *refs):
     pieces, (weights_ref, out_ref, total) = refs[:count], refs[count:]
     total[...] = jnp.zeros_like(total)
     nothing = jnp.zeros((BLK, BLK), weights_ref.dtype)
 
     def pair_step(pair, carry):
         slots = (2 * pair, 2 * pair + 1)
-        grad = gather_rows(pieces, blocks_of(cols_ref, slots))
+        rows, cols = blocks_of(cells_ref, pieces[0].shape[1] // BLK, slots)
+        grad = gather_rows(pieces, cols)
         w = []
         for s in slots:
             live = (s < counts_ref[0]).astype(jnp.float32)
@@ -99,11 +104,11 @@
         moved = lax.dot_general(
             grad, both, (((1,), (1,)), ((), ())), preferred_element_type=jnp.float32
         )
-        for k, r in enumerate(blocks_of(rows_ref, slots)):
+        for k, r in enumerate(rows):
             total[:, r] += moved[:, k * BLK : (k + 1) * BLK]
         return carry
 
-    lax.fori_loop(0, rows_ref.shape[0] // 2, pair_step, 0)
+    lax.fori_loop(0, cells_ref.shape[0] // 2, pair_step, 0)
     done = 0
     for i, piece in enumerate(pieces):
         height = piece.shape[0]
@@ -171,7 +176,8 @@
         table += [(int(side == "far"), k % X, swapped, start) for swapped in (0, 1)]
     flip, step, swapped, start = (jnp.array(v, jnp.int32) for v in zip(*table))
     chip = (half ^ flip) * HALF + (x - step + X) % X * 2
-    tables = (rows, cols, (chip + (core ^ swapped)) * height + start)
+    cells = rows * (out_grad.shape[1] // BLK) + cols
+    tables = (cells, (chip + (core ^ swapped)) * height + start)
 
     prior = weight_grads(pieces[:EARLY], 0, tables, hidden, slots)
     coded = weight_grads(pieces[EARLY:], EARLY, tables, hidden, slots, prior)
@@ -184,18 +190,19 @@
     input_grad = input_grads(pieces, (*tables, counts), weights, hidden)
 
     share = slots // lax.axis_size("dp")
-    parts = parts.astype(jnp.float32).reshape(-1, share, BLK + EXTRA, BLK)
-    summed = (parts[:, :, :BLK] * jnp.exp2(parts[:, :, BLK : BLK + 1] - SHIFT)).sum(0)
+    values = parts[:, :BLK].astype(jnp.float32)
+    powers = parts[:, BLK : BLK + 1].astype(jnp.float32)
+    summed = (values * jnp.exp2(powers - SHIFT)).reshape(-1, share, BLK, BLK).sum(0)
     mine = lax.axis_index("dp") * share + jnp.arange(share, dtype=jnp.int32)
     summed = jnp.where((mine < counts[0])[:, None, None], summed, 0.0)
     return summed[None], input_grad
 
 
 ORDER = (
-    ("near", 0), ("near", 1), ("near", X - 1), ("far", 0),
-    ("near", 2), ("far", 1), ("far", X - 1), ("far", 2), ("far", -2),
+    ("near", 0), ("near", 1), ("near", X - 1),
+    ("near", 2), ("far", 0), ("far", 1), ("far", X - 1), ("far", 2), ("far", -2),
 )
-EARLY = 8
+EARLY = 6
 CUT = 16
 GRANT = 8 * 2**20
 

time: 182 us -> 182 us (level)
  starting transfers between devices: 95.6 us -> 99.5 us
  local copies, waits for them, and re-layouts: 25.6 us -> 21.9 us
    ppermute x22 -> x23, starting transfers between devices: 69.7 us -> 74.9 us  [send(): lax.ppermute(value, 'tensor', [(i, target(i)) for i in range(MEMBERS)])]
    unnamed x58 -> x64, local copies, waits for them, and re-layouts: 24.9 us -> 21.9 us
    ppermute x22 -> x23, waiting for transfers between devices: 32.3 us -> 31.5 us  [send(): lax.ppermute(value, 'tensor', [(i, target(i)) for i in range(MEMBERS)])]
  transfers between devices with their start and end apart: 23 -> 24, of which waited for: 5 -> 5; matrix products, arithmetic and copies ran while one was open for 1% -> 0% of each run, Pallas kernels for 8% -> 8%
where the time goes in v3:
time: 182 us; the launch traced here: 181 us
  starting transfers between devices  99.5 us (55%)
  waiting for transfers between devices  31.5 us (17%)
  local copies, waits for them, and re-layouts  21.9 us (12%)
  Pallas kernels  21.5 us (12%)
  other arithmetic  4.14 us (2%)
  between operations  1.92 us (1%)
    ppermute x23, starting transfers between devices, send(): lax.ppermute(value, 'tensor', [(i, target(i)) for i in range(MEMBERS)])  74.9 us
    ppermute x23, waiting for transfers between devices, send(): lax.ppermute(value, 'tensor', [(i, target(i)) for i in range(MEMBERS)])  31.5 us
    all_to_all x1, starting transfers between devices, body(): lax.all_to_all(coded.astype(jnp.float16), 'dp', split_axis=0, concat_axis...  24.6 us
    unnamed x64, local copies, waits for them, and re-layouts  21.9 us
    pallas_call x3, Pallas kernels, call(): pl.pallas_call(kernel, in_specs=[table for _ in tables] + [held for _ in...  21.5 us
  transfers between devices with their start and end apart: 24, of which 5 were waited for; matrix products, arithmetic and copies ran while one was open for 0% of the time, Pallas kernels for 8%

profile of v3, /device:TPU:1, one launch (start us, length us, event | category | flops | bytes accessed | tf_op | source)
XLA Modules:
  0.0 180.5 jit_solution(2512117357748282517)
XLA Ops:
  0.7 11.6 %collective-permute-start.3 = (bf16[48,8192]{1,0:T(8,128)(2,1)}, bf16[48,8192]{1,0:T(8,128)(2,1)S(1)}, u32[]{:S(2)}, u32[]{:S(2)}) collective-permute-start(bf16[48,8192]{1,0:T(8,128)(2,1)} %refs_0_.3), channel_id=1, source_target_pairs={{0,8},{1,9},{2,10},{3,11},{4,12},{5,13},{6,14},{7,15},{8,0},{9,1},... | collective-permute-start | bytes 2359304 | tf_op jit(solution)/shard_map/ppermute | solution.py:36
  12.3 3.1 %collective-permute-start = (bf16[48,8192]{1,0:T(8,128)(2,1)}, bf16[48,8192]{1,0:T(8,128)(2,1)S(1)}, u32[]{:S(2)}, u32[]{:S(2)}) collective-permute-start(bf16[48,8192]{1,0:T(8,128)(2,1)} %refs_0_.3), channel_id=1, source_target_pairs={{0,2},{1,3},{2,4},{3,5},{4,6},{5,7},{6,0},{7,1},{8,10},{9,11},{10,... | collective-permute-start | bytes 2359304 | tf_op jit(solution)/shard_map/ppermute | solution.py:36
  15.4 3.4 %collective-permute-start.15 = (bf16[48,8192]{1,0:T(8,128)(2,1)}, bf16[48,8192]{1,0:T(8,128)(2,1)S(1)}, u32[]{:S(2)}, u32[]{:S(2)}) collective-permute-start(bf16[48,8192]{1,0:T(8,128)(2,1)} %refs_0_.3), channel_id=1, source_target_pairs={{0,6},{1,7},{2,0},{3,1},{4,2},{5,3},{6,4},{7,5},{8,14},{9,15},{10,... | collective-permute-start | bytes 2359304 | tf_op jit(solution)/shard_map/ppermute | solution.py:36
  18.8 3.4 %collective-permute-start.13 = (bf16[48,8192]{1,0:T(8,128)(2,1)}, bf16[48,8192]{1,0:T(8,128)(2,1)S(1)}, u32[]{:S(2)}, u32[]{:S(2)}) collective-permute-start(bf16[48,8192]{1,0:T(8,128)(2,1)} %refs_0_.3), channel_id=1, source_target_pairs={{0,1},{1,0},{2,3},{3,2},{4,5},{5,4},{6,7},{7,6},{8,9},{9,8},{10,11... | collective-permute-start | bytes 2359304 | tf_op jit(solution)/shard_map/ppermute | solution.py:36
  22.3 6.8 %collective-permute-done.3.refs_2_.refs_8_ = bf16[48,8192]{1,0:T(8,128)(2,1)S(1)} collective-permute-done((bf16[48,8192]{1,0:T(8,128)(2,1)}, bf16[48,8192]{1,0:T(8,128)(2,1)S(1)}, u32[]{:S(2)}, u32[]{:S(2)}) %collective-permute-start.3) | collective-permute-done | bytes 786464 | tf_op jit(solution)/shard_map/ppermute | solution.py:36
  29.1 5.2 %collective-permute-start.7 = (bf16[48,8192]{1,0:T(8,128)(2,1)S(1)}, bf16[48,8192]{1,0:T(8,128)(2,1)S(1)}, u32[]{:S(2)}, u32[]{:S(2)}) collective-permute-start(bf16[48,8192]{1,0:T(8,128)(2,1)S(1)} %collective-permute-done.3.refs_2_.refs_8_), channel_id=1, source_target_pairs={{0,6},{1,7},{2,0},{3,1},{4,2},{5,3},{6,4},{7,5},{8,14},{9,15},{10,... | collective-permute-start | bytes 2359304 | tf_op jit(solution)/shard_map/ppermute | solution.py:36
  34.3 3.5 %collective-permute-start.14 = (bf16[48,8192]{1,0:T(8,128)(2,1)S(1)}, bf16[48,8192]{1,0:T(8,128)(2,1)S(1)}, u32[]{:S(2)}, u32[]{:S(2)}) collective-permute-start(bf16[48,8192]{1,0:T(8,128)(2,1)S(1)} %collective-permute-done.refs_2_), channel_id=1, source_target_pairs={{0,1},{1,0},{2,3},{3,2},{4,5},{5,4},{6,7},{7,6},{8,9},{9,8},{10,11... | collective-permute-start | bytes 2359304 | tf_op jit(solution)/shard_map/ppermute | solution.py:36
  37.8 3.3 %collective-permute-start.16 = (bf16[48,8192]{1,0:T(8,128)(2,1)S(1)}, bf16[48,8192]{1,0:T(8,128)(2,1)S(1)}, u32[]{:S(2)}, u32[]{:S(2)}) collective-permute-start(bf16[48,8192]{1,0:T(8,128)(2,1)S(1)} %collective-permute-done.15.refs_4_), channel_id=1, source_target_pairs={{0,1},{1,0},{2,3},{3,2},{4,5},{5,4},{6,7},{7,6},{8,9},{9,8},{10,11... | collective-permute-start | bytes 2359304 | tf_op jit(solution)/shard_map/ppermute | solution.py:36
  42.0 3.1 %collective-permute-start.5 = (bf16[48,8192]{1,0:T(8,128)(2,1)S(1)}, bf16[48,8192]{1,0:T(8,128)(2,1)S(1)}, u32[]{:S(2)}, u32[]{:S(2)}) collective-permute-start(bf16[48,8192]{1,0:T(8,128)(2,1)S(1)} %collective-permute-done.3.refs_2_.refs_8_), channel_id=1, source_target_pairs={{0,2},{1,3},{2,4},{3,5},{4,6},{5,7},{6,0},{7,1},{8,10},{9,11},{10,... | collective-permute-start | bytes 2359304 | tf_op jit(solution)/shard_map/ppermute | solution.py:36
  46.0 2.8 %collective-permute-start.1 = (bf16[48,8192]{1,0:T(8,128)(2,1)S(1)}, bf16[48,8192]{1,0:T(8,128)(2,1)}, u32[]{:S(2)}, u32[]{:S(2)}) collective-permute-start(bf16[48,8192]{1,0:T(8,128)(2,1)S(1)} %collective-permute-done.refs_2_), channel_id=1, source_target_pairs={{0,2},{1,3},{2,4},{3,5},{4,6},{5,7},{6,0},{7,1},{8,10},{9,11},{10,... | collective-permute-start | bytes 2359304 | tf_op jit(solution)/shard_map/ppermute | solution.py:36
  48.9 3.4 %collective-permute-done.7.refs_6_.refs_12_ = bf16[48,8192]{1,0:T(8,128)(2,1)S(1)} collective-permute-done((bf16[48,8192]{1,0:T(8,128)(2,1)S(1)}, bf16[48,8192]{1,0:T(8,128)(2,1)S(1)}, u32[]{:S(2)}, u32[]{:S(2)}) %collective-permute-start.7) | collective-permute-done | bytes 786464 | tf_op jit(solution)/shard_map/ppermute | solution.py:36
  52.3 4.0 %collective-permute-start.4 = (bf16[48,8192]{1,0:T(8,128)(2,1)S(1)}, bf16[48,8192]{1,0:T(8,128)(2,1)S(1)}, u32[]{:S(2)}, u32[]{:S(2)}) collective-permute-start(bf16[48,8192]{1,0:T(8,128)(2,1)S(1)} %collective-permute-done.3.refs_2_.refs_8_), channel_id=1, source_target_pairs={{0,1},{1,0},{2,3},{3,2},{4,5},{5,4},{6,7},{7,6},{8,9},{9,8},{10,11... | collective-permute-start | bytes 2359304 | tf_op jit(solution)/shard_map/ppermute | solution.py:36
  58.1 4.6 %collective-permute-start.11 = (bf16[32,8192]{1,0:T(8,128)(2,1)S(1)}, bf16[32,8192]{1,0:T(8,128)(2,1)S(1)}, u32[]{:S(2)}, u32[]{:S(2)}) collective-permute-start(bf16[32,8192]{1,0:T(8,128)(2,1)S(1)} %slice.17), channel_id=1, source_target_pairs={{0,6},{1,7},{2,0},{3,1},{4,2},{5,3},{6,4},{7,5},{8,14},{9,15},{10,... | collective-permute-start | bytes 1572872 | tf_op jit(solution)/shard_map/ppermute | solution.py:36
  63.5 2.2 %collective-permute-start.8 = (bf16[48,8192]{1,0:T(8,128)(2,1)S(1)}, bf16[48,8192]{1,0:T(8,128)(2,1)}, u32[]{:S(2)}, u32[]{:S(2)}) collective-permute-start(bf16[48,8192]{1,0:T(8,128)(2,1)S(1)} %collective-permute-done.7.refs_6_.refs_12_), channel_id=1, source_target_pairs={{0,1},{1,0},{2,3},{3,2},{4,5},{5,4},{6,7},{7,6},{8,9},{9,8},{10,11... | collective-permute-start | bytes 2359304 | tf_op jit(solution)/shard_map/ppermute | solution.py:36
  65.7 2.1 %collective-permute-start.6 = (bf16[48,8192]{1,0:T(8,128)(2,1)S(1)}, bf16[48,8192]{1,0:T(8,128)(2,1)}, u32[]{:S(2)}, u32[]{:S(2)}) collective-permute-start(bf16[48,8192]{1,0:T(8,128)(2,1)S(1)} %collective-permute-done.5.refs_4_.refs_10_), channel_id=1, source_target_pairs={{0,1},{1,0},{2,3},{3,2},{4,5},{5,4},{6,7},{7,6},{8,9},{9,8},{10,11... | collective-permute-start | bytes 2359304 | tf_op jit(solution)/shard_map/ppermute | solution.py:36
  67.9 13.3 %collective-permute-done.1.refs_0_.refs_6_ = bf16[48,8192]{1,0:T(8,128)(2,1)} collective-permute-done((bf16[48,8192]{1,0:T(8,128)(2,1)S(1)}, bf16[48,8192]{1,0:T(8,128)(2,1)}, u32[]{:S(2)}, u32[]{:S(2)}) %collective-permute-start.1) | collective-permute-done | bytes 786464 | tf_op jit(solution)/shard_map/ppermute | solution.py:36
  81.2 2.8 %collective-permute-start.2 = (bf16[48,8192]{1,0:T(8,128)(2,1)}, bf16[48,8192]{1,0:T(8,128)(2,1)}, u32[]{:S(2)}, u32[]{:S(2)}) collective-permute-start(bf16[48,8192]{1,0:T(8,128)(2,1)} %collective-permute-done.1.refs_0_.refs_6_), channel_id=1, source_target_pairs={{0,1},{1,0},{2,3},{3,2},{4,5},{5,4},{6,7},{7,6},{8,9},{9,8},{10,11... | collective-permute-start | bytes 2359304 | tf_op jit(solution)/shard_map/ppermute | solution.py:36
  84.0 1.0 copy-done.22
  85.0 1.9 %collective-permute-start.9 = (bf16[16,8192]{1,0:T(8,128)(2,1)S(1)}, bf16[16,8192]{1,0:T(8,128)(2,1)}, u32[]{:S(2)}, u32[]{:S(2)}) collective-permute-start(bf16[16,8192]{1,0:T(8,128)(2,1)S(1)} %slice.16), channel_id=1, source_target_pairs={{0,2},{1,3},{2,4},{3,5},{4,6},{5,7},{6,0},{7,1},{8,10},{9,11},{10,... | collective-permute-start | bytes 786440 | tf_op jit(solution)/shard_map/ppermute | solution.py:36
  86.9 2.2 %collective-permute-start.12 = (bf16[32,8192]{1,0:T(8,128)(2,1)S(1)}, bf16[32,8192]{1,0:T(8,128)(2,1)}, u32[]{:S(2)}, u32[]{:S(2)}) collective-permute-start(bf16[32,8192]{1,0:T(8,128)(2,1)S(1)} %collective-permute-done.11.refs_10_.refs_16_), channel_id=1, source_target_pairs={{0,1},{1,0},{2,3},{3,2},{4,5},{5,4},{6,7},{7,6},{8,9},{9,8},{10,11... | collective-permute-start | bytes 1572872 | tf_op jit(solution)/shard_map/ppermute | solution.py:36
  89.1 6.9 %collective-permute-done.9.refs_8_.refs_14_ = bf16[16,8192]{1,0:T(8,128)(2,1)} collective-permute-done((bf16[16,8192]{1,0:T(8,128)(2,1)S(1)}, bf16[16,8192]{1,0:T(8,128)(2,1)}, u32[]{:S(2)}, u32[]{:S(2)}) %collective-permute-start.9) | collective-permute-done | bytes 262176 | tf_op jit(solution)/shard_map/ppermute | solution.py:36
  96.0 2.8 %collective-permute-start.10 = (bf16[16,8192]{1,0:T(8,128)(2,1)}, bf16[16,8192]{1,0:T(8,128)(2,1)}, u32[]{:S(2)}, u32[]{:S(2)}) collective-permute-start(bf16[16,8192]{1,0:T(8,128)(2,1)} %collective-permute-done.9.refs_8_.refs_14_), channel_id=1, source_target_pairs={{0,1},{1,0},{2,3},{3,2},{4,5},{5,4},{6,7},{7,6},{8,9},{9,8},{10,11... | collective-permute-start | bytes 786440 | tf_op jit(solution)/shard_map/ppermute | solution.py:36
  98.9 1.1 copy-done.1
  100.1 1.1 copy-done.4
  101.2 1.1 copy-done.7
  102.3 1.1 copy-done.10
  103.5 1.1 copy-done.13
  104.6 1.1 copy-done.16
  105.7 4.9 %shard_map.113.refs_13_ = f32[32,128,128]{2,1,0:T(8,128)S(1)} custom-call(s32[32]{0:T(128)S(1)} %add_bitcast_fusion.cells_ref, s32[18]{0:T(128)S(1)} %multiply_add_fusion.offs_ref, bf16[48,8192]{1,0:T(8,128)(2,1)S(1)} %copy-done.1, bf16[48,8192]{1,0:T(8,128)(2,1)S(1)} %copy-done.10, bf16[48,8192]{1,0:T(8,128)(2,1)S(1)} %copy-done.4, ...), custom_call_target="tpu_custom_call" | custom-call | flops 301989888 | bytes 8192000 | tf_op jit(solution)/shard_map/pallas_call | solution.py:124
  110.7 7.5 %shard_map.114 = f32[32,136,128]{2,1,0:T(8,128)S(1)} custom-call(s32[32]{0:T(128)S(1)} %add_bitcast_fusion.cells_ref, s32[18]{0:T(128)S(1)} %multiply_add_fusion.offs_ref, bf16[48,8192]{1,0:T(8,128)(2,1)} %collective-permute-done.1.refs_0_.refs_6_, bf16[48,8192]{1,0:T(8,128)(2,1)} %collective-permute-done.2.refs_1_, bf16[48,8192]{1,0:T(8,128)(2,1)S(1)} %copy-done.19, ...), custom_call_target="tpu_custom_call" | custom-call | flops 503316480 | bytes 13565952 | tf_op jit(solution)/shard_map/pallas_call | solution.py:124
  118.2 1.2 convert_element_type.9
  119.3 24.6 %all-to-all-start = ((f16[32,136,128]{2,1,0:T(8,128)(2,1)}), f16[32,136,128]{2,1,0:T(8,128)(2,1)}, u32[]{:S(2)}, u32[]{:S(2)}) async-start(f16[32,136,128]{2,1,0:T(8,128)(2,1)} %convert_element_type.9), calls=%async_computation | async-start | bytes 2228224 | tf_op jit(solution)/shard_map/all_to_all | solution.py:184
  144.0 2.2 %collective-permute-start.21 = (bf16[16,8192]{1,0:T(8,128)(2,1)}, bf16[16,8192]{1,0:T(8,128)(2,1)S(1)}, u32[]{:S(2)}, u32[]{:S(2)}) collective-permute-start(bf16[16,8192]{1,0:T(8,128)(2,1)} %collective-permute-done.9.refs_8_.refs_14_), channel_id=1, source_target_pairs={{0,1},{1,0},{2,3},{3,2},{4,5},{5,4},{6,7},{7,6},{8,9},{9,8},{10,11... | collective-permute-start | bytes 786440 | tf_op jit(solution)/shard_map/ppermute | solution.py:36
  146.2 2.1 %collective-permute-start.19 = (bf16[48,8192]{1,0:T(8,128)(2,1)S(1)}, bf16[48,8192]{1,0:T(8,128)(2,1)}, u32[]{:S(2)}, u32[]{:S(2)}) collective-permute-start(bf16[48,8192]{1,0:T(8,128)(2,1)S(1)} %collective-permute-done.5.refs_4_.refs_10_), channel_id=1, source_target_pairs={{0,1},{1,0},{2,3},{3,2},{4,5},{5,4},{6,7},{7,6},{8,9},{9,8},{10,11... | collective-permute-start | bytes 2359304 | tf_op jit(solution)/shard_map/ppermute | solution.py:36
  148.3 2.2 %collective-permute-start.20 = (bf16[48,8192]{1,0:T(8,128)(2,1)S(1)}, bf16[48,8192]{1,0:T(8,128)(2,1)}, u32[]{:S(2)}, u32[]{:S(2)}) collective-permute-start(bf16[48,8192]{1,0:T(8,128)(2,1)S(1)} %collective-permute-done.7.refs_6_.refs_12_), channel_id=1, source_target_pairs={{0,1},{1,0},{2,3},{3,2},{4,5},{5,4},{6,7},{7,6},{8,9},{9,8},{10,11... | collective-permute-start | bytes 2359304 | tf_op jit(solution)/shard_map/ppermute | solution.py:36
  150.5 2.1 %collective-permute-start.17 = (bf16[48,8192]{1,0:T(8,128)(2,1)}, bf16[48,8192]{1,0:T(8,128)(2,1)}, u32[]{:S(2)}, u32[]{:S(2)}) collective-permute-start(bf16[48,8192]{1,0:T(8,128)(2,1)} %collective-permute-done.1.refs_0_.refs_6_), channel_id=1, source_target_pairs={{0,1},{1,0},{2,3},{3,2},{4,5},{5,4},{6,7},{7,6},{8,9},{9,8},{10,11... | collective-permute-start | bytes 2359304 | tf_op jit(solution)/shard_map/ppermute | solution.py:36
  152.7 2.2 %collective-permute-start.18 = (bf16[48,8192]{1,0:T(8,128)(2,1)}, bf16[48,8192]{1,0:T(8,128)(2,1)}, u32[]{:S(2)}, u32[]{:S(2)}) collective-permute-start(bf16[48,8192]{1,0:T(8,128)(2,1)} %copy-done.18), channel_id=1, source_target_pairs={{0,1},{1,0},{2,3},{3,2},{4,5},{5,4},{6,7},{7,6},{8,9},{9,8},{10,11... | collective-permute-start | bytes 2359304 | tf_op jit(solution)/shard_map/ppermute | solution.py:36
  155.6 2.1 %collective-permute-start.22 = (bf16[32,8192]{1,0:T(8,128)(2,1)S(1)}, bf16[32,8192]{1,0:T(8,128)(2,1)S(1)}, u32[]{:S(2)}, u32[]{:S(2)}) collective-permute-start(bf16[32,8192]{1,0:T(8,128)(2,1)S(1)} %collective-permute-done.11.refs_10_.refs_16_), channel_id=1, source_target_pairs={{0,1},{1,0},{2,3},{3,2},{4,5},{5,4},{6,7},{7,6},{8,9},{9,8},{10,11... | collective-permute-start | bytes 1572872 | tf_op jit(solution)/shard_map/ppermute | solution.py:36
  158.4 1.0 collective-permute-done.22.refs_17_
  159.4 1.1 copy-done.5
  160.6 1.1 copy-done.8
  161.7 1.1 copy-done.11
  162.8 1.1 copy-done.14
  164.0 1.1 copy-done.17
  165.1 1.1 copy-done.20
  166.2 1.2 copy-done.21
  168.4 9.2 %shard_map.115 = bf16[768,896]{1,0:T(8,128)(2,1)} custom-call(s32[32]{0:T(128)S(1)} %add_bitcast_fusion.cells_ref, s32[18]{0:T(128)S(1)} %multiply_add_fusion.offs_ref, s32[1]{0:T(128)S(6)} %copy.12.counts_ref, bf16[48,8192]{1,0:T(8,128)(2,1)S(1)} %copy-done.2, bf16[48,8192]{1,0:T(8,128)(2,1)S(1)} %copy-done.11, bf16[48,8192]{1,0:T(8,128)(2,1)S(1)} %copy-done.5, ...), custom_call_target="tpu_custom_call" | custom-call | flops 805306368 | bytes 15007744 | tf_op jit(solution)/shard_map/pallas_call | solution.py:124
  178.5 1.5 multiply_reduce_fusion
  (75 shorter events, 7.8 us)
Async XLA Ops:
  0.6 98.2 %copy-start.26 = (s32[18]{0:T(128)S(1)}, s32[18]{0:T(128)}, u32[]{:S(2)}) copy-start(s32[18]{0:T(128)} %constant.84.clone) | copy-start | bytes 220
  0.6 98.2 %copy-start.27 = (s32[18]{0:T(128)S(1)}, s32[18]{0:T(128)}, u32[]{:S(2)}) copy-start(s32[18]{0:T(128)} %constant.86.clone) | copy-start | bytes 220
  0.7 98.2 %copy-start.28 = (s32[18]{0:T(128)S(1)}, s32[18]{0:T(128)}, u32[]{:S(2)}) copy-start(s32[18]{0:T(128)} %constant.87.clone) | copy-start | bytes 220
  0.7 98.2 %copy-start.29 = (s32[18]{0:T(128)S(1)}, s32[18]{0:T(128)}, u32[]{:S(2)}) copy-start(s32[18]{0:T(128)} %constant.93) | copy-start | bytes 220
  0.7 98.1 %copy-start.31 = (s32[1,32]{1,0:T(1,128)S(1)}, s32[1,32]{1,0:T(1,128)}, u32[]{:S(2)}) copy-start(s32[1,32]{1,0:T(1,128)} %param.13) | copy-start | bytes 388
  0.7 98.1 %copy-start.30 = (s32[1,32]{1,0:T(1,128)S(1)}, s32[1,32]{1,0:T(1,128)}, u32[]{:S(2)}) copy-start(s32[1,32]{1,0:T(1,128)} %param.14) | copy-start | bytes 388
  0.7 98.2 %copy-start = (bf16[768,896]{1,0:T(8,128)(2,1)S(1)}, bf16[768,896]{1,0:T(8,128)(2,1)}, u32[]{:S(2)}) copy-start(bf16[768,896]{1,0:T(8,128)(2,1)} %refs_12_.1) | copy-start | bytes 4128772
  0.7 28.4 %collective-permute-start.3 = (bf16[48,8192]{1,0:T(8,128)(2,1)}, bf16[48,8192]{1,0:T(8,128)(2,1)S(1)}, u32[]{:S(2)}, u32[]{:S(2)}) collective-permute-start(bf16[48,8192]{1,0:T(8,128)(2,1)} %refs_0_.3), channel_id=1, source_target_pairs={{0,8},{1,9},{2,10},{3,11},{4,12},{5,13},{6,14},{7,15},{8,0},{9,1},... | collective-permute-start | bytes 2359304 | tf_op jit(solution)/shard_map/ppermute | solution.py:36
  12.3 22.0 %collective-permute-start = (bf16[48,8192]{1,0:T(8,128)(2,1)}, bf16[48,8192]{1,0:T(8,128)(2,1)S(1)}, u32[]{:S(2)}, u32[]{:S(2)}) collective-permute-start(bf16[48,8192]{1,0:T(8,128)(2,1)} %refs_0_.3), channel_id=1, source_target_pairs={{0,2},{1,3},{2,4},{3,5},{4,6},{5,7},{6,0},{7,1},{8,10},{9,11},{10,... | collective-permute-start | bytes 2359304 | tf_op jit(solution)/shard_map/ppermute | solution.py:36
  15.4 22.4 %collective-permute-start.15 = (bf16[48,8192]{1,0:T(8,128)(2,1)}, bf16[48,8192]{1,0:T(8,128)(2,1)S(1)}, u32[]{:S(2)}, u32[]{:S(2)}) collective-permute-start(bf16[48,8192]{1,0:T(8,128)(2,1)} %refs_0_.3), channel_id=1, source_target_pairs={{0,6},{1,7},{2,0},{3,1},{4,2},{5,3},{6,4},{7,5},{8,14},{9,15},{10,... | collective-permute-start | bytes 2359304 | tf_op jit(solution)/shard_map/ppermute | solution.py:36
  18.8 26.3 %collective-permute-start.13 = (bf16[48,8192]{1,0:T(8,128)(2,1)}, bf16[48,8192]{1,0:T(8,128)(2,1)S(1)}, u32[]{:S(2)}, u32[]{:S(2)}) collective-permute-start(bf16[48,8192]{1,0:T(8,128)(2,1)} %refs_0_.3), channel_id=1, source_target_pairs={{0,1},{1,0},{2,3},{3,2},{4,5},{5,4},{6,7},{7,6},{8,9},{9,8},{10,11... | collective-permute-start | bytes 2359304 | tf_op jit(solution)/shard_map/ppermute | solution.py:36
  29.1 23.2 %collective-permute-start.7 = (bf16[48,8192]{1,0:T(8,128)(2,1)S(1)}, bf16[48,8192]{1,0:T(8,128)(2,1)S(1)}, u32[]{:S(2)}, u32[]{:S(2)}) collective-permute-start(bf16[48,8192]{1,0:T(8,128)(2,1)S(1)} %collective-permute-done.3.refs_2_.refs_8_), channel_id=1, source_target_pairs={{0,6},{1,7},{2,0},{3,1},{4,2},{5,3},{6,4},{7,5},{8,14},{9,15},{10,... | collective-permute-start | bytes 2359304 | tf_op jit(solution)/shard_map/ppermute | solution.py:36
  34.3 31.4 %copy-start.3 = (bf16[48,8192]{1,0:T(8,128)(2,1)}, bf16[48,8192]{1,0:T(8,128)(2,1)S(1)}, u32[]{:S(2)}) copy-start(bf16[48,8192]{1,0:T(8,128)(2,1)S(1)} %collective-permute-done.refs_2_) | copy-start | bytes 2359300
  34.3 22.9 %collective-permute-start.14 = (bf16[48,8192]{1,0:T(8,128)(2,1)S(1)}, bf16[48,8192]{1,0:T(8,128)(2,1)S(1)}, u32[]{:S(2)}, u32[]{:S(2)}) collective-permute-start(bf16[48,8192]{1,0:T(8,128)(2,1)S(1)} %collective-permute-done.refs_2_), channel_id=1, source_target_pairs={{0,1},{1,0},{2,3},{3,2},{4,5},{5,4},{6,7},{7,6},{8,9},{9,8},{10,11... | collective-permute-start | bytes 2359304 | tf_op jit(solution)/shard_map/ppermute | solution.py:36
  37.8 24.8 %collective-permute-start.16 = (bf16[48,8192]{1,0:T(8,128)(2,1)S(1)}, bf16[48,8192]{1,0:T(8,128)(2,1)S(1)}, u32[]{:S(2)}, u32[]{:S(2)}) collective-permute-start(bf16[48,8192]{1,0:T(8,128)(2,1)S(1)} %collective-permute-done.15.refs_4_), channel_id=1, source_target_pairs={{0,1},{1,0},{2,3},{3,2},{4,5},{5,4},{6,7},{7,6},{8,9},{9,8},{10,11... | collective-permute-start | bytes 2359304 | tf_op jit(solution)/shard_map/ppermute | solution.py:36
  42.0 23.7 %collective-permute-start.5 = (bf16[48,8192]{1,0:T(8,128)(2,1)S(1)}, bf16[48,8192]{1,0:T(8,128)(2,1)S(1)}, u32[]{:S(2)}, u32[]{:S(2)}) collective-permute-start(bf16[48,8192]{1,0:T(8,128)(2,1)S(1)} %collective-permute-done.3.refs_2_.refs_8_), channel_id=1, source_target_pairs={{0,2},{1,3},{2,4},{3,5},{4,6},{5,7},{6,0},{7,1},{8,10},{9,11},{10,... | collective-permute-start | bytes 2359304 | tf_op jit(solution)/shard_map/ppermute | solution.py:36
  46.0 35.1 %collective-permute-start.1 = (bf16[48,8192]{1,0:T(8,128)(2,1)S(1)}, bf16[48,8192]{1,0:T(8,128)(2,1)}, u32[]{:S(2)}, u32[]{:S(2)}) collective-permute-start(bf16[48,8192]{1,0:T(8,128)(2,1)S(1)} %collective-permute-done.refs_2_), channel_id=1, source_target_pairs={{0,2},{1,3},{2,4},{3,5},{4,6},{5,7},{6,0},{7,1},{8,10},{9,11},{10,... | collective-permute-start | bytes 2359304 | tf_op jit(solution)/shard_map/ppermute | solution.py:36
  52.3 31.7 %collective-permute-start.4 = (bf16[48,8192]{1,0:T(8,128)(2,1)S(1)}, bf16[48,8192]{1,0:T(8,128)(2,1)S(1)}, u32[]{:S(2)}, u32[]{:S(2)}) collective-permute-start(bf16[48,8192]{1,0:T(8,128)(2,1)S(1)} %collective-permute-done.3.refs_2_.refs_8_), channel_id=1, source_target_pairs={{0,1},{1,0},{2,3},{3,2},{4,5},{5,4},{6,7},{7,6},{8,9},{9,8},{10,11... | collective-permute-start | bytes 2359304 | tf_op jit(solution)/shard_map/ppermute | solution.py:36
  58.1 28.8 %collective-permute-start.11 = (bf16[32,8192]{1,0:T(8,128)(2,1)S(1)}, bf16[32,8192]{1,0:T(8,128)(2,1)S(1)}, u32[]{:S(2)}, u32[]{:S(2)}) collective-permute-start(bf16[32,8192]{1,0:T(8,128)(2,1)S(1)} %slice.17), channel_id=1, source_target_pairs={{0,6},{1,7},{2,0},{3,1},{4,2},{5,3},{6,4},{7,5},{8,14},{9,15},{10,... | collective-permute-start | bytes 1572872 | tf_op jit(solution)/shard_map/ppermute | solution.py:36
  63.5 47.1 %collective-permute-start.8 = (bf16[48,8192]{1,0:T(8,128)(2,1)S(1)}, bf16[48,8192]{1,0:T(8,128)(2,1)}, u32[]{:S(2)}, u32[]{:S(2)}) collective-permute-start(bf16[48,8192]{1,0:T(8,128)(2,1)S(1)} %collective-permute-done.7.refs_6_.refs_12_), channel_id=1, source_target_pairs={{0,1},{1,0},{2,3},{3,2},{4,5},{5,4},{6,7},{7,6},{8,9},{9,8},{10,11... | collective-permute-start | bytes 2359304 | tf_op jit(solution)/shard_map/ppermute | solution.py:36
  65.7 44.9 %collective-permute-start.6 = (bf16[48,8192]{1,0:T(8,128)(2,1)S(1)}, bf16[48,8192]{1,0:T(8,128)(2,1)}, u32[]{:S(2)}, u32[]{:S(2)}) collective-permute-start(bf16[48,8192]{1,0:T(8,128)(2,1)S(1)} %collective-permute-done.5.refs_4_.refs_10_), channel_id=1, source_target_pairs={{0,1},{1,0},{2,3},{3,2},{4,5},{5,4},{6,7},{7,6},{8,9},{9,8},{10,11... | collective-permute-start | bytes 2359304 | tf_op jit(solution)/shard_map/ppermute | solution.py:36
  81.2 29.5 %collective-permute-start.2 = (bf16[48,8192]{1,0:T(8,128)(2,1)}, bf16[48,8192]{1,0:T(8,128)(2,1)}, u32[]{:S(2)}, u32[]{:S(2)}) collective-permute-start(bf16[48,8192]{1,0:T(8,128)(2,1)} %collective-permute-done.1.refs_0_.refs_6_), channel_id=1, source_target_pairs={{0,1},{1,0},{2,3},{3,2},{4,5},{5,4},{6,7},{7,6},{8,9},{9,8},{10,11... | collective-permute-start | bytes 2359304 | tf_op jit(solution)/shard_map/ppermute | solution.py:36
  85.0 11.0 %collective-permute-start.9 = (bf16[16,8192]{1,0:T(8,128)(2,1)S(1)}, bf16[16,8192]{1,0:T(8,128)(2,1)}, u32[]{:S(2)}, u32[]{:S(2)}) collective-permute-start(bf16[16,8192]{1,0:T(8,128)(2,1)S(1)} %slice.16), channel_id=1, source_target_pairs={{0,2},{1,3},{2,4},{3,5},{4,6},{5,7},{6,0},{7,1},{8,10},{9,11},{10,... | collective-permute-start | bytes 786440 | tf_op jit(solution)/shard_map/ppermute | solution.py:36
  86.9 23.8 %collective-permute-start.12 = (bf16[32,8192]{1,0:T(8,128)(2,1)S(1)}, bf16[32,8192]{1,0:T(8,128)(2,1)}, u32[]{:S(2)}, u32[]{:S(2)}) collective-permute-start(bf16[32,8192]{1,0:T(8,128)(2,1)S(1)} %collective-permute-done.11.refs_10_.refs_16_), channel_id=1, source_target_pairs={{0,1},{1,0},{2,3},{3,2},{4,5},{5,4},{6,7},{7,6},{8,9},{9,8},{10,11... | collective-permute-start | bytes 1572872 | tf_op jit(solution)/shard_map/ppermute | solution.py:36
  96.0 14.6 %collective-permute-start.10 = (bf16[16,8192]{1,0:T(8,128)(2,1)}, bf16[16,8192]{1,0:T(8,128)(2,1)}, u32[]{:S(2)}, u32[]{:S(2)}) collective-permute-start(bf16[16,8192]{1,0:T(8,128)(2,1)} %collective-permute-done.9.refs_8_.refs_14_), channel_id=1, source_target_pairs={{0,1},{1,0},{2,3},{3,2},{4,5},{5,4},{6,7},{7,6},{8,9},{9,8},{10,11... | collective-permute-start | bytes 786440 | tf_op jit(solution)/shard_map/ppermute | solution.py:36
  98.9 1.1 copy-start.1
  100.1 1.1 copy-start.4
  101.2 1.1 copy-start.7
  102.3 1.1 copy-start.10
  103.5 1.1 copy-start.13
  104.6 1.1 copy-start.16
  105.7 4.9 %copy-start.19 = (bf16[48,8192]{1,0:T(8,128)(2,1)S(1)}, bf16[48,8192]{1,0:T(8,128)(2,1)}, u32[]{:S(2)}) copy-start(bf16[48,8192]{1,0:T(8,128)(2,1)} %copy-done.18) | copy-start | bytes 2359300
  105.7 4.9 %copy-start.23 = (bf16[48,8192]{1,0:T(8,128)(2,1)S(1)}, bf16[48,8192]{1,0:T(8,128)(2,1)}, u32[]{:S(2)}) copy-start(bf16[48,8192]{1,0:T(8,128)(2,1)} %copy-done.22) | copy-start | bytes 2359300
  119.3 40.1 %copy-start.2 = (bf16[48,8192]{1,0:T(8,128)(2,1)S(1)}, bf16[48,8192]{1,0:T(8,128)(2,1)}, u32[]{:S(2)}) copy-start(bf16[48,8192]{1,0:T(8,128)(2,1)} %refs_0_.3) | copy-start | bytes 2359300
  119.3 58.2 %all-to-all-start = ((f16[32,136,128]{2,1,0:T(8,128)(2,1)}), f16[32,136,128]{2,1,0:T(8,128)(2,1)}, u32[]{:S(2)}, u32[]{:S(2)}) async-start(f16[32,136,128]{2,1,0:T(8,128)(2,1)} %convert_element_type.9), calls=%async_computation | async-start | bytes 2228224 | tf_op jit(solution)/shard_map/all_to_all | solution.py:184
  144.0 10.9 %collective-permute-start.21 = (bf16[16,8192]{1,0:T(8,128)(2,1)}, bf16[16,8192]{1,0:T(8,128)(2,1)S(1)}, u32[]{:S(2)}, u32[]{:S(2)}) collective-permute-start(bf16[16,8192]{1,0:T(8,128)(2,1)} %collective-permute-done.9.refs_8_.refs_14_), channel_id=1, source_target_pairs={{0,1},{1,0},{2,3},{3,2},{4,5},{5,4},{6,7},{7,6},{8,9},{9,8},{10,11... | collective-permute-start | bytes 786440 | tf_op jit(solution)/shard_map/ppermute | solution.py:36
  146.2 13.2 %collective-permute-start.19 = (bf16[48,8192]{1,0:T(8,128)(2,1)S(1)}, bf16[48,8192]{1,0:T(8,128)(2,1)}, u32[]{:S(2)}, u32[]{:S(2)}) collective-permute-start(bf16[48,8192]{1,0:T(8,128)(2,1)S(1)} %collective-permute-done.5.refs_4_.refs_10_), channel_id=1, source_target_pairs={{0,1},{1,0},{2,3},{3,2},{4,5},{5,4},{6,7},{7,6},{8,9},{9,8},{10,11... | collective-permute-start | bytes 2359304 | tf_op jit(solution)/shard_map/ppermute | solution.py:36
  148.3 11.1 %collective-permute-start.20 = (bf16[48,8192]{1,0:T(8,128)(2,1)S(1)}, bf16[48,8192]{1,0:T(8,128)(2,1)}, u32[]{:S(2)}, u32[]{:S(2)}) collective-permute-start(bf16[48,8192]{1,0:T(8,128)(2,1)S(1)} %collective-permute-done.7.refs_6_.refs_12_), channel_id=1, source_target_pairs={{0,1},{1,0},{2,3},{3,2},{4,5},{5,4},{6,7},{7,6},{8,9},{9,8},{10,11... | collective-permute-start | bytes 2359304 | tf_op jit(solution)/shard_map/ppermute | solution.py:36
  150.5 8.9 %collective-permute-start.17 = (bf16[48,8192]{1,0:T(8,128)(2,1)}, bf16[48,8192]{1,0:T(8,128)(2,1)}, u32[]{:S(2)}, u32[]{:S(2)}) collective-permute-start(bf16[48,8192]{1,0:T(8,128)(2,1)} %collective-permute-done.1.refs_0_.refs_6_), channel_id=1, source_target_pairs={{0,1},{1,0},{2,3},{3,2},{4,5},{5,4},{6,7},{7,6},{8,9},{9,8},{10,11... | collective-permute-start | bytes 2359304 | tf_op jit(solution)/shard_map/ppermute | solution.py:36
  152.7 6.7 %collective-permute-start.18 = (bf16[48,8192]{1,0:T(8,128)(2,1)}, bf16[48,8192]{1,0:T(8,128)(2,1)}, u32[]{:S(2)}, u32[]{:S(2)}) collective-permute-start(bf16[48,8192]{1,0:T(8,128)(2,1)} %copy-done.18), channel_id=1, source_target_pairs={{0,1},{1,0},{2,3},{3,2},{4,5},{5,4},{6,7},{7,6},{8,9},{9,8},{10,11... | collective-permute-start | bytes 2359304 | tf_op jit(solution)/shard_map/ppermute | solution.py:36
  155.6 3.8 %collective-permute-start.22 = (bf16[32,8192]{1,0:T(8,128)(2,1)S(1)}, bf16[32,8192]{1,0:T(8,128)(2,1)S(1)}, u32[]{:S(2)}, u32[]{:S(2)}) collective-permute-start(bf16[32,8192]{1,0:T(8,128)(2,1)S(1)} %collective-permute-done.11.refs_10_.refs_16_), channel_id=1, source_target_pairs={{0,1},{1,0},{2,3},{3,2},{4,5},{5,4},{6,7},{7,6},{8,9},{9,8},{10,11... | collective-permute-start | bytes 1572872 | tf_op jit(solution)/shard_map/ppermute | solution.py:36
  159.4 1.1 copy-start.5
  160.6 1.1 copy-start.8
  161.7 1.1 copy-start.11
  162.8 1.1 copy-start.14
  164.0 1.1 copy-start.17
  165.1 1.1 copy-start.20
  166.2 1.2 copy-start.21
  (8 other events, 7.1 us)

commit v4 on v3

--- a/solution.py
+++ b/solution.py
@@ -49,7 +49,7 @@
     return rows, cols
 
 
-def weight_kernel(count, first, coded, cells_ref, offs_ref, *refs):
+def weight_kernel(count, first, prior, coded, cells_ref, offs_ref, *refs):
     pieces, hidden_ref, out_ref = refs[:count], refs[count], refs[-1]
     spans = [
         pl.ds(pl.multiple_of(offs_ref[first + i], 16), piece.shape[0])
@@ -72,8 +72,9 @@
         )
         for k, s in enumerate(slots):
             block = blocks[k * BLK : (k + 1) * BLK, k * BLK : (k + 1) * BLK]
+            if prior:
+                block = block + refs[count + 1][s]
             if coded:
-                block = block + refs[count + 1][s]
                 top = jnp.max(jnp.abs(block), axis=0, keepdims=True)
                 power = jnp.ceil(jnp.log2(jnp.maximum(top, TINY)))
                 out_ref[s, :BLK, :] = block * jnp.exp2(SHIFT - power)
@@ -132,11 +133,10 @@
     )(*tables, *operands)
 
 
-def weight_grads(pieces, first, tables, hidden, slots, prior=None):
-    coded = prior is not None
-    kernel = functools.partial(weight_kernel, len(pieces), first, coded)
+def weight_grads(pieces, first, tables, hidden, slots, prior=None, coded=False):
+    kernel = functools.partial(weight_kernel, len(pieces), first, prior is not None, coded)
     out = jax.ShapeDtypeStruct((slots, BLK + EXTRA * coded, BLK), jnp.float32)
-    operands = (*pieces, hidden) + ((prior,) if coded else ())
+    operands = (*pieces, hidden) + (() if prior is None else (prior,))
     flops = 2 * slots * sum(p.shape[0] for p in pieces) * BLK * BLK
     return call(kernel, tables, operands, out, [], flops, GRANT)
 
@@ -180,19 +180,17 @@
     tables = (cells, (chip + (core ^ swapped)) * height + start)
 
     prior = weight_grads(pieces[:EARLY], 0, tables, hidden, slots)
-    coded = weight_grads(pieces[EARLY:], EARLY, tables, hidden, slots, prior)
-    parts = lax.all_to_all(
-        coded.astype(jnp.float16), "dp", split_axis=0, concat_axis=0, tiled=True
-    )
-    for i in range(EARLY, len(pieces), 2):
+    prior = weight_grads(pieces[EARLY:LATE], EARLY, tables, hidden, slots, prior)
+    coded = weight_grads(pieces[LATE:], LATE, tables, hidden, slots, prior, coded=True)
+    parts = lax.all_to_all(coded.astype(jnp.float16), "dp", split_axis=0, concat_axis=0, tiled=True)
+    for i in range(AGAIN, len(pieces), 2):
         shard, _ = lax.optimization_barrier((pieces[i], coded))
         pieces[i + 1] = send(shard, swap_core)
     input_grad = input_grads(pieces, (*tables, counts), weights, hidden)
 
     share = slots // lax.axis_size("dp")
-    values = parts[:, :BLK].astype(jnp.float32)
-    powers = parts[:, BLK : BLK + 1].astype(jnp.float32)
-    summed = (values * jnp.exp2(powers - SHIFT)).reshape(-1, share, BLK, BLK).sum(0)
+    parts = parts.astype(jnp.float32).reshape(-1, share, BLK + EXTRA, BLK)
+    summed = (parts[:, :, :BLK] * jnp.exp2(parts[:, :, BLK : BLK + 1] - SHIFT)).sum(0)
     mine = lax.axis_index("dp") * share + jnp.arange(share, dtype=jnp.int32)
     summed = jnp.where((mine < counts[0])[:, None, None], summed, 0.0)
     return summed[None], input_grad
@@ -203,6 +201,8 @@
     ("near", 2), ("far", 0), ("far", 1), ("far", X - 1), ("far", 2), ("far", -2),
 )
 EARLY = 6
+LATE = 14
+AGAIN = 10
 CUT = 16
 GRANT = 8 * 2**20
 

time: 182 us -> 182 us (level)
  the two profiles are of different devices: /device:TPU:1 before, /device:TPU:16 now
where the time goes in v4:
time: 182 us; the launch traced here: 181 us
  starting transfers between devices  87.4 us (48%)
  waiting for transfers between devices  40.3 us (22%)
  Pallas kernels  25.1 us (14%)
  local copies, waits for them, and re-layouts  21.3 us (12%)
  other arithmetic  4.79 us (3%)
    ppermute x21, starting transfers between devices, send(): lax.ppermute(value, 'tensor', [(i, target(i)) for i in range(MEMBERS)])  62.6 us
    ppermute x21, waiting for transfers between devices, send(): lax.ppermute(value, 'tensor', [(i, target(i)) for i in range(MEMBERS)])  38.1 us
    pallas_call x4, Pallas kernels, call(): pl.pallas_call(kernel, in_specs=[table for _ in tables] + [held for _ in...  25.1 us
    all_to_all x1, starting transfers between devices, body(): lax.all_to_all(coded.astype(jnp.float16), 'dp', split_axis=0, concat_axis...  24.8 us
    unnamed x50, local copies, waits for them, and re-layouts  20.5 us
  transfers between devices with their start and end apart: 22, of which 8 were waited for; matrix products, arithmetic and copies ran while one was open for 1% of the time, Pallas kernels for 11%

profile of v4, /device:TPU:16, one launch (start us, length us, event | category | flops | bytes accessed | tf_op | source)
XLA Modules:
  0.0 180.6 jit_solution(2980435349083500706)
XLA Ops:
  0.6 11.1 %collective-permute-start = (bf16[48,8192]{1,0:T(8,128)(2,1)}, bf16[48,8192]{1,0:T(8,128)(2,1)S(1)}, u32[]{:S(2)}, u32[]{:S(2)}) collective-permute-start(bf16[48,8192]{1,0:T(8,128)(2,1)} %refs_0_.3), channel_id=1, source_target_pairs={{0,8},{1,9},{2,10},{3,11},{4,12},{5,13},{6,14},{7,15},{8,0},{9,1},... | collective-permute-start | bytes 2359304 | tf_op jit(solution)/shard_map/ppermute | solution.py:36
  11.7 3.4 %collective-permute-start.7 = (bf16[48,8192]{1,0:T(8,128)(2,1)}, bf16[48,8192]{1,0:T(8,128)(2,1)S(1)}, u32[]{:S(2)}, u32[]{:S(2)}) collective-permute-start(bf16[48,8192]{1,0:T(8,128)(2,1)} %refs_0_.3), channel_id=1, source_target_pairs={{0,2},{1,3},{2,4},{3,5},{4,6},{5,7},{6,0},{7,1},{8,10},{9,11},{10,... | collective-permute-start | bytes 2359304 | tf_op jit(solution)/shard_map/ppermute | solution.py:36
  15.1 3.7 %collective-permute-start.15 = (bf16[48,8192]{1,0:T(8,128)(2,1)}, bf16[48,8192]{1,0:T(8,128)(2,1)S(1)}, u32[]{:S(2)}, u32[]{:S(2)}) collective-permute-start(bf16[48,8192]{1,0:T(8,128)(2,1)} %refs_0_.3), channel_id=1, source_target_pairs={{0,6},{1,7},{2,0},{3,1},{4,2},{5,3},{6,4},{7,5},{8,14},{9,15},{10,... | collective-permute-start | bytes 2359304 | tf_op jit(solution)/shard_map/ppermute | solution.py:36
  18.8 1.9 %collective-permute-start.13 = (bf16[48,8192]{1,0:T(8,128)(2,1)}, bf16[48,8192]{1,0:T(8,128)(2,1)S(1)}, u32[]{:S(2)}, u32[]{:S(2)}) collective-permute-start(bf16[48,8192]{1,0:T(8,128)(2,1)} %refs_0_.3), channel_id=1, source_target_pairs={{0,1},{1,0},{2,3},{3,2},{4,5},{5,4},{6,7},{7,6},{8,9},{9,8},{10,11... | collective-permute-start | bytes 2359304 | tf_op jit(solution)/shard_map/ppermute | solution.py:36
  20.7 8.9 %collective-permute-done.refs_2_.refs_8_ = bf16[48,8192]{1,0:T(8,128)(2,1)S(1)} collective-permute-done((bf16[48,8192]{1,0:T(8,128)(2,1)}, bf16[48,8192]{1,0:T(8,128)(2,1)S(1)}, u32[]{:S(2)}, u32[]{:S(2)}) %collective-permute-start) | collective-permute-done | bytes 786464 | tf_op jit(solution)/shard_map/ppermute | solution.py:36
  29.6 4.7 %collective-permute-start.4 = (bf16[48,8192]{1,0:T(8,128)(2,1)S(1)}, bf16[48,8192]{1,0:T(8,128)(2,1)S(1)}, u32[]{:S(2)}, u32[]{:S(2)}) collective-permute-start(bf16[48,8192]{1,0:T(8,128)(2,1)S(1)} %collective-permute-done.refs_2_.refs_8_), channel_id=1, source_target_pairs={{0,6},{1,7},{2,0},{3,1},{4,2},{5,3},{6,4},{7,5},{8,14},{9,15},{10,... | collective-permute-start | bytes 2359304 | tf_op jit(solution)/shard_map/ppermute | solution.py:36
  34.3 1.9 %collective-permute-start.14 = (bf16[48,8192]{1,0:T(8,128)(2,1)S(1)}, bf16[48,8192]{1,0:T(8,128)(2,1)S(1)}, u32[]{:S(2)}, u32[]{:S(2)}) collective-permute-start(bf16[48,8192]{1,0:T(8,128)(2,1)S(1)} %collective-permute-done.7.refs_2_), channel_id=1, source_target_pairs={{0,1},{1,0},{2,3},{3,2},{4,5},{5,4},{6,7},{7,6},{8,9},{9,8},{10,11... | collective-permute-start | bytes 2359304 | tf_op jit(solution)/shard_map/ppermute | solution.py:36
  36.2 1.4 collective-permute-done.15.refs_4_
  37.6 1.9 %collective-permute-start.16 = (bf16[48,8192]{1,0:T(8,128)(2,1)S(1)}, bf16[48,8192]{1,0:T(8,128)(2,1)S(1)}, u32[]{:S(2)}, u32[]{:S(2)}) collective-permute-start(bf16[48,8192]{1,0:T(8,128)(2,1)S(1)} %collective-permute-done.15.refs_4_), channel_id=1, source_target_pairs={{0,1},{1,0},{2,3},{3,2},{4,5},{5,4},{6,7},{7,6},{8,9},{9,8},{10,11... | collective-permute-start | bytes 2359304 | tf_op jit(solution)/shard_map/ppermute | solution.py:36
  40.5 3.4 %collective-permute-start.1 = (bf16[48,8192]{1,0:T(8,128)(2,1)S(1)}, bf16[48,8192]{1,0:T(8,128)(2,1)S(1)}, u32[]{:S(2)}, u32[]{:S(2)}) collective-permute-start(bf16[48,8192]{1,0:T(8,128)(2,1)S(1)} %collective-permute-done.refs_2_.refs_8_), channel_id=1, source_target_pairs={{0,2},{1,3},{2,4},{3,5},{4,6},{5,7},{6,0},{7,1},{8,10},{9,11},{10,... | collective-permute-start | bytes 2359304 | tf_op jit(solution)/shard_map/ppermute | solution.py:36
  44.7 3.1 %collective-permute-start.8 = (bf16[48,8192]{1,0:T(8,128)(2,1)S(1)}, bf16[48,8192]{1,0:T(8,128)(2,1)}, u32[]{:S(2)}, u32[]{:S(2)}) collective-permute-start(bf16[48,8192]{1,0:T(8,128)(2,1)S(1)} %collective-permute-done.7.refs_2_), channel_id=1, source_target_pairs={{0,2},{1,3},{2,4},{3,5},{4,6},{5,7},{6,0},{7,1},{8,10},{9,11},{10,... | collective-permute-start | bytes 2359304 | tf_op jit(solution)/shard_map/ppermute | solution.py:36
  47.9 4.9 %collective-permute-done.4.refs_6_.refs_12_ = bf16[48,8192]{1,0:T(8,128)(2,1)S(1)} collective-permute-done((bf16[48,8192]{1,0:T(8,128)(2,1)S(1)}, bf16[48,8192]{1,0:T(8,128)(2,1)S(1)}, u32[]{:S(2)}, u32[]{:S(2)}) %collective-permute-start.4) | collective-permute-done | bytes 786464 | tf_op jit(solution)/shard_map/ppermute | solution.py:36
  52.8 1.9 %collective-permute-start.10 = (bf16[48,8192]{1,0:T(8,128)(2,1)S(1)}, bf16[48,8192]{1,0:T(8,128)(2,1)S(1)}, u32[]{:S(2)}, u32[]{:S(2)}) collective-permute-start(bf16[48,8192]{1,0:T(8,128)(2,1)S(1)} %collective-permute-done.refs_2_.refs_8_), channel_id=1, source_target_pairs={{0,1},{1,0},{2,3},{3,2},{4,5},{5,4},{6,7},{7,6},{8,9},{9,8},{10,11... | collective-permute-start | bytes 2359304 | tf_op jit(solution)/shard_map/ppermute | solution.py:36
  55.6 4.9 %collective-permute-start.5 = (bf16[32,8192]{1,0:T(8,128)(2,1)S(1)}, bf16[32,8192]{1,0:T(8,128)(2,1)S(1)}, u32[]{:S(2)}, u32[]{:S(2)}) collective-permute-start(bf16[32,8192]{1,0:T(8,128)(2,1)S(1)} %slice.17), channel_id=1, source_target_pairs={{0,6},{1,7},{2,0},{3,1},{4,2},{5,3},{6,4},{7,5},{8,14},{9,15},{10,... | collective-permute-start | bytes 1572872 | tf_op jit(solution)/shard_map/ppermute | solution.py:36
  61.4 2.1 %collective-permute-start.12 = (bf16[48,8192]{1,0:T(8,128)(2,1)S(1)}, bf16[48,8192]{1,0:T(8,128)(2,1)}, u32[]{:S(2)}, u32[]{:S(2)}) collective-permute-start(bf16[48,8192]{1,0:T(8,128)(2,1)S(1)} %collective-permute-done.4.refs_6_.refs_12_), channel_id=1, source_target_pairs={{0,1},{1,0},{2,3},{3,2},{4,5},{5,4},{6,7},{7,6},{8,9},{9,8},{10,11... | collective-permute-start | bytes 2359304 | tf_op jit(solution)/shard_map/ppermute | solution.py:36
  64.0 1.9 %collective-permute-start.11 = (bf16[48,8192]{1,0:T(8,128)(2,1)S(1)}, bf16[48,8192]{1,0:T(8,128)(2,1)}, u32[]{:S(2)}, u32[]{:S(2)}) collective-permute-start(bf16[48,8192]{1,0:T(8,128)(2,1)S(1)} %collective-permute-done.1.refs_4_.refs_10_), channel_id=1, source_target_pairs={{0,1},{1,0},{2,3},{3,2},{4,5},{5,4},{6,7},{7,6},{8,9},{9,8},{10,11... | collective-permute-start | bytes 2359304 | tf_op jit(solution)/shard_map/ppermute | solution.py:36
  65.9 14.6 %collective-permute-done.8.refs_0_.refs_6_ = bf16[48,8192]{1,0:T(8,128)(2,1)} collective-permute-done((bf16[48,8192]{1,0:T(8,128)(2,1)S(1)}, bf16[48,8192]{1,0:T(8,128)(2,1)}, u32[]{:S(2)}, u32[]{:S(2)}) %collective-permute-start.8) | collective-permute-done | bytes 786464 | tf_op jit(solution)/shard_map/ppermute | solution.py:36
  80.5 1.9 %collective-permute-start.9 = (bf16[48,8192]{1,0:T(8,128)(2,1)}, bf16[48,8192]{1,0:T(8,128)(2,1)}, u32[]{:S(2)}, u32[]{:S(2)}) collective-permute-start(bf16[48,8192]{1,0:T(8,128)(2,1)} %collective-permute-done.8.refs_0_.refs_6_), channel_id=1, source_target_pairs={{0,1},{1,0},{2,3},{3,2},{4,5},{5,4},{6,7},{7,6},{8,9},{9,8},{10,11... | collective-permute-start | bytes 2359304 | tf_op jit(solution)/shard_map/ppermute | solution.py:36
  84.1 2.2 %collective-permute-start.2 = (bf16[16,8192]{1,0:T(8,128)(2,1)}, bf16[16,8192]{1,0:T(8,128)(2,1)}, u32[]{:S(2)}, u32[]{:S(2)}) collective-permute-start(bf16[16,8192]{1,0:T(8,128)(2,1)} %slice.16), channel_id=1, source_target_pairs={{0,2},{1,3},{2,4},{3,5},{4,6},{5,7},{6,0},{7,1},{8,10},{9,11},{10,... | collective-permute-start | bytes 786440 | tf_op jit(solution)/shard_map/ppermute | solution.py:36
  86.3 2.1 %collective-permute-start.6 = (bf16[32,8192]{1,0:T(8,128)(2,1)S(1)}, bf16[32,8192]{1,0:T(8,128)(2,1)}, u32[]{:S(2)}, u32[]{:S(2)}) collective-permute-start(bf16[32,8192]{1,0:T(8,128)(2,1)S(1)} %collective-permute-done.5.refs_2_.refs_16_), channel_id=1, source_target_pairs={{0,1},{1,0},{2,3},{3,2},{4,5},{5,4},{6,7},{7,6},{8,9},{9,8},{10,11... | collective-permute-start | bytes 1572872 | tf_op jit(solution)/shard_map/ppermute | solution.py:36
  89.2 7.0 %collective-permute-done.2.refs_0_.refs_14_ = bf16[16,8192]{1,0:T(8,128)(2,1)} collective-permute-done((bf16[16,8192]{1,0:T(8,128)(2,1)}, bf16[16,8192]{1,0:T(8,128)(2,1)}, u32[]{:S(2)}, u32[]{:S(2)}) %collective-permute-start.2) | collective-permute-done | bytes 262176 | tf_op jit(solution)/shard_map/ppermute | solution.py:36
  96.2 1.9 %collective-permute-start.3 = (bf16[16,8192]{1,0:T(8,128)(2,1)}, bf16[16,8192]{1,0:T(8,128)(2,1)S(1)}, u32[]{:S(2)}, u32[]{:S(2)}) collective-permute-start(bf16[16,8192]{1,0:T(8,128)(2,1)} %collective-permute-done.2.refs_0_.refs_14_), channel_id=1, source_target_pairs={{0,1},{1,0},{2,3},{3,2},{4,5},{5,4},{6,7},{7,6},{8,9},{9,8},{10,11... | collective-permute-start | bytes 786440 | tf_op jit(solution)/shard_map/ppermute | solution.py:36
  98.8 1.1 copy-done.1
  99.9 1.1 copy-done.7
  101.0 1.1 copy-done.10
  102.2 1.1 copy-done.13
  103.3 1.1 copy-done.16
  104.4 1.1 copy-done.19
  105.6 4.9 %shard_map.113.refs_9_ = f32[32,128,128]{2,1,0:T(8,128)S(1)} custom-call(s32[32]{0:T(128)S(1)} %add_bitcast_fusion.cells_ref, s32[18]{0:T(128)S(1)} %multiply_add_fusion.offs_ref, bf16[48,8192]{1,0:T(8,128)(2,1)S(1)} %copy-done.1, bf16[48,8192]{1,0:T(8,128)(2,1)S(1)} %copy-done.13, bf16[48,8192]{1,0:T(8,128)(2,1)S(1)} %copy-done.7, ...), custom_call_target="tpu_custom_call" | custom-call | flops 301989888 | bytes 8192000 | tf_op jit(solution)/shard_map/pallas_call | solution.py:125
  110.5 6.2 %shard_map.114.refs_5_ = f32[32,128,128]{2,1,0:T(8,128)S(1)} custom-call(s32[32]{0:T(128)S(1)} %add_bitcast_fusion.cells_ref, s32[18]{0:T(128)S(1)} %multiply_add_fusion.offs_ref, bf16[48,8192]{1,0:T(8,128)(2,1)} %collective-permute-done.8.refs_0_.refs_6_, bf16[48,8192]{1,0:T(8,128)(2,1)} %collective-permute-done.9.refs_1_.refs_7_, ...), custom_call_target="tpu_custom_call" | custom-call | flops 402653184 | bytes 11862016 | tf_op jit(solution)/shard_map/pallas_call | solution.py:125
  116.7 5.1 %shard_map.115 = f32[32,136,128]{2,1,0:T(8,128)S(1)} custom-call(s32[32]{0:T(128)S(1)} %add_bitcast_fusion.cells_ref, s32[18]{0:T(128)S(1)} %multiply_add_fusion.offs_ref, bf16[16,8192]{1,0:T(8,128)(2,1)} %collective-permute-done.2.refs_0_.refs_14_, bf16[16,8192]{1,0:T(8,128)(2,1)S(1)} %collective-permute-done.3.refs_1_, ...), custom_call_target="tpu_custom_call" | custom-call | flops 100663296 | bytes 7274496 | tf_op jit(solution)/shard_map/pallas_call | solution.py:125
  121.8 1.1 convert_element_type.4
  123.0 24.8 %all-to-all-start = ((f16[32,136,128]{2,1,0:T(8,128)(2,1)}), f16[32,136,128]{2,1,0:T(8,128)(2,1)}, u32[]{:S(2)}, u32[]{:S(2)}) async-start(f16[32,136,128]{2,1,0:T(8,128)(2,1)} %convert_element_type.4), calls=%async_computation | async-start | bytes 2228224 | tf_op jit(solution)/shard_map/all_to_all | solution.py:185
  147.8 1.9 %collective-permute-start.17 = (bf16[48,8192]{1,0:T(8,128)(2,1)S(1)}, bf16[48,8192]{1,0:T(8,128)(2,1)}, u32[]{:S(2)}, u32[]{:S(2)}) collective-permute-start(bf16[48,8192]{1,0:T(8,128)(2,1)S(1)} %collective-permute-done.1.refs_4_.refs_10_), channel_id=1, source_target_pairs={{0,1},{1,0},{2,3},{3,2},{4,5},{5,4},{6,7},{7,6},{8,9},{9,8},{10,11... | collective-permute-start | bytes 2359304 | tf_op jit(solution)/shard_map/ppermute | solution.py:36
  149.7 2.4 %collective-permute-start.18 = (bf16[48,8192]{1,0:T(8,128)(2,1)S(1)}, bf16[48,8192]{1,0:T(8,128)(2,1)}, u32[]{:S(2)}, u32[]{:S(2)}) collective-permute-start(bf16[48,8192]{1,0:T(8,128)(2,1)S(1)} %collective-permute-done.4.refs_6_.refs_12_), channel_id=1, source_target_pairs={{0,1},{1,0},{2,3},{3,2},{4,5},{5,4},{6,7},{7,6},{8,9},{9,8},{10,11... | collective-permute-start | bytes 2359304 | tf_op jit(solution)/shard_map/ppermute | solution.py:36
  152.2 1.9 %collective-permute-start.20 = (bf16[32,8192]{1,0:T(8,128)(2,1)S(1)}, bf16[32,8192]{1,0:T(8,128)(2,1)S(1)}, u32[]{:S(2)}, u32[]{:S(2)}) collective-permute-start(bf16[32,8192]{1,0:T(8,128)(2,1)S(1)} %collective-permute-done.5.refs_2_.refs_16_), channel_id=1, source_target_pairs={{0,1},{1,0},{2,3},{3,2},{4,5},{5,4},{6,7},{7,6},{8,9},{9,8},{10,11... | collective-permute-start | bytes 1572872 | tf_op jit(solution)/shard_map/ppermute | solution.py:36
  154.1 2.4 %collective-permute-start.19 = (bf16[16,8192]{1,0:T(8,128)(2,1)}, bf16[16,8192]{1,0:T(8,128)(2,1)}, u32[]{:S(2)}, u32[]{:S(2)}) collective-permute-start(bf16[16,8192]{1,0:T(8,128)(2,1)} %collective-permute-done.2.refs_0_.refs_14_), channel_id=1, source_target_pairs={{0,1},{1,0},{2,3},{3,2},{4,5},{5,4},{6,7},{7,6},{8,9},{9,8},{10,11... | collective-permute-start | bytes 786440 | tf_op jit(solution)/shard_map/ppermute | solution.py:36
  158.0 1.1 copy-done.5
  159.1 1.1 copy-done.8
  160.3 1.1 copy-done.11
  161.4 1.1 copy-done.14
  162.5 1.1 copy-done.17
  163.7 1.1 copy-done.20
  164.8 1.1 copy-done.23
  165.9 1.2 copy-done.24
  167.2 9.0 %shard_map.116 = bf16[768,896]{1,0:T(8,128)(2,1)} custom-call(s32[32]{0:T(128)S(1)} %add_bitcast_fusion.cells_ref, s32[18]{0:T(128)S(1)} %multiply_add_fusion.offs_ref, s32[1]{0:T(128)S(6)} %copy.12.counts_ref, bf16[48,8192]{1,0:T(8,128)(2,1)S(1)} %copy-done.2, bf16[48,8192]{1,0:T(8,128)(2,1)S(1)} %copy-done.14, bf16[48,8192]{1,0:T(8,128)(2,1)S(1)} %copy-done.8, ...), custom_call_target="tpu_custom_call" | custom-call | flops 805306368 | bytes 15007744 | tf_op jit(solution)/shard_map/pallas_call | solution.py:125
  176.2 2.2 %all-to-all-done = f16[32,136,128]{2,1,0:T(8,128)(2,1)} async-done(((f16[32,136,128]{2,1,0:T(8,128)(2,1)}), f16[32,136,128]{2,1,0:T(8,128)(2,1)}, u32[]{:S(2)}, u32[]{:S(2)}) %all-to-all-start) | async-done | bytes 1114144 | tf_op jit(solution)/shard_map/all_to_all | solution.py:185
  178.4 1.4 bitcast_convert_fusion
  (59 shorter events, 8.9 us)
Async XLA Ops:
  0.6 98.1 %copy-start = (bf16[768,896]{1,0:T(8,128)(2,1)S(1)}, bf16[768,896]{1,0:T(8,128)(2,1)}, u32[]{:S(2)}) copy-start(bf16[768,896]{1,0:T(8,128)(2,1)} %refs_4_.1) | copy-start | bytes 4128772
  0.6 29.0 %collective-permute-start = (bf16[48,8192]{1,0:T(8,128)(2,1)}, bf16[48,8192]{1,0:T(8,128)(2,1)S(1)}, u32[]{:S(2)}, u32[]{:S(2)}) collective-permute-start(bf16[48,8192]{1,0:T(8,128)(2,1)} %refs_0_.3), channel_id=1, source_target_pairs={{0,8},{1,9},{2,10},{3,11},{4,12},{5,13},{6,14},{7,15},{8,0},{9,1},... | collective-permute-start | bytes 2359304 | tf_op jit(solution)/shard_map/ppermute | solution.py:36
  11.7 22.6 %collective-permute-start.7 = (bf16[48,8192]{1,0:T(8,128)(2,1)}, bf16[48,8192]{1,0:T(8,128)(2,1)S(1)}, u32[]{:S(2)}, u32[]{:S(2)}) collective-permute-start(bf16[48,8192]{1,0:T(8,128)(2,1)} %refs_0_.3), channel_id=1, source_target_pairs={{0,2},{1,3},{2,4},{3,5},{4,6},{5,7},{6,0},{7,1},{8,10},{9,11},{10,... | collective-permute-start | bytes 2359304 | tf_op jit(solution)/shard_map/ppermute | solution.py:36
  15.1 22.5 %collective-permute-start.15 = (bf16[48,8192]{1,0:T(8,128)(2,1)}, bf16[48,8192]{1,0:T(8,128)(2,1)S(1)}, u32[]{:S(2)}, u32[]{:S(2)}) collective-permute-start(bf16[48,8192]{1,0:T(8,128)(2,1)} %refs_0_.3), channel_id=1, source_target_pairs={{0,6},{1,7},{2,0},{3,1},{4,2},{5,3},{6,4},{7,5},{8,14},{9,15},{10,... | collective-permute-start | bytes 2359304 | tf_op jit(solution)/shard_map/ppermute | solution.py:36
  18.8 25.1 %collective-permute-start.13 = (bf16[48,8192]{1,0:T(8,128)(2,1)}, bf16[48,8192]{1,0:T(8,128)(2,1)S(1)}, u32[]{:S(2)}, u32[]{:S(2)}) collective-permute-start(bf16[48,8192]{1,0:T(8,128)(2,1)} %refs_0_.3), channel_id=1, source_target_pairs={{0,1},{1,0},{2,3},{3,2},{4,5},{5,4},{6,7},{7,6},{8,9},{9,8},{10,11... | collective-permute-start | bytes 2359304 | tf_op jit(solution)/shard_map/ppermute | solution.py:36
  29.6 34.4 %copy-start.3 = (bf16[48,8192]{1,0:T(8,128)(2,1)}, bf16[48,8192]{1,0:T(8,128)(2,1)S(1)}, u32[]{:S(2)}) copy-start(bf16[48,8192]{1,0:T(8,128)(2,1)S(1)} %collective-permute-done.refs_2_.refs_8_) | copy-start | bytes 2359300
  29.6 23.2 %collective-permute-start.4 = (bf16[48,8192]{1,0:T(8,128)(2,1)S(1)}, bf16[48,8192]{1,0:T(8,128)(2,1)S(1)}, u32[]{:S(2)}, u32[]{:S(2)}) collective-permute-start(bf16[48,8192]{1,0:T(8,128)(2,1)S(1)} %collective-permute-done.refs_2_.refs_8_), channel_id=1, source_target_pairs={{0,6},{1,7},{2,0},{3,1},{4,2},{5,3},{6,4},{7,5},{8,14},{9,15},{10,... | collective-permute-start | bytes 2359304 | tf_op jit(solution)/shard_map/ppermute | solution.py:36
  34.3 48.8 %copy-start.6 = (bf16[48,8192]{1,0:T(8,128)(2,1)}, bf16[48,8192]{1,0:T(8,128)(2,1)S(1)}, u32[]{:S(2)}) copy-start(bf16[48,8192]{1,0:T(8,128)(2,1)S(1)} %collective-permute-done.7.refs_2_) | copy-start | bytes 2359300
  34.3 20.4 %collective-permute-start.14 = (bf16[48,8192]{1,0:T(8,128)(2,1)S(1)}, bf16[48,8192]{1,0:T(8,128)(2,1)S(1)}, u32[]{:S(2)}, u32[]{:S(2)}) collective-permute-start(bf16[48,8192]{1,0:T(8,128)(2,1)S(1)} %collective-permute-done.7.refs_2_), channel_id=1, source_target_pairs={{0,1},{1,0},{2,3},{3,2},{4,5},{5,4},{6,7},{7,6},{8,9},{9,8},{10,11... | collective-permute-start | bytes 2359304 | tf_op jit(solution)/shard_map/ppermute | solution.py:36
  37.6 22.9 %collective-permute-start.16 = (bf16[48,8192]{1,0:T(8,128)(2,1)S(1)}, bf16[48,8192]{1,0:T(8,128)(2,1)S(1)}, u32[]{:S(2)}, u32[]{:S(2)}) collective-permute-start(bf16[48,8192]{1,0:T(8,128)(2,1)S(1)} %collective-permute-done.15.refs_4_), channel_id=1, source_target_pairs={{0,1},{1,0},{2,3},{3,2},{4,5},{5,4},{6,7},{7,6},{8,9},{9,8},{10,11... | collective-permute-start | bytes 2359304 | tf_op jit(solution)/shard_map/ppermute | solution.py:36
  39.5 0.9 copy-start.9
  40.5 23.5 %collective-permute-start.1 = (bf16[48,8192]{1,0:T(8,128)(2,1)S(1)}, bf16[48,8192]{1,0:T(8,128)(2,1)S(1)}, u32[]{:S(2)}, u32[]{:S(2)}) collective-permute-start(bf16[48,8192]{1,0:T(8,128)(2,1)S(1)} %collective-permute-done.refs_2_.refs_8_), channel_id=1, source_target_pairs={{0,2},{1,3},{2,4},{3,5},{4,6},{5,7},{6,0},{7,1},{8,10},{9,11},{10,... | collective-permute-start | bytes 2359304 | tf_op jit(solution)/shard_map/ppermute | solution.py:36
  43.9 0.9 copy-start.12
  44.7 35.7 %collective-permute-start.8 = (bf16[48,8192]{1,0:T(8,128)(2,1)S(1)}, bf16[48,8192]{1,0:T(8,128)(2,1)}, u32[]{:S(2)}, u32[]{:S(2)}) collective-permute-start(bf16[48,8192]{1,0:T(8,128)(2,1)S(1)} %collective-permute-done.7.refs_2_), channel_id=1, source_target_pairs={{0,2},{1,3},{2,4},{3,5},{4,6},{5,7},{6,0},{7,1},{8,10},{9,11},{10,... | collective-permute-start | bytes 2359304 | tf_op jit(solution)/shard_map/ppermute | solution.py:36
  52.8 30.3 %collective-permute-start.10 = (bf16[48,8192]{1,0:T(8,128)(2,1)S(1)}, bf16[48,8192]{1,0:T(8,128)(2,1)S(1)}, u32[]{:S(2)}, u32[]{:S(2)}) collective-permute-start(bf16[48,8192]{1,0:T(8,128)(2,1)S(1)} %collective-permute-done.refs_2_.refs_8_), channel_id=1, source_target_pairs={{0,1},{1,0},{2,3},{3,2},{4,5},{5,4},{6,7},{7,6},{8,9},{9,8},{10,11... | collective-permute-start | bytes 2359304 | tf_op jit(solution)/shard_map/ppermute | solution.py:36
  54.8 0.9 copy-start.15
  55.6 30.6 %collective-permute-start.5 = (bf16[32,8192]{1,0:T(8,128)(2,1)S(1)}, bf16[32,8192]{1,0:T(8,128)(2,1)S(1)}, u32[]{:S(2)}, u32[]{:S(2)}) collective-permute-start(bf16[32,8192]{1,0:T(8,128)(2,1)S(1)} %slice.17), channel_id=1, source_target_pairs={{0,6},{1,7},{2,0},{3,1},{4,2},{5,3},{6,4},{7,5},{8,14},{9,15},{10,... | collective-permute-start | bytes 1572872 | tf_op jit(solution)/shard_map/ppermute | solution.py:36
  60.5 0.9 copy-start.18
  61.4 49.0 %collective-permute-start.12 = (bf16[48,8192]{1,0:T(8,128)(2,1)S(1)}, bf16[48,8192]{1,0:T(8,128)(2,1)}, u32[]{:S(2)}, u32[]{:S(2)}) collective-permute-start(bf16[48,8192]{1,0:T(8,128)(2,1)S(1)} %collective-permute-done.4.refs_6_.refs_12_), channel_id=1, source_target_pairs={{0,1},{1,0},{2,3},{3,2},{4,5},{5,4},{6,7},{7,6},{8,9},{9,8},{10,11... | collective-permute-start | bytes 2359304 | tf_op jit(solution)/shard_map/ppermute | solution.py:36
  64.0 46.5 %collective-permute-start.11 = (bf16[48,8192]{1,0:T(8,128)(2,1)S(1)}, bf16[48,8192]{1,0:T(8,128)(2,1)}, u32[]{:S(2)}, u32[]{:S(2)}) collective-permute-start(bf16[48,8192]{1,0:T(8,128)(2,1)S(1)} %collective-permute-done.1.refs_4_.refs_10_), channel_id=1, source_target_pairs={{0,1},{1,0},{2,3},{3,2},{4,5},{5,4},{6,7},{7,6},{8,9},{9,8},{10,11... | collective-permute-start | bytes 2359304 | tf_op jit(solution)/shard_map/ppermute | solution.py:36
  80.5 30.0 %collective-permute-start.9 = (bf16[48,8192]{1,0:T(8,128)(2,1)}, bf16[48,8192]{1,0:T(8,128)(2,1)}, u32[]{:S(2)}, u32[]{:S(2)}) collective-permute-start(bf16[48,8192]{1,0:T(8,128)(2,1)} %collective-permute-done.8.refs_0_.refs_6_), channel_id=1, source_target_pairs={{0,1},{1,0},{2,3},{3,2},{4,5},{5,4},{6,7},{7,6},{8,9},{9,8},{10,11... | collective-permute-start | bytes 2359304 | tf_op jit(solution)/shard_map/ppermute | solution.py:36
  83.1 0.9 copy-start.21
  84.1 12.1 %collective-permute-start.2 = (bf16[16,8192]{1,0:T(8,128)(2,1)}, bf16[16,8192]{1,0:T(8,128)(2,1)}, u32[]{:S(2)}, u32[]{:S(2)}) collective-permute-start(bf16[16,8192]{1,0:T(8,128)(2,1)} %slice.16), channel_id=1, source_target_pairs={{0,2},{1,3},{2,4},{3,5},{4,6},{5,7},{6,0},{7,1},{8,10},{9,11},{10,... | collective-permute-start | bytes 786440 | tf_op jit(solution)/shard_map/ppermute | solution.py:36
  86.3 30.4 %collective-permute-start.6 = (bf16[32,8192]{1,0:T(8,128)(2,1)S(1)}, bf16[32,8192]{1,0:T(8,128)(2,1)}, u32[]{:S(2)}, u32[]{:S(2)}) collective-permute-start(bf16[32,8192]{1,0:T(8,128)(2,1)S(1)} %collective-permute-done.5.refs_2_.refs_16_), channel_id=1, source_target_pairs={{0,1},{1,0},{2,3},{3,2},{4,5},{5,4},{6,7},{7,6},{8,9},{9,8},{10,11... | collective-permute-start | bytes 1572872 | tf_op jit(solution)/shard_map/ppermute | solution.py:36
  96.2 20.5 %collective-permute-start.3 = (bf16[16,8192]{1,0:T(8,128)(2,1)}, bf16[16,8192]{1,0:T(8,128)(2,1)S(1)}, u32[]{:S(2)}, u32[]{:S(2)}) collective-permute-start(bf16[16,8192]{1,0:T(8,128)(2,1)} %collective-permute-done.2.refs_0_.refs_14_), channel_id=1, source_target_pairs={{0,1},{1,0},{2,3},{3,2},{4,5},{5,4},{6,7},{7,6},{8,9},{9,8},{10,11... | collective-permute-start | bytes 786440 | tf_op jit(solution)/shard_map/ppermute | solution.py:36
  98.8 1.1 copy-start.1
  99.9 1.1 copy-start.7
  101.0 1.1 copy-start.10
  102.2 1.1 copy-start.13
  103.3 1.1 copy-start.16
  104.4 1.1 copy-start.19
  105.6 4.9 %copy-start.4 = (bf16[48,8192]{1,0:T(8,128)(2,1)S(1)}, bf16[48,8192]{1,0:T(8,128)(2,1)}, u32[]{:S(2)}) copy-start(bf16[48,8192]{1,0:T(8,128)(2,1)} %copy-done.3) | copy-start | bytes 2359300
  105.6 4.9 %copy-start.22 = (bf16[48,8192]{1,0:T(8,128)(2,1)S(1)}, bf16[48,8192]{1,0:T(8,128)(2,1)}, u32[]{:S(2)}) copy-start(bf16[48,8192]{1,0:T(8,128)(2,1)} %copy-done.21) | copy-start | bytes 2359300
  121.8 36.2 %copy-start.2 = (bf16[48,8192]{1,0:T(8,128)(2,1)S(1)}, bf16[48,8192]{1,0:T(8,128)(2,1)}, u32[]{:S(2)}) copy-start(bf16[48,8192]{1,0:T(8,128)(2,1)} %refs_0_.3) | copy-start | bytes 2359300
  123.0 55.4 %all-to-all-start = ((f16[32,136,128]{2,1,0:T(8,128)(2,1)}), f16[32,136,128]{2,1,0:T(8,128)(2,1)}, u32[]{:S(2)}, u32[]{:S(2)}) async-start(f16[32,136,128]{2,1,0:T(8,128)(2,1)} %convert_element_type.4), calls=%async_computation | async-start | bytes 2228224 | tf_op jit(solution)/shard_map/all_to_all | solution.py:185
  147.8 10.2 %collective-permute-start.17 = (bf16[48,8192]{1,0:T(8,128)(2,1)S(1)}, bf16[48,8192]{1,0:T(8,128)(2,1)}, u32[]{:S(2)}, u32[]{:S(2)}) collective-permute-start(bf16[48,8192]{1,0:T(8,128)(2,1)S(1)} %collective-permute-done.1.refs_4_.refs_10_), channel_id=1, source_target_pairs={{0,1},{1,0},{2,3},{3,2},{4,5},{5,4},{6,7},{7,6},{8,9},{9,8},{10,11... | collective-permute-start | bytes 2359304 | tf_op jit(solution)/shard_map/ppermute | solution.py:36
  149.7 8.3 %collective-permute-start.18 = (bf16[48,8192]{1,0:T(8,128)(2,1)S(1)}, bf16[48,8192]{1,0:T(8,128)(2,1)}, u32[]{:S(2)}, u32[]{:S(2)}) collective-permute-start(bf16[48,8192]{1,0:T(8,128)(2,1)S(1)} %collective-permute-done.4.refs_6_.refs_12_), channel_id=1, source_target_pairs={{0,1},{1,0},{2,3},{3,2},{4,5},{5,4},{6,7},{7,6},{8,9},{9,8},{10,11... | collective-permute-start | bytes 2359304 | tf_op jit(solution)/shard_map/ppermute | solution.py:36
  152.2 5.8 %collective-permute-start.20 = (bf16[32,8192]{1,0:T(8,128)(2,1)S(1)}, bf16[32,8192]{1,0:T(8,128)(2,1)S(1)}, u32[]{:S(2)}, u32[]{:S(2)}) collective-permute-start(bf16[32,8192]{1,0:T(8,128)(2,1)S(1)} %collective-permute-done.5.refs_2_.refs_16_), channel_id=1, source_target_pairs={{0,1},{1,0},{2,3},{3,2},{4,5},{5,4},{6,7},{7,6},{8,9},{9,8},{10,11... | collective-permute-start | bytes 1572872 | tf_op jit(solution)/shard_map/ppermute | solution.py:36
  154.1 3.9 %collective-permute-start.19 = (bf16[16,8192]{1,0:T(8,128)(2,1)}, bf16[16,8192]{1,0:T(8,128)(2,1)}, u32[]{:S(2)}, u32[]{:S(2)}) collective-permute-start(bf16[16,8192]{1,0:T(8,128)(2,1)} %collective-permute-done.2.refs_0_.refs_14_), channel_id=1, source_target_pairs={{0,1},{1,0},{2,3},{3,2},{4,5},{5,4},{6,7},{7,6},{8,9},{9,8},{10,11... | collective-permute-start | bytes 786440 | tf_op jit(solution)/shard_map/ppermute | solution.py:36
  158.0 1.1 copy-start.5
  159.1 1.1 copy-start.8
  160.3 1.1 copy-start.11
  161.4 1.1 copy-start.14
  162.5 1.1 copy-start.17
  163.7 1.1 copy-start.20
  164.8 1.1 copy-start.23
  165.9 1.2 copy-start.24

commit v5 on v3

--- a/solution.py
+++ b/solution.py
@@ -190,19 +190,18 @@
     input_grad = input_grads(pieces, (*tables, counts), weights, hidden)
 
     share = slots // lax.axis_size("dp")
-    values = parts[:, :BLK].astype(jnp.float32)
-    powers = parts[:, BLK : BLK + 1].astype(jnp.float32)
-    summed = (values * jnp.exp2(powers - SHIFT)).reshape(-1, share, BLK, BLK).sum(0)
+    parts = parts.astype(jnp.float32).reshape(-1, share, BLK + EXTRA, BLK)
+    summed = (parts[:, :, :BLK] * jnp.exp2(parts[:, :, BLK : BLK + 1] - SHIFT)).sum(0)
     mine = lax.axis_index("dp") * share + jnp.arange(share, dtype=jnp.int32)
     summed = jnp.where((mine < counts[0])[:, None, None], summed, 0.0)
     return summed[None], input_grad
 
 
 ORDER = (
-    ("near", 0), ("near", 1), ("near", X - 1),
-    ("near", 2), ("far", 0), ("far", 1), ("far", X - 1), ("far", 2), ("far", -2),
+    ("near", 0), ("near", 1), ("near", X - 1), ("far", 0),
+    ("near", 2), ("far", 1), ("far", X - 1), ("far", 2), ("far", -2),
 )
-EARLY = 6
+EARLY = 8
 CUT = 16
 GRANT = 8 * 2**20
 

time: 182 us -> 181 us (level)
  starting transfers between devices: 99.5 us -> 95.6 us
  local copies, waits for them, and re-layouts: 21.9 us -> 24.3 us
    ppermute x23 -> x22, starting transfers between devices: 74.9 us -> 69.7 us  [send(): lax.ppermute(value, 'tensor', [(i, target(i)) for i in range(MEMBERS)])]
    unnamed x64 -> x50, local copies, waits for them, and re-layouts: 21.9 us -> 23.6 us
    ppermute x23 -> x22, waiting for transfers between devices: 31.5 us -> 31.6 us  [send(): lax.ppermute(value, 'tensor', [(i, target(i)) for i in range(MEMBERS)])]
  transfers between devices with their start and end apart: 24 -> 23, of which waited for: 5 -> 5; matrix products, arithmetic and copies ran while one was open for 0% -> 1% of each run, Pallas kernels for 8% -> 8%
where the time goes in v5:
time: 181 us; the launch traced here: 179 us
  starting transfers between devices  95.6 us (53%)
  waiting for transfers between devices  31.6 us (17%)
  local copies, waits for them, and re-layouts  24.3 us (13%)
  Pallas kernels  20.9 us (12%)
  other arithmetic  4.78 us (3%)
    ppermute x22, starting transfers between devices, send(): lax.ppermute(value, 'tensor', [(i, target(i)) for i in range(MEMBERS)])  69.7 us
    ppermute x22, waiting for transfers between devices, send(): lax.ppermute(value, 'tensor', [(i, target(i)) for i in range(MEMBERS)])  31.6 us
    all_to_all x1, starting transfers between devices, body(): lax.all_to_all(coded.astype(jnp.float16), 'dp', split_axis=0, concat_axis...  25.9 us
    unnamed x50, local copies, waits for them, and re-layouts  23.6 us
    pallas_call x3, Pallas kernels, call(): pl.pallas_call(kernel, in_specs=[table for _ in tables] + [held for _ in...  20.9 us
  transfers between devices with their start and end apart: 23, of which 5 were waited for; matrix products, arithmetic and copies ran while one was open for 1% of the time, Pallas kernels for 8%

profile of v5, /device:TPU:1, one launch (start us, length us, event | category | flops | bytes accessed | tf_op | source)
XLA Modules:
  0.0 179.0 jit_solution(3730605068718159553)
XLA Ops:
  0.6 11.6 %collective-permute-start.3 = (bf16[48,8192]{1,0:T(8,128)(2,1)}, bf16[48,8192]{1,0:T(8,128)(2,1)S(1)}, u32[]{:S(2)}, u32[]{:S(2)}) collective-permute-start(bf16[48,8192]{1,0:T(8,128)(2,1)} %refs_0_.3), channel_id=1, source_target_pairs={{0,8},{1,9},{2,10},{3,11},{4,12},{5,13},{6,14},{7,15},{8,0},{9,1},... | collective-permute-start | bytes 2359304 | tf_op jit(solution)/shard_map/ppermute | solution.py:36
  12.2 3.1 %collective-permute-start = (bf16[48,8192]{1,0:T(8,128)(2,1)}, bf16[48,8192]{1,0:T(8,128)(2,1)S(1)}, u32[]{:S(2)}, u32[]{:S(2)}) collective-permute-start(bf16[48,8192]{1,0:T(8,128)(2,1)} %refs_0_.3), channel_id=1, source_target_pairs={{0,2},{1,3},{2,4},{3,5},{4,6},{5,7},{6,0},{7,1},{8,10},{9,11},{10,... | collective-permute-start | bytes 2359304 | tf_op jit(solution)/shard_map/ppermute | solution.py:36
  15.4 3.4 %collective-permute-start.14 = (bf16[48,8192]{1,0:T(8,128)(2,1)}, bf16[48,8192]{1,0:T(8,128)(2,1)S(1)}, u32[]{:S(2)}, u32[]{:S(2)}) collective-permute-start(bf16[48,8192]{1,0:T(8,128)(2,1)} %refs_0_.3), channel_id=1, source_target_pairs={{0,6},{1,7},{2,0},{3,1},{4,2},{5,3},{6,4},{7,5},{8,14},{9,15},{10,... | collective-permute-start | bytes 2359304 | tf_op jit(solution)/shard_map/ppermute | solution.py:36
  18.7 3.4 %collective-permute-start.12 = (bf16[48,8192]{1,0:T(8,128)(2,1)}, bf16[48,8192]{1,0:T(8,128)(2,1)S(1)}, u32[]{:S(2)}, u32[]{:S(2)}) collective-permute-start(bf16[48,8192]{1,0:T(8,128)(2,1)} %refs_0_.3), channel_id=1, source_target_pairs={{0,1},{1,0},{2,3},{3,2},{4,5},{5,4},{6,7},{7,6},{8,9},{9,8},{10,11... | collective-permute-start | bytes 2359304 | tf_op jit(solution)/shard_map/ppermute | solution.py:36
  22.2 6.8 %collective-permute-done.3.refs_6_ = bf16[48,8192]{1,0:T(8,128)(2,1)S(1)} collective-permute-done((bf16[48,8192]{1,0:T(8,128)(2,1)}, bf16[48,8192]{1,0:T(8,128)(2,1)S(1)}, u32[]{:S(2)}, u32[]{:S(2)}) %collective-permute-start.3) | collective-permute-done | bytes 786464 | tf_op jit(solution)/shard_map/ppermute | solution.py:36
  29.0 5.2 %collective-permute-start.6 = (bf16[48,8192]{1,0:T(8,128)(2,1)S(1)}, bf16[48,8192]{1,0:T(8,128)(2,1)S(1)}, u32[]{:S(2)}, u32[]{:S(2)}) collective-permute-start(bf16[48,8192]{1,0:T(8,128)(2,1)S(1)} %collective-permute-done.3.refs_6_), channel_id=1, source_target_pairs={{0,6},{1,7},{2,0},{3,1},{4,2},{5,3},{6,4},{7,5},{8,14},{9,15},{10,... | collective-permute-start | bytes 2359304 | tf_op jit(solution)/shard_map/ppermute | solution.py:36
  34.2 3.5 %collective-permute-start.16 = (bf16[48,8192]{1,0:T(8,128)(2,1)S(1)}, bf16[48,8192]{1,0:T(8,128)(2,1)S(1)}, u32[]{:S(2)}, u32[]{:S(2)}) collective-permute-start(bf16[48,8192]{1,0:T(8,128)(2,1)S(1)} %collective-permute-done.3.refs_6_), channel_id=1, source_target_pairs={{0,1},{1,0},{2,3},{3,2},{4,5},{5,4},{6,7},{7,6},{8,9},{9,8},{10,11... | collective-permute-start | bytes 2359304 | tf_op jit(solution)/shard_map/ppermute | solution.py:36
  37.7 1.9 %collective-permute-start.13 = (bf16[48,8192]{1,0:T(8,128)(2,1)S(1)}, bf16[48,8192]{1,0:T(8,128)(2,1)S(1)}, u32[]{:S(2)}, u32[]{:S(2)}) collective-permute-start(bf16[48,8192]{1,0:T(8,128)(2,1)S(1)} %collective-permute-done.refs_2_), channel_id=1, source_target_pairs={{0,1},{1,0},{2,3},{3,2},{4,5},{5,4},{6,7},{7,6},{8,9},{9,8},{10,11... | collective-permute-start | bytes 2359304 | tf_op jit(solution)/shard_map/ppermute | solution.py:36
  39.6 1.9 %collective-permute-start.4 = (bf16[48,8192]{1,0:T(8,128)(2,1)S(1)}, bf16[48,8192]{1,0:T(8,128)(2,1)S(1)}, u32[]{:S(2)}, u32[]{:S(2)}) collective-permute-start(bf16[48,8192]{1,0:T(8,128)(2,1)S(1)} %collective-permute-done.3.refs_6_), channel_id=1, source_target_pairs={{0,2},{1,3},{2,4},{3,5},{4,6},{5,7},{6,0},{7,1},{8,10},{9,11},{10,... | collective-permute-start | bytes 2359304 | tf_op jit(solution)/shard_map/ppermute | solution.py:36
  42.5 2.1 %collective-permute-start.1 = (bf16[48,8192]{1,0:T(8,128)(2,1)S(1)}, bf16[48,8192]{1,0:T(8,128)(2,1)}, u32[]{:S(2)}, u32[]{:S(2)}) collective-permute-start(bf16[48,8192]{1,0:T(8,128)(2,1)S(1)} %collective-permute-done.refs_2_), channel_id=1, source_target_pairs={{0,2},{1,3},{2,4},{3,5},{4,6},{5,7},{6,0},{7,1},{8,10},{9,11},{10,... | collective-permute-start | bytes 2359304 | tf_op jit(solution)/shard_map/ppermute | solution.py:36
  45.4 6.7 %collective-permute-done.6.refs_4_.refs_12_ = bf16[48,8192]{1,0:T(8,128)(2,1)S(1)} collective-permute-done((bf16[48,8192]{1,0:T(8,128)(2,1)S(1)}, bf16[48,8192]{1,0:T(8,128)(2,1)S(1)}, u32[]{:S(2)}, u32[]{:S(2)}) %collective-permute-start.6) | collective-permute-done | bytes 786464 | tf_op jit(solution)/shard_map/ppermute | solution.py:36
  52.2 4.0 %collective-permute-start.15 = (bf16[48,8192]{1,0:T(8,128)(2,1)S(1)}, bf16[48,8192]{1,0:T(8,128)(2,1)S(1)}, u32[]{:S(2)}, u32[]{:S(2)}) collective-permute-start(bf16[48,8192]{1,0:T(8,128)(2,1)S(1)} %collective-permute-done.14.refs_4_), channel_id=1, source_target_pairs={{0,1},{1,0},{2,3},{3,2},{4,5},{5,4},{6,7},{7,6},{8,9},{9,8},{10,11... | collective-permute-start | bytes 2359304 | tf_op jit(solution)/shard_map/ppermute | solution.py:36
  58.0 4.6 %collective-permute-start.10 = (bf16[32,8192]{1,0:T(8,128)(2,1)S(1)}, bf16[32,8192]{1,0:T(8,128)(2,1)S(1)}, u32[]{:S(2)}, u32[]{:S(2)}) collective-permute-start(bf16[32,8192]{1,0:T(8,128)(2,1)S(1)} %slice.17), channel_id=1, source_target_pairs={{0,6},{1,7},{2,0},{3,1},{4,2},{5,3},{6,4},{7,5},{8,14},{9,15},{10,... | collective-permute-start | bytes 1572872 | tf_op jit(solution)/shard_map/ppermute | solution.py:36
  63.5 2.2 %collective-permute-start.7 = (bf16[48,8192]{1,0:T(8,128)(2,1)S(1)}, bf16[48,8192]{1,0:T(8,128)(2,1)}, u32[]{:S(2)}, u32[]{:S(2)}) collective-permute-start(bf16[48,8192]{1,0:T(8,128)(2,1)S(1)} %collective-permute-done.6.refs_4_.refs_12_), channel_id=1, source_target_pairs={{0,1},{1,0},{2,3},{3,2},{4,5},{5,4},{6,7},{7,6},{8,9},{9,8},{10,11... | collective-permute-start | bytes 2359304 | tf_op jit(solution)/shard_map/ppermute | solution.py:36
  65.7 2.1 %collective-permute-start.5 = (bf16[48,8192]{1,0:T(8,128)(2,1)S(1)}, bf16[48,8192]{1,0:T(8,128)(2,1)}, u32[]{:S(2)}, u32[]{:S(2)}) collective-permute-start(bf16[48,8192]{1,0:T(8,128)(2,1)S(1)} %collective-permute-done.4.refs_2_.refs_10_), channel_id=1, source_target_pairs={{0,1},{1,0},{2,3},{3,2},{4,5},{5,4},{6,7},{7,6},{8,9},{9,8},{10,11... | collective-permute-start | bytes 2359304 | tf_op jit(solution)/shard_map/ppermute | solution.py:36
  67.9 10.4 %collective-permute-done.1.refs_0_.refs_8_ = bf16[48,8192]{1,0:T(8,128)(2,1)} collective-permute-done((bf16[48,8192]{1,0:T(8,128)(2,1)S(1)}, bf16[48,8192]{1,0:T(8,128)(2,1)}, u32[]{:S(2)}, u32[]{:S(2)}) %collective-permute-start.1) | collective-permute-done | bytes 786464 | tf_op jit(solution)/shard_map/ppermute | solution.py:36
  78.3 3.3 %collective-permute-start.2 = (bf16[48,8192]{1,0:T(8,128)(2,1)}, bf16[48,8192]{1,0:T(8,128)(2,1)}, u32[]{:S(2)}, u32[]{:S(2)}) collective-permute-start(bf16[48,8192]{1,0:T(8,128)(2,1)} %collective-permute-done.1.refs_0_.refs_8_), channel_id=1, source_target_pairs={{0,1},{1,0},{2,3},{3,2},{4,5},{5,4},{6,7},{7,6},{8,9},{9,8},{10,11... | collective-permute-start | bytes 2359304 | tf_op jit(solution)/shard_map/ppermute | solution.py:36
  83.2 1.9 %collective-permute-start.8 = (bf16[16,8192]{1,0:T(8,128)(2,1)}, bf16[16,8192]{1,0:T(8,128)(2,1)}, u32[]{:S(2)}, u32[]{:S(2)}) collective-permute-start(bf16[16,8192]{1,0:T(8,128)(2,1)} %slice.16), channel_id=1, source_target_pairs={{0,2},{1,3},{2,4},{3,5},{4,6},{5,7},{6,0},{7,1},{8,10},{9,11},{10,... | collective-permute-start | bytes 786440 | tf_op jit(solution)/shard_map/ppermute | solution.py:36
  85.2 1.9 %collective-permute-start.11 = (bf16[32,8192]{1,0:T(8,128)(2,1)S(1)}, bf16[32,8192]{1,0:T(8,128)(2,1)}, u32[]{:S(2)}, u32[]{:S(2)}) collective-permute-start(bf16[32,8192]{1,0:T(8,128)(2,1)S(1)} %collective-permute-done.10.refs_8_.refs_16_), channel_id=1, source_target_pairs={{0,1},{1,0},{2,3},{3,2},{4,5},{5,4},{6,7},{7,6},{8,9},{9,8},{10,11... | collective-permute-start | bytes 1572872 | tf_op jit(solution)/shard_map/ppermute | solution.py:36
  87.8 6.7 %collective-permute-done.8.refs_6_.refs_14_ = bf16[16,8192]{1,0:T(8,128)(2,1)} collective-permute-done((bf16[16,8192]{1,0:T(8,128)(2,1)}, bf16[16,8192]{1,0:T(8,128)(2,1)}, u32[]{:S(2)}, u32[]{:S(2)}) %collective-permute-start.8) | collective-permute-done | bytes 262176 | tf_op jit(solution)/shard_map/ppermute | solution.py:36
  94.5 2.8 %collective-permute-start.9 = (bf16[16,8192]{1,0:T(8,128)(2,1)}, bf16[16,8192]{1,0:T(8,128)(2,1)}, u32[]{:S(2)}, u32[]{:S(2)}) collective-permute-start(bf16[16,8192]{1,0:T(8,128)(2,1)} %collective-permute-done.8.refs_6_.refs_14_), channel_id=1, source_target_pairs={{0,1},{1,0},{2,3},{3,2},{4,5},{5,4},{6,7},{7,6},{8,9},{9,8},{10,11... | collective-permute-start | bytes 786440 | tf_op jit(solution)/shard_map/ppermute | solution.py:36
  98.0 1.1 copy-done.1
  99.2 1.1 copy-done.4
  100.3 1.1 copy-done.7
  101.4 1.1 copy-done.10
  102.6 1.1 copy-done.13
  103.7 1.1 copy-done.16
  104.8 1.1 copy-done.19
  106.0 1.1 copy-done.22
  107.1 4.9 %shard_map.113.refs_11_ = f32[32,128,128]{2,1,0:T(8,128)S(1)} custom-call(s32[32]{0:T(128)S(1)} %add_bitcast_fusion.cells_ref, s32[18]{0:T(128)S(1)} %multiply_add_fusion.offs_ref, bf16[48,8192]{1,0:T(8,128)(2,1)S(1)} %copy-done.1, bf16[48,8192]{1,0:T(8,128)(2,1)S(1)} %copy-done.13, bf16[48,8192]{1,0:T(8,128)(2,1)S(1)} %copy-done.7, ...), custom_call_target="tpu_custom_call" | custom-call | flops 402653184 | bytes 9764864 | tf_op jit(solution)/shard_map/pallas_call | solution.py:124
  112.1 6.9 %shard_map.114 = f32[32,136,128]{2,1,0:T(8,128)S(1)} custom-call(s32[32]{0:T(128)S(1)} %add_bitcast_fusion.cells_ref, s32[18]{0:T(128)S(1)} %multiply_add_fusion.offs_ref, bf16[48,8192]{1,0:T(8,128)(2,1)} %collective-permute-done.1.refs_0_.refs_8_, bf16[48,8192]{1,0:T(8,128)(2,1)} %collective-permute-done.2.refs_1_, ...), custom_call_target="tpu_custom_call" | custom-call | flops 402653184 | bytes 11993088 | tf_op jit(solution)/shard_map/pallas_call | solution.py:124
  119.0 1.1 convert_element_type.4
  120.2 25.9 %all-to-all-start = ((f16[32,136,128]{2,1,0:T(8,128)(2,1)}), f16[32,136,128]{2,1,0:T(8,128)(2,1)}, u32[]{:S(2)}, u32[]{:S(2)}) async-start(f16[32,136,128]{2,1,0:T(8,128)(2,1)} %convert_element_type.4), calls=%async_computation | async-start | bytes 2228224 | tf_op jit(solution)/shard_map/all_to_all | solution.py:184
  146.1 2.2 %collective-permute-start.17 = (bf16[48,8192]{1,0:T(8,128)(2,1)}, bf16[48,8192]{1,0:T(8,128)(2,1)}, u32[]{:S(2)}, u32[]{:S(2)}) collective-permute-start(bf16[48,8192]{1,0:T(8,128)(2,1)} %collective-permute-done.1.refs_0_.refs_8_), channel_id=1, source_target_pairs={{0,1},{1,0},{2,3},{3,2},{4,5},{5,4},{6,7},{7,6},{8,9},{9,8},{10,11... | collective-permute-start | bytes 2359304 | tf_op jit(solution)/shard_map/ppermute | solution.py:36
  148.3 2.1 %collective-permute-start.18 = (bf16[48,8192]{1,0:T(8,128)(2,1)S(1)}, bf16[48,8192]{1,0:T(8,128)(2,1)}, u32[]{:S(2)}, u32[]{:S(2)}) collective-permute-start(bf16[48,8192]{1,0:T(8,128)(2,1)S(1)} %collective-permute-done.4.refs_2_.refs_10_), channel_id=1, source_target_pairs={{0,1},{1,0},{2,3},{3,2},{4,5},{5,4},{6,7},{7,6},{8,9},{9,8},{10,11... | collective-permute-start | bytes 2359304 | tf_op jit(solution)/shard_map/ppermute | solution.py:36
  150.4 2.2 %collective-permute-start.19 = (bf16[48,8192]{1,0:T(8,128)(2,1)S(1)}, bf16[48,8192]{1,0:T(8,128)(2,1)}, u32[]{:S(2)}, u32[]{:S(2)}) collective-permute-start(bf16[48,8192]{1,0:T(8,128)(2,1)S(1)} %collective-permute-done.6.refs_4_.refs_12_), channel_id=1, source_target_pairs={{0,1},{1,0},{2,3},{3,2},{4,5},{5,4},{6,7},{7,6},{8,9},{9,8},{10,11... | collective-permute-start | bytes 2359304 | tf_op jit(solution)/shard_map/ppermute | solution.py:36
  152.6 2.1 %collective-permute-start.21 = (bf16[32,8192]{1,0:T(8,128)(2,1)S(1)}, bf16[32,8192]{1,0:T(8,128)(2,1)S(1)}, u32[]{:S(2)}, u32[]{:S(2)}) collective-permute-start(bf16[32,8192]{1,0:T(8,128)(2,1)S(1)} %collective-permute-done.10.refs_8_.refs_16_), channel_id=1, source_target_pairs={{0,1},{1,0},{2,3},{3,2},{4,5},{5,4},{6,7},{7,6},{8,9},{9,8},{10,11... | collective-permute-start | bytes 1572872 | tf_op jit(solution)/shard_map/ppermute | solution.py:36
  154.8 2.2 %collective-permute-start.20 = (bf16[16,8192]{1,0:T(8,128)(2,1)}, bf16[16,8192]{1,0:T(8,128)(2,1)}, u32[]{:S(2)}, u32[]{:S(2)}) collective-permute-start(bf16[16,8192]{1,0:T(8,128)(2,1)} %collective-permute-done.8.refs_6_.refs_14_), channel_id=1, source_target_pairs={{0,1},{1,0},{2,3},{3,2},{4,5},{5,4},{6,7},{7,6},{8,9},{9,8},{10,11... | collective-permute-start | bytes 786440 | tf_op jit(solution)/shard_map/ppermute | solution.py:36
  158.6 1.1 copy-done.5
  159.7 1.1 copy-done.8
  160.8 1.1 copy-done.11
  162.0 1.1 copy-done.14
  163.1 1.1 copy-done.17
  164.2 1.1 copy-done.20
  165.4 1.1 copy-done.23
  166.5 1.2 copy-done.24
  167.7 9.0 %shard_map.115 = bf16[768,896]{1,0:T(8,128)(2,1)} custom-call(s32[32]{0:T(128)S(1)} %add_bitcast_fusion.cells_ref, s32[18]{0:T(128)S(1)} %multiply_add_fusion.offs_ref, s32[1]{0:T(128)S(6)} %copy.12.counts_ref, bf16[48,8192]{1,0:T(8,128)(2,1)S(1)} %copy-done.2, bf16[48,8192]{1,0:T(8,128)(2,1)S(1)} %copy-done.14, bf16[48,8192]{1,0:T(8,128)(2,1)S(1)} %copy-done.8, ...), custom_call_target="tpu_custom_call" | custom-call | flops 805306368 | bytes 15007744 | tf_op jit(solution)/shard_map/pallas_call | solution.py:124
  176.8 1.4 bitcast_convert_fusion
  (60 shorter events, 9.4 us)
Async XLA Ops:
  0.6 97.4 %copy-start = (bf16[768,896]{1,0:T(8,128)(2,1)S(1)}, bf16[768,896]{1,0:T(8,128)(2,1)}, u32[]{:S(2)}) copy-start(bf16[768,896]{1,0:T(8,128)(2,1)} %refs_10_.1) | copy-start | bytes 4128772
  0.6 28.4 %collective-permute-start.3 = (bf16[48,8192]{1,0:T(8,128)(2,1)}, bf16[48,8192]{1,0:T(8,128)(2,1)S(1)}, u32[]{:S(2)}, u32[]{:S(2)}) collective-permute-start(bf16[48,8192]{1,0:T(8,128)(2,1)} %refs_0_.3), channel_id=1, source_target_pairs={{0,8},{1,9},{2,10},{3,11},{4,12},{5,13},{6,14},{7,15},{8,0},{9,1},... | collective-permute-start | bytes 2359304 | tf_op jit(solution)/shard_map/ppermute | solution.py:36
  12.2 25.5 %collective-permute-start = (bf16[48,8192]{1,0:T(8,128)(2,1)}, bf16[48,8192]{1,0:T(8,128)(2,1)S(1)}, u32[]{:S(2)}, u32[]{:S(2)}) collective-permute-start(bf16[48,8192]{1,0:T(8,128)(2,1)} %refs_0_.3), channel_id=1, source_target_pairs={{0,2},{1,3},{2,4},{3,5},{4,6},{5,7},{6,0},{7,1},{8,10},{9,11},{10,... | collective-permute-start | bytes 2359304 | tf_op jit(solution)/shard_map/ppermute | solution.py:36
  15.4 24.3 %collective-permute-start.14 = (bf16[48,8192]{1,0:T(8,128)(2,1)}, bf16[48,8192]{1,0:T(8,128)(2,1)S(1)}, u32[]{:S(2)}, u32[]{:S(2)}) collective-permute-start(bf16[48,8192]{1,0:T(8,128)(2,1)} %refs_0_.3), channel_id=1, source_target_pairs={{0,6},{1,7},{2,0},{3,1},{4,2},{5,3},{6,4},{7,5},{8,14},{9,15},{10,... | collective-permute-start | bytes 2359304 | tf_op jit(solution)/shard_map/ppermute | solution.py:36
  18.7 22.8 %collective-permute-start.12 = (bf16[48,8192]{1,0:T(8,128)(2,1)}, bf16[48,8192]{1,0:T(8,128)(2,1)S(1)}, u32[]{:S(2)}, u32[]{:S(2)}) collective-permute-start(bf16[48,8192]{1,0:T(8,128)(2,1)} %refs_0_.3), channel_id=1, source_target_pairs={{0,1},{1,0},{2,3},{3,2},{4,5},{5,4},{6,7},{7,6},{8,9},{9,8},{10,11... | collective-permute-start | bytes 2359304 | tf_op jit(solution)/shard_map/ppermute | solution.py:36
  29.0 36.7 %copy-start.3 = (bf16[48,8192]{1,0:T(8,128)(2,1)}, bf16[48,8192]{1,0:T(8,128)(2,1)S(1)}, u32[]{:S(2)}) copy-start(bf16[48,8192]{1,0:T(8,128)(2,1)S(1)} %collective-permute-done.3.refs_6_) | copy-start | bytes 2359300
  29.0 23.2 %collective-permute-start.6 = (bf16[48,8192]{1,0:T(8,128)(2,1)S(1)}, bf16[48,8192]{1,0:T(8,128)(2,1)S(1)}, u32[]{:S(2)}, u32[]{:S(2)}) collective-permute-start(bf16[48,8192]{1,0:T(8,128)(2,1)S(1)} %collective-permute-done.3.refs_6_), channel_id=1, source_target_pairs={{0,6},{1,7},{2,0},{3,1},{4,2},{5,3},{6,4},{7,5},{8,14},{9,15},{10,... | collective-permute-start | bytes 2359304 | tf_op jit(solution)/shard_map/ppermute | solution.py:36
  34.2 22.9 %collective-permute-start.16 = (bf16[48,8192]{1,0:T(8,128)(2,1)S(1)}, bf16[48,8192]{1,0:T(8,128)(2,1)S(1)}, u32[]{:S(2)}, u32[]{:S(2)}) collective-permute-start(bf16[48,8192]{1,0:T(8,128)(2,1)S(1)} %collective-permute-done.3.refs_6_), channel_id=1, source_target_pairs={{0,1},{1,0},{2,3},{3,2},{4,5},{5,4},{6,7},{7,6},{8,9},{9,8},{10,11... | collective-permute-start | bytes 2359304 | tf_op jit(solution)/shard_map/ppermute | solution.py:36
  37.7 24.9 %collective-permute-start.13 = (bf16[48,8192]{1,0:T(8,128)(2,1)S(1)}, bf16[48,8192]{1,0:T(8,128)(2,1)S(1)}, u32[]{:S(2)}, u32[]{:S(2)}) collective-permute-start(bf16[48,8192]{1,0:T(8,128)(2,1)S(1)} %collective-permute-done.refs_2_), channel_id=1, source_target_pairs={{0,1},{1,0},{2,3},{3,2},{4,5},{5,4},{6,7},{7,6},{8,9},{9,8},{10,11... | collective-permute-start | bytes 2359304 | tf_op jit(solution)/shard_map/ppermute | solution.py:36
  39.6 26.1 %collective-permute-start.4 = (bf16[48,8192]{1,0:T(8,128)(2,1)S(1)}, bf16[48,8192]{1,0:T(8,128)(2,1)S(1)}, u32[]{:S(2)}, u32[]{:S(2)}) collective-permute-start(bf16[48,8192]{1,0:T(8,128)(2,1)S(1)} %collective-permute-done.3.refs_6_), channel_id=1, source_target_pairs={{0,2},{1,3},{2,4},{3,5},{4,6},{5,7},{6,0},{7,1},{8,10},{9,11},{10,... | collective-permute-start | bytes 2359304 | tf_op jit(solution)/shard_map/ppermute | solution.py:36
  41.6 0.9 copy-start.12
  42.5 35.8 %collective-permute-start.1 = (bf16[48,8192]{1,0:T(8,128)(2,1)S(1)}, bf16[48,8192]{1,0:T(8,128)(2,1)}, u32[]{:S(2)}, u32[]{:S(2)}) collective-permute-start(bf16[48,8192]{1,0:T(8,128)(2,1)S(1)} %collective-permute-done.refs_2_), channel_id=1, source_target_pairs={{0,2},{1,3},{2,4},{3,5},{4,6},{5,7},{6,0},{7,1},{8,10},{9,11},{10,... | collective-permute-start | bytes 2359304 | tf_op jit(solution)/shard_map/ppermute | solution.py:36
  44.6 0.9 copy-start.6
  52.2 30.1 %collective-permute-start.15 = (bf16[48,8192]{1,0:T(8,128)(2,1)S(1)}, bf16[48,8192]{1,0:T(8,128)(2,1)S(1)}, u32[]{:S(2)}, u32[]{:S(2)}) collective-permute-start(bf16[48,8192]{1,0:T(8,128)(2,1)S(1)} %collective-permute-done.14.refs_4_), channel_id=1, source_target_pairs={{0,1},{1,0},{2,3},{3,2},{4,5},{5,4},{6,7},{7,6},{8,9},{9,8},{10,11... | collective-permute-start | bytes 2359304 | tf_op jit(solution)/shard_map/ppermute | solution.py:36
  56.2 0.9 copy-start.9
  57.1 0.9 copy-start.15
  58.0 27.2 %collective-permute-start.10 = (bf16[32,8192]{1,0:T(8,128)(2,1)S(1)}, bf16[32,8192]{1,0:T(8,128)(2,1)S(1)}, u32[]{:S(2)}, u32[]{:S(2)}) collective-permute-start(bf16[32,8192]{1,0:T(8,128)(2,1)S(1)} %slice.17), channel_id=1, source_target_pairs={{0,6},{1,7},{2,0},{3,1},{4,2},{5,3},{6,4},{7,5},{8,14},{9,15},{10,... | collective-permute-start | bytes 1572872 | tf_op jit(solution)/shard_map/ppermute | solution.py:36
  62.6 0.9 copy-start.18
  63.5 48.5 %collective-permute-start.7 = (bf16[48,8192]{1,0:T(8,128)(2,1)S(1)}, bf16[48,8192]{1,0:T(8,128)(2,1)}, u32[]{:S(2)}, u32[]{:S(2)}) collective-permute-start(bf16[48,8192]{1,0:T(8,128)(2,1)S(1)} %collective-permute-done.6.refs_4_.refs_12_), channel_id=1, source_target_pairs={{0,1},{1,0},{2,3},{3,2},{4,5},{5,4},{6,7},{7,6},{8,9},{9,8},{10,11... | collective-permute-start | bytes 2359304 | tf_op jit(solution)/shard_map/ppermute | solution.py:36
  65.7 46.3 %collective-permute-start.5 = (bf16[48,8192]{1,0:T(8,128)(2,1)S(1)}, bf16[48,8192]{1,0:T(8,128)(2,1)}, u32[]{:S(2)}, u32[]{:S(2)}) collective-permute-start(bf16[48,8192]{1,0:T(8,128)(2,1)S(1)} %collective-permute-done.4.refs_2_.refs_10_), channel_id=1, source_target_pairs={{0,1},{1,0},{2,3},{3,2},{4,5},{5,4},{6,7},{7,6},{8,9},{9,8},{10,11... | collective-permute-start | bytes 2359304 | tf_op jit(solution)/shard_map/ppermute | solution.py:36
  78.3 33.7 %collective-permute-start.2 = (bf16[48,8192]{1,0:T(8,128)(2,1)}, bf16[48,8192]{1,0:T(8,128)(2,1)}, u32[]{:S(2)}, u32[]{:S(2)}) collective-permute-start(bf16[48,8192]{1,0:T(8,128)(2,1)} %collective-permute-done.1.refs_0_.refs_8_), channel_id=1, source_target_pairs={{0,1},{1,0},{2,3},{3,2},{4,5},{5,4},{6,7},{7,6},{8,9},{9,8},{10,11... | collective-permute-start | bytes 2359304 | tf_op jit(solution)/shard_map/ppermute | solution.py:36
  82.3 0.9 copy-start.21
  83.2 11.3 %collective-permute-start.8 = (bf16[16,8192]{1,0:T(8,128)(2,1)}, bf16[16,8192]{1,0:T(8,128)(2,1)}, u32[]{:S(2)}, u32[]{:S(2)}) collective-permute-start(bf16[16,8192]{1,0:T(8,128)(2,1)} %slice.16), channel_id=1, source_target_pairs={{0,2},{1,3},{2,4},{3,5},{4,6},{5,7},{6,0},{7,1},{8,10},{9,11},{10,... | collective-permute-start | bytes 786440 | tf_op jit(solution)/shard_map/ppermute | solution.py:36
  85.2 26.9 %collective-permute-start.11 = (bf16[32,8192]{1,0:T(8,128)(2,1)S(1)}, bf16[32,8192]{1,0:T(8,128)(2,1)}, u32[]{:S(2)}, u32[]{:S(2)}) collective-permute-start(bf16[32,8192]{1,0:T(8,128)(2,1)S(1)} %collective-permute-done.10.refs_8_.refs_16_), channel_id=1, source_target_pairs={{0,1},{1,0},{2,3},{3,2},{4,5},{5,4},{6,7},{7,6},{8,9},{9,8},{10,11... | collective-permute-start | bytes 1572872 | tf_op jit(solution)/shard_map/ppermute | solution.py:36
  94.5 17.5 %collective-permute-start.9 = (bf16[16,8192]{1,0:T(8,128)(2,1)}, bf16[16,8192]{1,0:T(8,128)(2,1)}, u32[]{:S(2)}, u32[]{:S(2)}) collective-permute-start(bf16[16,8192]{1,0:T(8,128)(2,1)} %collective-permute-done.8.refs_6_.refs_14_), channel_id=1, source_target_pairs={{0,1},{1,0},{2,3},{3,2},{4,5},{5,4},{6,7},{7,6},{8,9},{9,8},{10,11... | collective-permute-start | bytes 786440 | tf_op jit(solution)/shard_map/ppermute | solution.py:36
  98.0 1.1 copy-start.1
  99.2 1.1 copy-start.4
  100.3 1.1 copy-start.7
  101.4 1.1 copy-start.10
  102.6 1.1 copy-start.13
  103.7 1.1 copy-start.16
  104.8 1.1 copy-start.19
  106.0 1.1 copy-start.22
  119.0 39.5 %copy-start.2 = (bf16[48,8192]{1,0:T(8,128)(2,1)S(1)}, bf16[48,8192]{1,0:T(8,128)(2,1)}, u32[]{:S(2)}) copy-start(bf16[48,8192]{1,0:T(8,128)(2,1)} %refs_0_.3) | copy-start | bytes 2359300
  120.2 56.6 %all-to-all-start = ((f16[32,136,128]{2,1,0:T(8,128)(2,1)}), f16[32,136,128]{2,1,0:T(8,128)(2,1)}, u32[]{:S(2)}, u32[]{:S(2)}) async-start(f16[32,136,128]{2,1,0:T(8,128)(2,1)} %convert_element_type.4), calls=%async_computation | async-start | bytes 2228224 | tf_op jit(solution)/shard_map/all_to_all | solution.py:184
  146.1 12.5 %collective-permute-start.17 = (bf16[48,8192]{1,0:T(8,128)(2,1)}, bf16[48,8192]{1,0:T(8,128)(2,1)}, u32[]{:S(2)}, u32[]{:S(2)}) collective-permute-start(bf16[48,8192]{1,0:T(8,128)(2,1)} %collective-permute-done.1.refs_0_.refs_8_), channel_id=1, source_target_pairs={{0,1},{1,0},{2,3},{3,2},{4,5},{5,4},{6,7},{7,6},{8,9},{9,8},{10,11... | collective-permute-start | bytes 2359304 | tf_op jit(solution)/shard_map/ppermute | solution.py:36
  148.3 10.3 %collective-permute-start.18 = (bf16[48,8192]{1,0:T(8,128)(2,1)S(1)}, bf16[48,8192]{1,0:T(8,128)(2,1)}, u32[]{:S(2)}, u32[]{:S(2)}) collective-permute-start(bf16[48,8192]{1,0:T(8,128)(2,1)S(1)} %collective-permute-done.4.refs_2_.refs_10_), channel_id=1, source_target_pairs={{0,1},{1,0},{2,3},{3,2},{4,5},{5,4},{6,7},{7,6},{8,9},{9,8},{10,11... | collective-permute-start | bytes 2359304 | tf_op jit(solution)/shard_map/ppermute | solution.py:36
  150.4 8.1 %collective-permute-start.19 = (bf16[48,8192]{1,0:T(8,128)(2,1)S(1)}, bf16[48,8192]{1,0:T(8,128)(2,1)}, u32[]{:S(2)}, u32[]{:S(2)}) collective-permute-start(bf16[48,8192]{1,0:T(8,128)(2,1)S(1)} %collective-permute-done.6.refs_4_.refs_12_), channel_id=1, source_target_pairs={{0,1},{1,0},{2,3},{3,2},{4,5},{5,4},{6,7},{7,6},{8,9},{9,8},{10,11... | collective-permute-start | bytes 2359304 | tf_op jit(solution)/shard_map/ppermute | solution.py:36
  152.6 5.9 %collective-permute-start.21 = (bf16[32,8192]{1,0:T(8,128)(2,1)S(1)}, bf16[32,8192]{1,0:T(8,128)(2,1)S(1)}, u32[]{:S(2)}, u32[]{:S(2)}) collective-permute-start(bf16[32,8192]{1,0:T(8,128)(2,1)S(1)} %collective-permute-done.10.refs_8_.refs_16_), channel_id=1, source_target_pairs={{0,1},{1,0},{2,3},{3,2},{4,5},{5,4},{6,7},{7,6},{8,9},{9,8},{10,11... | collective-permute-start | bytes 1572872 | tf_op jit(solution)/shard_map/ppermute | solution.py:36
  154.8 3.8 %collective-permute-start.20 = (bf16[16,8192]{1,0:T(8,128)(2,1)}, bf16[16,8192]{1,0:T(8,128)(2,1)}, u32[]{:S(2)}, u32[]{:S(2)}) collective-permute-start(bf16[16,8192]{1,0:T(8,128)(2,1)} %collective-permute-done.8.refs_6_.refs_14_), channel_id=1, source_target_pairs={{0,1},{1,0},{2,3},{3,2},{4,5},{5,4},{6,7},{7,6},{8,9},{9,8},{10,11... | collective-permute-start | bytes 786440 | tf_op jit(solution)/shard_map/ppermute | solution.py:36
  158.6 1.1 copy-start.5
  159.7 1.1 copy-start.8
  160.8 1.1 copy-start.11
  162.0 1.1 copy-start.14
  163.1 1.1 copy-start.17
  164.2 1.1 copy-start.20
  165.4 1.1 copy-start.23
  166.5 1.2 copy-start.24
